TPU v7x, 32 devices: a whole 2x2x4 slice. The times are simulated.
32 devices in a mesh: groups: 1, tensor: 16 (over z, y, core), replica: 2 (over x).
Axes of the slice: x: 2, y: 2, z: 4, core: 2. Of those that a mesh axis runs over, the one named last changes fastest.
Arguments:
- q_latent: bfloat16 [256, 1536], P(('groups', 'tensor', 'replica')), may hold values from -6 to 6
- q_gain: float32 [1536], replicated, may hold values from 0.25 to 1.75
- q_up: bfloat16 [1536, 12288], P(None, 'tensor'), may hold values from -0.15625 to 0.15625
- w_uk: bfloat16 [64, 128, 512], P('tensor'), may hold values from -0.5 to 0.5
- w_uv: bfloat16 [64, 512, 128], P('tensor'), may hold values from -1 to 1
- w_o: bfloat16 [8192, 7168], P('tensor', 'replica'), may hold values from -0.0625 to 0.0625
- new_kv: bfloat16 [256, 576], P(('groups', 'tensor', 'replica')), may hold values from -6 to 6
- latent_cache: bfloat16 [64, 1024, 576], P(('groups', 'tensor', 'replica')), may hold values from -64 to 64
- cache_len: int32 [64], P(('groups', 'tensor', 'replica')), may hold values from 128 to 1024, as said below
- draft_count: int32 [64], P(('groups', 'tensor', 'replica')), may hold values from 1 to 4, as said below
Outputs:
- attn_out: bfloat16 [256, 7168], P(('groups', 'tensor', 'replica'))
Inputs may be any that keep to these rules, and one draw needn't show every extreme that they name: `cache_len`: some request of every draw uses all 1024 slots. The first draft_count rows of a request are in use; some request of every draw uses all 4.
All inputs are finite; a program needn't handle non-finite values.
Results may differ from a plain program's by a relative error of at most 0.024.
The roundings to bfloat16 on the way count: a program that leaves them out, or rounds other values in their place, can miss the bound.
Values may be sent and summed in bfloat16 or wider, within the bound.
No kernel may reach another device: no remote copies, remote signals or barrier semaphores. Data moves between devices by JAX's collectives and lax.ppermute only.
A program may use at most 64 MiB of HBM per device.

v0:
```python
import jax
import jax.numpy as jnp
from jax import lax
from jax.sharding import PartitionSpec as P

LATENT = 512
ROPE = 64
NOPE = 128
VDIM = 128
DRAFT = 4
REQ_DEV = 2


rms_eps = 1e-06
rope_base = 50000.0


def normalize(rows_in, gain_row):
    values_f = rows_in.astype(jnp.float32)
    scaled = values_f * lax.rsqrt(jnp.mean(values_f * values_f, axis=-1, keepdims=True) + rms_eps)
    return (scaled * gain_row).astype(jnp.bfloat16)


def rotate(rope_part, positions):
    half_width = rope_part.shape[-1] // 2
    frequency = rope_base ** (
        -(jnp.arange(half_width).astype(jnp.float32) * 2.0 / rope_part.shape[-1])
    )
    angles = positions[:, None, None] * frequency
    cosine = jnp.cos(angles)
    sine = jnp.sin(angles)
    widened = rope_part.astype(jnp.float32)
    first_half = widened[..., :half_width]
    second_half = widened[..., half_width:]
    turned = jnp.concatenate(
        [first_half * cosine - second_half * sine, second_half * cosine + first_half * sine],
        axis=-1,
    )
    return turned.astype(jnp.bfloat16)


def attend(query_rows, new_rows, cache_rows, length, draft_total):
    queries = query_rows.reshape(-1, query_rows.shape[-1])
    contract = (((1,), (1,)), ((), ()))
    score_scale = (NOPE + ROPE) ** (-0.5)
    cache_scores = (
        lax.dot_general(queries, cache_rows, contract, preferred_element_type=jnp.float32)
        * score_scale
    )
    new_scores = (
        lax.dot_general(queries, new_rows, contract, preferred_element_type=jnp.float32)
        * score_scale
    )
    row_draft = jnp.arange(queries.shape[0]) // query_rows.shape[1]
    cache_seen = jnp.arange(cache_rows.shape[0]) < length
    new_seen = jnp.arange(new_rows.shape[0])[None, :] <= row_draft[:, None]
    cache_scores = jnp.where(cache_seen[None, :], cache_scores, -jnp.inf)
    new_scores = jnp.where(new_seen, new_scores, -jnp.inf)
    row_peak = jnp.maximum(jnp.max(cache_scores, axis=1), jnp.max(new_scores, axis=1))[:, None]
    cache_exp = jnp.exp(cache_scores - row_peak)
    new_exp = jnp.exp(new_scores - row_peak)
    denominator = jnp.sum(cache_exp, axis=1, keepdims=True) + jnp.sum(
        new_exp, axis=1, keepdims=True
    )
    cache_weights = (cache_exp / denominator).astype(jnp.bfloat16)
    new_weights = (new_exp / denominator).astype(jnp.bfloat16)
    latent_mix = jnp.dot(cache_weights, cache_rows[:, :LATENT], preferred_element_type=jnp.float32)
    latent_mix = latent_mix + jnp.dot(
        new_weights, new_rows[:, :LATENT], preferred_element_type=jnp.float32
    )
    latent_mix = jnp.where((row_draft < draft_total)[:, None], latent_mix, 0.0).astype(jnp.bfloat16)
    return latent_mix.reshape(query_rows.shape[0], query_rows.shape[1], LATENT)


def shards(q_latent, q_gain, q_up, w_uk, w_uv, w_o, new_kv, latent_cache, cache_len, draft_count):
    rows_dev = q_latent.shape[0]
    owners = lax.axis_size("tensor")
    heads_dev = w_uk.shape[0]
    head_count = heads_dev * owners
    normed = normalize(q_latent, q_gain)
    query_full = jnp.dot(
        lax.all_gather(normed, "tensor", axis=0, tiled=True),
        q_up,
        preferred_element_type=jnp.float32,
    ).astype(jnp.bfloat16)
    query_full = query_full.reshape(owners, rows_dev, heads_dev, NOPE + ROPE)
    absorbed = jnp.einsum(
        "pihn,hnl->iphl", query_full[..., :NOPE], w_uk, preferred_element_type=jnp.float32
    ).astype(jnp.bfloat16)
    rope_part = jnp.swapaxes(query_full[..., NOPE:], 0, 1)
    packed_queries = jnp.concatenate([absorbed, rope_part], axis=-1).reshape(
        rows_dev, owners, heads_dev * (LATENT + ROPE)
    )
    arrived = lax.all_to_all(packed_queries, "tensor", split_axis=1, concat_axis=1, tiled=True)
    arrived = arrived.reshape(rows_dev, head_count, LATENT + ROPE)
    row_length = jnp.broadcast_to(cache_len[:, None], (REQ_DEV, DRAFT)).reshape(-1)
    positions = (row_length + jnp.arange(rows_dev) % DRAFT).astype(jnp.float32)
    rotated = rotate(arrived[..., LATENT:], positions)
    query = jnp.concatenate([arrived[..., :LATENT], rotated], axis=-1)
    latent_out = jax.vmap(attend)(
        query.reshape(REQ_DEV, DRAFT, head_count, LATENT + ROPE),
        new_kv.reshape(REQ_DEV, DRAFT, LATENT + ROPE),
        latent_cache,
        cache_len,
        draft_count,
    )
    latent_out = latent_out.reshape(rows_dev, owners, heads_dev * LATENT)
    returned = lax.all_to_all(latent_out, "tensor", split_axis=1, concat_axis=1, tiled=True)
    returned = returned.reshape(rows_dev, owners, heads_dev, LATENT)
    head_values = jnp.einsum(
        "ithl,hlv->tihv", returned, w_uv, preferred_element_type=jnp.float32
    ).astype(jnp.bfloat16)
    head_values = head_values.reshape(owners * rows_dev, heads_dev * VDIM)
    replicas = lax.axis_size("replica")
    spread = lax.all_gather(head_values, "replica", axis=0, tiled=True)
    spread = spread.reshape(replicas, owners, rows_dev, heads_dev * VDIM)
    block_rows = replicas * rows_dev
    product = jnp.einsum("rtiv,vc->tric", spread, w_o, preferred_element_type=jnp.float32)
    shares = lax.psum_scatter(
        product.reshape(block_rows * lax.axis_size("tensor"), w_o.shape[1]).astype(jnp.bfloat16),
        "tensor",
        scatter_dimension=0,
        tiled=True,
    ).astype(jnp.float32)
    shares = shares.astype(jnp.bfloat16).reshape(replicas, rows_dev, w_o.shape[1])
    placed = lax.all_to_all(shares, "replica", split_axis=0, concat_axis=2, tiled=True)
    return placed.reshape(rows_dev, replicas * w_o.shape[1])


def solution(mesh):
    return jax.shard_map(
        shards,
        mesh=mesh,
        in_specs=(
            P(("groups", "tensor", "replica"), None),
            P(),
            P(None, "tensor"),
            P("tensor", None, None),
            P("tensor", None, None),
            P("tensor", "replica"),
            P(("groups", "tensor", "replica"), None),
            P(("groups", "tensor", "replica"), None, None),
            P(("groups", "tensor", "replica")),
            P(("groups", "tensor", "replica")),
        ),
        out_specs=P(("groups", "tensor", "replica"), None),
        check_vma=False,
    )
```

profile of v0, /device:TPU:0, one launch (start us, length us, event | category | flops | bytes accessed | tf_op | source)
XLA Modules:
  0.0 170.3 jit_solution(1543536647572965304)
XLA Ops:
  6.5 1.0 fusion.27
  7.6 0.8 fusion.29
  8.4 24.2 %all_gather.6 = bf16[128,1536]{1,0:T(8,128)(2,1)S(1)} all-gather(bf16[8,1536]{1,0:T(8,128)(2,1)S(1)} %fusion.29), channel_id=1, replica_groups=mesh['groups'=1,'tensor'=16,'replica'=2] {'tensor'}, dimensions={0}, use_global_device_ids=true | all-gather | bytes 417792 | tf_op jit(solution)/shard_map/all_gather | solution.py:82
  32.6 0.5 convolution_convert_fusion.2
  33.0 0.2 reshape.207
  33.4 0.2 copy-done.1
  33.6 0.3 fusion.15
  34.0 0.5 copy.53
  34.5 1.3 reshape.221
  35.8 3.6 %all-to-all-start = ((bf16[8,16,2304]{2,0,1:T(8,128)(2,1)}), bf16[8,16,2304]{2,0,1:T(8,128)(2,1)S(1)}, u32[]{:S(2)}, u32[]{:S(2)}) async-start(bf16[8,16,2304]{2,0,1:T(8,128)(2,1)} %reshape.221), calls=%async_computation | async-start | bytes 1179648 | tf_op jit(solution)/shard_map/all_to_all | solution.py:94
  40.0 14.9 %all-to-all-done = bf16[8,16,2304]{2,0,1:T(8,128)(2,1)S(1)} async-done(((bf16[8,16,2304]{2,0,1:T(8,128)(2,1)}), bf16[8,16,2304]{2,0,1:T(8,128)(2,1)S(1)}, u32[]{:S(2)}, u32[]{:S(2)}) %all-to-all-start) | async-done | bytes 589856 | tf_op jit(solution)/shard_map/all_to_all | solution.py:94
  54.9 0.9 copy.39
  55.8 1.9 %reshape.209 = bf16[8,64,576]{2,1,0:T(8,128)(2,1)S(1)} reshape(bf16[8,16,2304]{2,1,0:T(8,128)(2,1)} %copy.39) | data formatting | bytes 1179648 | tf_op jit(solution)/shard_map/reshape | solution.py:95
  57.8 0.2 subtract_convert_fusion
  57.9 0.1 pad_maximum_fusion.1
  58.1 0.3 fusion.39
  58.4 1.0 copy-done.5
  59.4 1.1 fusion.4
  60.5 0.6 fusion.5
  61.1 0.4 fusion.30
  61.4 1.1 fusion.12
  62.5 0.3 reshape.212
  62.9 0.3 copy.43
  63.2 18.3 %all_to_all.25 = bf16[8,16,2048]{2,0,1:T(8,128)(2,1)S(1)} all-to-all(bf16[8,16,2048]{2,0,1:T(8,128)(2,1)S(1)} %copy.43), channel_id=1, replica_groups=mesh['groups'=1,'tensor'=16,'replica'=2] {'tensor'}, dimensions={1} | all-to-all | bytes 1048576 | tf_op jit(solution)/shard_map/all_to_all | solution.py:108
  81.5 0.4 reshape.222
  81.9 1.7 %fusion.16 = bf16[16,8,4,128]{3,0,1,2:T(8,128)(2,1)S(1)} fusion(bf16[4,512,128]{2,1,0:T(8,128)(2,1)} %param.14, bf16[8,16,4,512]{3,2,0,1:T(4,128)(2,1)S(1)} %reshape.222), kind=kOutput, calls=%fused_computation.17 | convolution fusion | flops 67174400 | bytes 1179648 | tf_op jit(solution)/shard_map/ithl,hlv->tihv/dot_general | solution.py:110
  83.7 6.2 %all_gather.7 = bf16[256,512]{1,0:T(8,128)(2,1)S(1)} all-gather(bf16[128,512]{1,0:T(8,128)(2,1)S(1)} %bitcast.51), channel_id=1, replica_groups=mesh['groups'=1,'tensor'=16,'replica'=2] {'replica'}, dimensions={0}, use_global_device_ids=true | all-gather | bytes 393216 | tf_op jit(solution)/shard_map/all_gather | solution.py:115
  89.9 3.2 %fusion = bf16[16,2,8,3584]{3,2,0,1:T(8,128)(2,1)S(1)} fusion(bf16[2,16,8,512]{3,2,1,0:T(8,128)(2,1)S(1)} %bitcast.53, bf16[512,3584]{1,0:T(8,128)(2,1)} %param.15), kind=kOutput, calls=%fused_computation.1 | convolution fusion | flops 940441600 | bytes 5767168 | tf_op jit(solution)/shard_map/rtiv,vc->tric/dot_general | solution.py:118
  93.1 1.4 copy.47
  94.5 60.6 %reduce-scatter.2.cloned.1.call-done = bf16[16,3584]{1,0:T(8,128)(2,1)} async-done(((bf16[256,3584]{1,0:T(8,128)(2,1)}), bf16[16,3584]{1,0:T(8,128)(2,1)}) %reduce-scatter.2.cloned.1.call-update) | async-done | bytes 114704 | tf_op jit(solution)/shard_map/reduce_scatter | solution.py:119
  155.1 7.7 %all_to_all.26 = bf16[2,8,3584]{2,1,0:T(8,128)(2,1)S(1)} all-to-all(bf16[2,8,3584]{2,1,0:T(8,128)(2,1)} %bitcast.54), channel_id=1, replica_groups=mesh['groups'=1,'tensor'=16,'replica'=2] {'replica'}, dimensions={0} | all-to-all | bytes 229376 | tf_op jit(solution)/shard_map/all_to_all | solution.py:126
  162.9 0.6 copy.69
  (33 shorter events, 0.9 us)
Async XLA Ops:
  6.5 26.0 %copy-start = (bf16[1536,768]{1,0:T(8,128)(2,1)S(1)}, bf16[1536,768]{1,0:T(8,128)(2,1)}, u32[]{:S(2)}) copy-start(bf16[1536,768]{1,0:T(8,128)(2,1)} %param.12) | copy-start | bytes 7077892
  32.6 1.0 copy-start.1
  34.0 5.5 %copy-start.4 = (s32[2]{0:T(128)S(1)}, s32[2]{0:T(128)}, u32[]{:S(2)}) copy-start(s32[2]{0:T(128)} %param.18) | copy-start | bytes 28
  34.0 5.7 %copy-start.2 = (bf16[8,576]{1,0:T(8,128)(2,1)S(1)}, bf16[8,576]{1,0:T(8,128)(2,1)}, u32[]{:S(2)}) copy-start(bf16[8,576]{1,0:T(8,128)(2,1)} %param.16) | copy-start | bytes 27652
  34.0 5.7 %copy-start.3 = (s32[2]{0:T(128)S(1)}, s32[2]{0:T(128)}, u32[]{:S(2)}) copy-start(s32[2]{0:T(128)} %param.19) | copy-start | bytes 28
  35.8 19.1 %all-to-all-start = ((bf16[8,16,2304]{2,0,1:T(8,128)(2,1)}), bf16[8,16,2304]{2,0,1:T(8,128)(2,1)S(1)}, u32[]{:S(2)}, u32[]{:S(2)}) async-start(bf16[8,16,2304]{2,0,1:T(8,128)(2,1)} %reshape.221), calls=%async_computation | async-start | bytes 1179648 | tf_op jit(solution)/shard_map/all_to_all | solution.py:94
  39.4 115.7 %reduce-scatter.2.cloned.1.call-start = ((), (), s32[]{:S(2)}) async-start(), calls=%async_computation.4 | async-start | bytes 1949696 | tf_op jit(solution)/shard_map/reduce_scatter | solution.py:119
  57.7 1.7 copy-start.5
Sparse Core Ops, SparseCore 0:
  94.7 60.4 reduce-scatter.1
where the time goes:
time: 171 us; the launch traced here: 170 us
  waiting for transfers between devices  75.5 us (44%)
  blocking collectives  56.5 us (33%)
  between operations  13.7 us (8%)
  local copies, waits for them, and re-layouts  9.49 us (6%)
  matrix products  8.49 us (5%)
  starting transfers between devices  3.62 us (2%)
  other arithmetic  3.07 us (2%)
    reduce_scatter x1, waiting for transfers between devices, shards(): lax.psum_scatter(product.reshape(block_rows * lax.axis_size('tensor'), w_...  60.6 us
    all_gather x1, blocking collectives, shards(): lax.all_gather(normed, 'tensor', axis=0, tiled=True)  24.2 us
    all_to_all x1, blocking collectives, shards(): lax.all_to_all(latent_out, 'tensor', split_axis=1, concat_axis=1, tiled=T...  18.3 us
    all_to_all x1, waiting for transfers between devices, shards(): lax.all_to_all(packed_queries, 'tensor', split_axis=1, concat_axis=1, til...  14.9 us
    all_to_all x1, blocking collectives, shards(): lax.all_to_all(shares, 'replica', split_axis=0, concat_axis=2, tiled=True)  7.73 us
    all_gather x1, blocking collectives, shards(): spread = lax.all_gather(head_values, 'replica', axis=0, tiled=True)  6.21 us
    all_to_all x1, starting transfers between devices, shards(): lax.all_to_all(packed_queries, 'tensor', split_axis=1, concat_axis=1, til...  3.58 us
  transfers between devices with their start and end apart: 2, of which 2 were waited for; matrix products, arithmetic and copies ran while one was open for 0% of the time, Pallas kernels for 0%

commit v1 on v0

v1 whole, which is shorter than its diff:
```python
import functools

import jax
import jax.numpy as jnp
from jax import lax
from jax.experimental import pallas as pl
from jax.experimental.pallas import tpu as pltpu
from jax.sharding import PartitionSpec as P

LATENT = 512
ROPE = 64
NOPE = 128
VDIM = 128
QKD = NOPE + ROPE
LANES = 128

rms_eps = 1e-06
rope_base = 50000.0

VMEM = pltpu.MemorySpace.VMEM
SMEM = pltpu.MemorySpace.SMEM
bf16 = jnp.bfloat16
f32 = jnp.float32


def vmem_spec():
    return pl.BlockSpec(memory_space=VMEM)


def smem_spec():
    return pl.BlockSpec(memory_space=SMEM)


def mm(a, b):
    return jnp.dot(a, b, preferred_element_type=f32)


def mm_nt(a, b):
    return lax.dot_general(a, b, (((1,), (1,)), ((), ())), preferred_element_type=f32)


def query_kernel(reqs, drafts, heads, me_ref, x_ref, gain_ref, up_ref, uk_ref, out_ref):
    owners = out_ref.shape[0]
    rows_dev = reqs * drafts
    hd = heads * drafts
    x = x_ref[...].astype(f32)
    scaled = x * lax.rsqrt(jnp.mean(x * x, axis=-1, keepdims=True) + rms_eps)
    normed = (scaled * gain_ref[...]).astype(bf16)
    full = mm(normed, up_ref[...]).astype(bf16)
    count = owners * reqs * hd
    shape = (count, owners * rows_dev)
    n = lax.broadcasted_iota(jnp.int32, shape, 0)
    m = lax.broadcasted_iota(jnp.int32, shape, 1)
    target = n // (reqs * hd)
    local = (n // hd) % reqs * drafts + n % drafts
    source = m // rows_dev
    spread = jnp.where((target == (source ^ me_ref[0])) & (local == m % rows_dev), 1.0, 0.0)
    wide = mm(spread.astype(bf16), full)
    row_head = (lax.broadcasted_iota(jnp.int32, (count, 1), 0) // drafts) % heads
    absorbed = None
    rope = None
    for h in range(heads):
        mine = row_head == h
        nope_h = jnp.where(mine, wide[:, h * QKD : h * QKD + NOPE], 0.0).astype(bf16)
        part = mm(nope_h, uk_ref[h])
        absorbed = part if absorbed is None else absorbed + part
        rope_h = jnp.where(mine, wide[:, h * QKD + NOPE : (h + 1) * QKD], 0.0)
        rope = rope_h if rope is None else rope + rope_h
    chunks = LATENT // LANES
    absorbed = absorbed.reshape(owners, reqs, hd, LATENT)
    rope = rope.reshape(owners, reqs, hd, ROPE)
    for q in range(reqs):
        for c in range(chunks):
            at = (q * chunks + c) * hd
            out_ref[:, at : at + hd, :] = absorbed[:, q, :, c * LANES : (c + 1) * LANES].astype(bf16)
    per = LANES // ROPE
    for b in range(reqs // per):
        at = (reqs * chunks + b) * hd
        both = jnp.concatenate([rope[:, b * per + i] for i in range(per)], axis=-1)
        out_ref[:, at : at + hd, :] = both.astype(bf16)


def attend_kernel(reqs, drafts, heads, len_ref, count_ref, q_ref, cos_ref, sin_ref, new_ref, cache_ref, out_ref):
    owners = q_ref.shape[0]
    hd = heads * drafts
    count = owners * hd
    chunks = LATENT // LANES
    per = LANES // ROPE
    slots = cache_ref.shape[2]
    scale = QKD ** (-0.5)
    rotated = []
    for b in range(reqs // per):
        at = (reqs * chunks + b) * hd
        x = q_ref[:, at : at + hd, :].astype(f32).reshape(count, LANES)
        lane = lax.broadcasted_iota(jnp.int32, x.shape, 1) % ROPE
        half = ROPE // 2
        other = jnp.where(lane < half, pltpu.roll(x, LANES - half, 1), pltpu.roll(x, half, 1))
        x = x.reshape(owners, hd, LANES) * cos_ref[b] + other.reshape(owners, hd, LANES) * sin_ref[b]
        x = x.astype(bf16).reshape(count, LANES)
        rotated += [x[:, i * ROPE : (i + 1) * ROPE] for i in range(per)]
    draft = lax.broadcasted_iota(jnp.int32, (count, 1), 0) % drafts
    new_at = lax.broadcasted_iota(jnp.int32, (count, new_ref.shape[0]), 1)
    slot = lax.broadcasted_iota(jnp.int32, (1, slots), 1)
    for q in range(reqs):
        absorbed = jnp.concatenate(
            [
                q_ref[:, (q * chunks + c) * hd : (q * chunks + c + 1) * hd, :].reshape(count, LANES)
                for c in range(chunks)
            ],
            axis=-1,
        )
        keys = cache_ref[q]
        rows = new_ref[...]
        score = (mm(absorbed, keys[:LATENT]) + mm(rotated[q], keys[LATENT:])) * scale
        fresh = (mm_nt(absorbed, rows[:, :LATENT]) + mm_nt(rotated[q], rows[:, LATENT:])) * scale
        score = jnp.where(slot < len_ref[q], score, -jnp.inf)
        seen = (new_at >= q * drafts) & (new_at - q * drafts <= draft)
        fresh = jnp.where(seen, fresh, -jnp.inf)
        peak = jnp.maximum(
            jnp.max(score, axis=1, keepdims=True), jnp.max(fresh, axis=1, keepdims=True)
        )
        score = jnp.exp(score - peak)
        fresh = jnp.exp(fresh - peak)
        total = jnp.sum(score, axis=1, keepdims=True) + jnp.sum(fresh, axis=1, keepdims=True)
        inverse = 1.0 / total
        mix = mm_nt((score * inverse).astype(bf16), keys[:LATENT])
        mix = mix + mm((fresh * inverse).astype(bf16), rows[:, :LATENT])
        mix = jnp.where(draft < count_ref[q], mix, 0.0).astype(bf16)
        out_ref[:, q * hd : (q + 1) * hd, :] = mix.reshape(owners, hd, LATENT)


def value_kernel(reqs, drafts, heads, latent_ref, uv_ref, out_ref):
    owners = latent_ref.shape[0]
    hd = heads * drafts
    rows = owners * reqs * drafts
    latent = latent_ref[...].reshape(owners * reqs * hd, LATENT)
    shape = (rows, owners * reqs * hd)
    m = lax.broadcasted_iota(jnp.int32, shape, 0)
    n = lax.broadcasted_iota(jnp.int32, shape, 1)
    wanted = (m // drafts) * hd + m % drafts
    for h in range(heads):
        pick = jnp.where(n == wanted + h * drafts, 1.0, 0.0).astype(bf16)
        mine = mm(pick, latent).astype(bf16)
        out_ref[:, h * VDIM : (h + 1) * VDIM] = mm(mine, uv_ref[h]).astype(bf16)


def output_kernel(core_ref, own_ref, other_ref, w_own_ref, w_other_ref, out_ref):
    out_ref[...] = (mm(own_ref[...], w_own_ref[...]) + mm(other_ref[...], w_other_ref[...])).astype(bf16)


def sum_kernel(replicas, pairs, x_ref, out_ref):
    width = x_ref.shape[-1]
    for r in range(replicas):
        for c in range(2):
            total = None
            for p in range(pairs):
                part = x_ref[(r * pairs + p) * 2 + c].astype(f32)
                total = part if total is None else total + part
            at = (r * 2 + c) * width
            out_ref[:, at : at + width] = total.astype(bf16)


def step(x, axis, size, k):
    return lax.ppermute(x, axis, [(i, i ^ k) for i in range(size)])


def shards(q_latent, q_gain, q_up, w_uk, w_uv, w_o, new_kv, latent_cache, cache_len, draft_count):
    rows_dev, qlat = q_latent.shape
    owners = lax.axis_size("tensor")
    replicas = lax.axis_size("replica")
    heads = w_uk.shape[0]
    reqs = cache_len.shape[0]
    drafts = rows_dev // reqs
    hd = heads * drafts
    me = lax.axis_index("tensor")
    core = me % 2

    half = w_o.shape[1] // 2
    away = lax.dynamic_slice_in_dim(w_o, (1 - core) * half, half, axis=1)
    w_other = step(away, "tensor", owners, 1)

    inner = min(4, owners)
    blocks = [q_latent] + [step(q_latent, "tensor", owners, k) for k in range(inner, owners, inner)]
    rows = jnp.stack(blocks)
    size = inner // 2
    rows = rows[:, None]
    while size:
        rows = jnp.concatenate([rows, step(rows, "tensor", owners, size)], axis=1)
        size //= 2
    order = [0]
    size = inner // 2
    while size:
        order = order + [o ^ size for o in order]
        size //= 2
    inverse = [order.index(i) for i in range(inner)]
    rows = jnp.stack([rows[:, i] for i in inverse], axis=1)
    rows = rows.reshape(owners * rows_dev, qlat)

    chunks = LATENT // LANES
    packed = (reqs * chunks + reqs * ROPE // LANES) * hd
    params = pltpu.CompilerParams(vmem_limit_bytes=32 * 1024 * 1024)
    queries = pl.pallas_call(
        functools.partial(query_kernel, reqs, drafts, heads),
        out_shape=jax.ShapeDtypeStruct((owners, packed, LANES), bf16),
        in_specs=[smem_spec()] + [vmem_spec()] * 4,
        out_specs=vmem_spec(),
        compiler_params=params,
        name="query",
    )(me[None].astype(jnp.int32), rows, q_gain[None, :], q_up, w_uk)
    arrived = lax.all_to_all(queries, "tensor", split_axis=0, concat_axis=0, tiled=True)

    frequency = rope_base ** (-(jnp.arange(ROPE // 2).astype(f32) * 2.0 / ROPE))
    positions = (cache_len[:, None] + jnp.arange(drafts)[None, :]).astype(f32)
    angles = positions[:, :, None] * frequency
    per = LANES // ROPE

    def table(first, second):
        lanes = jnp.concatenate([first, second], axis=-1)
        lanes = lanes.reshape(reqs // per, per, drafts, ROPE)
        lanes = jnp.swapaxes(lanes, 1, 2).reshape(reqs // per, 1, drafts, LANES)
        return jnp.broadcast_to(lanes, (reqs // per, heads, drafts, LANES)).reshape(reqs // per, hd, LANES)

    cosine = jnp.cos(angles)
    sine = jnp.sin(angles)
    latent = pl.pallas_call(
        functools.partial(attend_kernel, reqs, drafts, heads),
        out_shape=jax.ShapeDtypeStruct((owners, reqs * hd, LATENT), bf16),
        in_specs=[smem_spec()] * 2 + [vmem_spec()] * 5,
        out_specs=vmem_spec(),
        compiler_params=params,
        name="attend",
    )(cache_len, draft_count, arrived, table(cosine, cosine), table(-sine, sine), new_kv, jnp.swapaxes(latent_cache, 1, 2))
    returned = lax.all_to_all(latent, "tensor", split_axis=0, concat_axis=0, tiled=True)

    values = pl.pallas_call(
        functools.partial(value_kernel, reqs, drafts, heads),
        out_shape=jax.ShapeDtypeStruct((owners * rows_dev, heads * VDIM), bf16),
        in_specs=[vmem_spec()] * 2,
        out_specs=vmem_spec(),
        compiler_params=params,
        name="values",
    )(returned, w_uv)
    own = lax.all_gather(values, "replica", axis=0, tiled=True)
    other = step(own, "tensor", owners, 1)

    total_rows = own.shape[0]
    tile = half
    for t in (256, 128):
        if half % t == 0:
            tile = t
            break
    tiles = half // tile
    place = core if half % LANES == 0 else jnp.zeros_like(core)
    w_own = w_o if half % LANES == 0 else lax.dynamic_slice_in_dim(w_o, core * half, half, axis=1)
    depth = own.shape[1]
    product = pl.pallas_call(
        output_kernel,
        out_shape=jax.ShapeDtypeStruct((total_rows, half), bf16),
        grid_spec=pltpu.PrefetchScalarGridSpec(
            num_scalar_prefetch=1,
            grid=(tiles,),
            in_specs=[
                pl.BlockSpec((total_rows, depth), lambda i, c: (0, 0)),
                pl.BlockSpec((total_rows, depth), lambda i, c: (0, 0)),
                pl.BlockSpec((depth, tile), lambda i, c: (0, c[0] * tiles + i)),
                pl.BlockSpec((depth, tile), lambda i, c: (0, i)),
            ],
            out_specs=pl.BlockSpec((total_rows, tile), lambda i, c: (0, i)),
        ),
        compiler_params=params,
        name="output",
    )(place[None].astype(jnp.int32), own, other, w_own, w_other)
    product = product.reshape(replicas * owners, rows_dev, half)
    placed = lax.all_to_all(product, ("replica", "tensor"), split_axis=0, concat_axis=0, tiled=True)
    return pl.pallas_call(
        functools.partial(sum_kernel, replicas, owners // 2),
        out_shape=jax.ShapeDtypeStruct((rows_dev, replicas * 2 * half), bf16),
        in_specs=[vmem_spec()],
        out_specs=vmem_spec(),
        compiler_params=params,
        name="combine",
    )(placed)


def solution(mesh):
    rows = ("groups", "tensor", "replica")
    return jax.shard_map(
        shards,
        mesh=mesh,
        in_specs=(
            P(rows, None),
            P(),
            P(None, "tensor"),
            P("tensor", None, None),
            P("tensor", None, None),
            P("tensor", "replica"),
            P(rows, None),
            P(rows, None, None),
            P(rows),
            P(rows),
        ),
        out_specs=P(rows, None),
        check_vma=False,
    )
```

time: 171 us -> 106 us (0.62)
  waiting for transfers between devices: 75.5 us -> 23.1 us
  between operations: 13.7 us -> 0.16 us
  Pallas kernels: 0 us -> 12.4 us
  matrix products: 8.49 us -> 0 us
  starting transfers between devices: 3.62 us -> 11.3 us
  local copies, waits for them, and re-layouts: 9.49 us -> 4.86 us
  blocking collectives: 56.5 us -> 53 us
  other arithmetic: 3.07 us -> 1.06 us
    reduce_scatter x1 -> x0, waiting for transfers between devices: 60.6 us -> none  [shards(): lax.psum_scatter(product.reshape(block_rows * lax.axis_size('tensor'), w_...]
    all_gather x2 -> x1, blocking collectives: 30.4 us -> 6.21 us  [shards(): own = lax.all_gather(values, 'replica', axis=0, tiled=True)]
    all_to_all x2, blocking collectives: 26.1 us -> 46.8 us  [the longest x1 28.5 us: shards(): lax.all_to_all(product, ('replica', 'tensor'), split_axis=0, concat_axis=...]
    pallas_call x0 -> x5, Pallas kernels: none -> 12.4 us  [the longest x1 5.2 us: shards(): pl.pallas_call(output_kernel, out_shape=jax.ShapeDtypeStruct((total_rows,...]
    ppermute x0 -> x7, waiting for transfers between devices: none -> 11.2 us  [step(): return lax.ppermute(x, axis, [(i, i ^ k) for i in range(size)])]
    dot_general x8 -> x0, matrix products: 8.49 us -> none  [the longest x1 3.16 us: shards(): jnp.einsum('rtiv,vc->tric', spread, w_o, preferred_element_type=jnp.float32)]
    ppermute x0 -> x7, starting transfers between devices: none -> 7.57 us  [step(): return lax.ppermute(x, axis, [(i, i ^ k) for i in range(size)])]
    reshape x9 -> x0, local copies, waits for them, and re-layouts: 5.05 us -> none  [the longest x1 1.9 us: shards(): arrived = arrived.reshape(rows_dev, head_count, LATENT + ROPE)]
  transfers between devices with their start and end apart: 2 -> 8, of which waited for: 2 -> 6; matrix products, arithmetic and copies ran while one was open for 0% -> 4% of each run, Pallas kernels for 0% -> 4%
where the time goes in v1:
time: 106 us
  blocking collectives  53 us (50%)
  waiting for transfers between devices  23.1 us (22%)
  Pallas kernels  12.4 us (12%)
  starting transfers between devices  11.3 us (11%)
  local copies, waits for them, and re-layouts  4.86 us (5%)
  other arithmetic  1.06 us (1%)
    all_to_all x1, blocking collectives, shards(): lax.all_to_all(product, ('replica', 'tensor'), split_axis=0, concat_axis=...  28.5 us
    all_to_all x1, blocking collectives, shards(): lax.all_to_all(latent, 'tensor', split_axis=0, concat_axis=0, tiled=True)  18.4 us
    all_to_all x1, waiting for transfers between devices, shards(): lax.all_to_all(queries, 'tensor', split_axis=0, concat_axis=0, tiled=True)  11.9 us
    ppermute x7, waiting for transfers between devices, step(): return lax.ppermute(x, axis, [(i, i ^ k) for i in range(size)])  11.2 us
    ppermute x7, starting transfers between devices, step(): return lax.ppermute(x, axis, [(i, i ^ k) for i in range(size)])  7.57 us
    all_gather x1, blocking collectives, shards(): own = lax.all_gather(values, 'replica', axis=0, tiled=True)  6.21 us
    pallas_call x1, Pallas kernels, shards(): pl.pallas_call(output_kernel, out_shape=jax.ShapeDtypeStruct((total_rows,...  5.2 us
    all_to_all x1, starting transfers between devices, shards(): lax.all_to_all(queries, 'tensor', split_axis=0, concat_axis=0, tiled=True)  3.73 us
  transfers between devices with their start and end apart: 8, of which 6 were waited for; matrix products, arithmetic and copies ran while one was open for 4% of the time, Pallas kernels for 4%

profile of v1, /device:TPU:0, one launch (start us, length us, event | category | flops | bytes accessed | tf_op | source)
XLA Modules:
  0.0 105.9 jit_solution(16573730694930308187)
XLA Ops:
  0.0 3.1 %collective-permute-start = (bf16[8,1536]{1,0:T(8,128)(2,1)}, bf16[8,1536]{1,0:T(8,128)(2,1)S(1)}, u32[]{:S(2)}, u32[]{:S(2)}) collective-permute-start(bf16[8,1536]{1,0:T(8,128)(2,1)} %param.10), channel_id=1, source_target_pairs={{0,8},{2,10},{4,12},{6,14},{8,0},{10,2},{12,4},{14,6},{16,24},{18,... | collective-permute-start | bytes 73736 | tf_op jit(solution)/shard_map/ppermute | solution.py:164
  3.1 2.6 %collective-permute-start.1 = (bf16[8,1536]{1,0:T(8,128)(2,1)}, bf16[8,1536]{1,0:T(8,128)(2,1)S(1)}, u32[]{:S(2)}, u32[]{:S(2)}) collective-permute-start(bf16[8,1536]{1,0:T(8,128)(2,1)} %param.10), channel_id=1, source_target_pairs={{0,16},{2,18},{4,20},{6,22},{8,24},{10,26},{12,28},{14,30},{16,0},... | collective-permute-start | bytes 73736 | tf_op jit(solution)/shard_map/ppermute | solution.py:164
  5.6 0.0 collective-permute-start.2
  5.7 2.7 %collective-permute-done.1 = bf16[8,1536]{1,0:T(8,128)(2,1)S(1)} collective-permute-done((bf16[8,1536]{1,0:T(8,128)(2,1)}, bf16[8,1536]{1,0:T(8,128)(2,1)S(1)}, u32[]{:S(2)}, u32[]{:S(2)}) %collective-permute-start.1) | collective-permute-done | bytes 24608 | tf_op jit(solution)/shard_map/ppermute | solution.py:164
  8.3 3.1 %collective-permute-done.2 = bf16[8,1536]{1,0:T(8,128)(2,1)S(1)} collective-permute-done((bf16[8,1536]{1,0:T(8,128)(2,1)}, bf16[8,1536]{1,0:T(8,128)(2,1)S(1)}, u32[]{:S(2)}, u32[]{:S(2)}) %collective-permute-start.2) | collective-permute-done | bytes 24608 | tf_op jit(solution)/shard_map/ppermute | solution.py:164
  11.5 0.8 maximum_bitcast_fusion
  12.2 1.6 %collective-permute-start.3 = (bf16[4,1,8,1536]{3,2,0,1:T(8,128)(2,1)S(1)}, bf16[4,1,8,1536]{3,2,0,1:T(8,128)(2,1)S(1)}, u32[]{:S(2)}, u32[]{:S(2)}) collective-permute-start(bf16[4,1,8,1536]{3,2,0,1:T(8,128)(2,1)S(1)} %maximum_bitcast_fusion), channel_id=1, source_target_pairs={{0,4},{2,6},{4,0},{6,2},{8,12},{10,14},{12,8},{14,10},{16,20},{18,... | collective-permute-start | bytes 294920 | tf_op jit(solution)/shard_map/ppermute | solution.py:164
  13.8 3.1 %collective-permute-done.3 = bf16[4,1,8,1536]{3,2,0,1:T(8,128)(2,1)S(1)} collective-permute-done((bf16[4,1,8,1536]{3,2,0,1:T(8,128)(2,1)S(1)}, bf16[4,1,8,1536]{3,2,0,1:T(8,128)(2,1)S(1)}, u32[]{:S(2)}, u32[]{:S(2)}) %collective-permute-start.3) | collective-permute-done | bytes 98336 | tf_op jit(solution)/shard_map/ppermute | solution.py:164
  16.9 0.1 collective-permute-start.4
  17.0 0.7 broadcast_in_dim.37.gain_ref
  17.7 0.7 collective-permute-done.4
  18.5 0.1 pad_maximum_fusion
  18.6 0.0 copy-start.4
  18.6 1.0 copy-done.4
  19.6 2.3 %query.1 = bf16[16,144,128]{2,1,0:T(8,128)(2,1)} custom-call(s32[1]{0:T(128)} %bitcast.1.me_ref, bf16[128,1536]{1,0:T(8,128)(2,1)S(1)} %bitcast.23, f32[1,1536]{1,0:T(1,128)S(1)} %broadcast_in_dim.37.gain_ref, bf16[1536,768]{1,0:T(8,128)(2,1)S(1)} %copy-done.1, bf16[4,128,512]{2,1,0:T(8,128)(2,1)S(1)} %copy-done.4), custom_call_target="tpu_custom_call" | custom-call | tf_op jit(solution)/shard_map/query/pallas_call | solution.py:202
  21.9 3.7 %all-to-all-start = ((bf16[16,144,128]{2,1,0:T(8,128)(2,1)}), bf16[16,144,128]{2,1,0:T(8,128)(2,1)S(1)}, u32[]{:S(2)}, u32[]{:S(2)}) async-start(bf16[16,144,128]{2,1,0:T(8,128)(2,1)} %query.1), calls=%async_computation | async-start | bytes 1179648 | tf_op jit(solution)/shard_map/all_to_all | solution.py:210
  25.7 2.9 %constant_dynamic-slice_fusion = bf16[512,1792]{1,0:T(8,128)(2,1)} fusion(bf16[512,3584]{1,0:T(8,128)(2,1)} %w_own_ref.1, s32[]{:T(128)S(6)} %select_n.11), kind=kLoop, calls=%fused_computation.9 | loop fusion | bytes 3670020 | tf_op jit(solution)/shard_map/dynamic_slice | solution.py:179
  28.5 0.3 collective-permute-start.6
  28.8 0.1 fusion
  29.0 0.1 maximum_bitcast_fusion.1
  29.0 0.1 broadcast_in_dim.38
  29.1 0.1 broadcast_in_dim.41
  29.2 11.9 %all-to-all-done.q_ref = bf16[16,144,128]{2,1,0:T(8,128)(2,1)S(1)} async-done(((bf16[16,144,128]{2,1,0:T(8,128)(2,1)}), bf16[16,144,128]{2,1,0:T(8,128)(2,1)S(1)}, u32[]{:S(2)}, u32[]{:S(2)}) %all-to-all-start) | async-done | bytes 589856 | tf_op jit(solution)/shard_map/all_to_all | solution.py:210
  41.1 0.0 copy-start
  41.2 3.2 %attend.1 = bf16[16,32,512]{2,1,0:T(8,128)(2,1)S(1)} custom-call(s32[2]{0:T(128)S(1)} %copy-done.6, s32[2]{0:T(128)S(1)} %copy-done.7, bf16[16,144,128]{2,1,0:T(8,128)(2,1)S(1)} %all-to-all-done.q_ref, f32[1,16,128]{2,1,0:T(8,128)S(1)} %bitcast.24, f32[1,16,128]{2,1,0:T(8,128)S(1)} %bitcast.25, bf16[8,576]{1,0:T(8,128)(2,1)S(1)} %copy-done.5, ...), custom_call_target="tpu_custom_call" | custom-call | tf_op jit(solution)/shard_map/attend/pallas_call | solution.py:225
  44.3 18.4 %all_to_all.15.latent_ref = bf16[16,32,512]{2,1,0:T(8,128)(2,1)S(1)} all-to-all(bf16[16,32,512]{2,1,0:T(8,128)(2,1)S(1)} %attend.1), channel_id=1, replica_groups=mesh['groups'=1,'tensor'=16,'replica'=2] {'tensor'}, dimensions={0} | all-to-all | bytes 1048576 | tf_op jit(solution)/shard_map/all_to_all | solution.py:233
  62.7 1.0 values.1
  63.7 6.2 %all_gather.3.own_ref = bf16[256,512]{1,0:T(8,128)(2,1)S(1)} all-gather(bf16[128,512]{1,0:T(8,128)(2,1)S(1)} %values.1), channel_id=1, replica_groups=mesh['groups'=1,'tensor'=16,'replica'=2] {'replica'}, dimensions={0}, use_global_device_ids=true | all-gather | bytes 393216 | tf_op jit(solution)/shard_map/all_gather | solution.py:243
  69.9 1.5 %collective-permute-done.5.other_ref = bf16[256,512]{1,0:T(8,128)(2,1)S(1)} collective-permute-done((bf16[256,512]{1,0:T(8,128)(2,1)S(1)}, bf16[256,512]{1,0:T(8,128)(2,1)S(1)}, u32[]{:S(2)}, u32[]{:S(2)}) %collective-permute-start.5) | collective-permute-done | bytes 262176 | tf_op jit(solution)/shard_map/ppermute | solution.py:164
  71.4 5.2 %output.1 = bf16[256,1792]{1,0:T(8,128)(2,1)S(1)} custom-call(s32[1]{0:T(128)} %bitcast.core_ref, bf16[256,512]{1,0:T(8,128)(2,1)S(1)} %all_gather.3.own_ref, bf16[256,512]{1,0:T(8,128)(2,1)S(1)} %collective-permute-done.5.other_ref, bf16[512,3584]{1,0:T(8,128)(2,1)S(1)} %copy-done, bf16[512,1792]{1,0:T(8,128)(2,1)} %collective-permute-done.6.w_other_ref), custom_call_target="tpu_custom_call" | custom-call | tf_op jit(solution)/shard_map/output/pallas_call | solution.py:256
  76.7 28.5 %all_to_all.16.x_ref = bf16[32,8,1792]{2,1,0:T(8,128)(2,1)S(1)} all-to-all(bf16[32,8,1792]{2,1,0:T(8,128)(2,1)S(1)} %bitcast.21), channel_id=1, replica_groups=mesh['groups'=1,'tensor'=16,'replica'=2] {'replica','tensor'}, dimensions={0} | all-to-all | bytes 1835008 | tf_op jit(solution)/shard_map/all_to_all | solution.py:274
  105.1 0.8 combine.1
  (23 shorter events, 0.1 us)
Async XLA Ops:
  0.0 18.6 %copy-start.1 = (bf16[1536,768]{1,0:T(8,128)(2,1)S(1)}, bf16[1536,768]{1,0:T(8,128)(2,1)}, u32[]{:S(2)}) copy-start(bf16[1536,768]{1,0:T(8,128)(2,1)} %up_ref.1) | copy-start | bytes 7077892
  0.0 5.6 %collective-permute-start = (bf16[8,1536]{1,0:T(8,128)(2,1)}, bf16[8,1536]{1,0:T(8,128)(2,1)S(1)}, u32[]{:S(2)}, u32[]{:S(2)}) collective-permute-start(bf16[8,1536]{1,0:T(8,128)(2,1)} %param.10), channel_id=1, source_target_pairs={{0,8},{2,10},{4,12},{6,14},{8,0},{10,2},{12,4},{14,6},{16,24},{18,... | collective-permute-start | bytes 73736 | tf_op jit(solution)/shard_map/ppermute | solution.py:164
  3.1 5.3 %collective-permute-start.1 = (bf16[8,1536]{1,0:T(8,128)(2,1)}, bf16[8,1536]{1,0:T(8,128)(2,1)S(1)}, u32[]{:S(2)}, u32[]{:S(2)}) collective-permute-start(bf16[8,1536]{1,0:T(8,128)(2,1)} %param.10), channel_id=1, source_target_pairs={{0,16},{2,18},{4,20},{6,22},{8,24},{10,26},{12,28},{14,30},{16,0},... | collective-permute-start | bytes 73736 | tf_op jit(solution)/shard_map/ppermute | solution.py:164
  5.6 5.8 %collective-permute-start.2 = (bf16[8,1536]{1,0:T(8,128)(2,1)}, bf16[8,1536]{1,0:T(8,128)(2,1)S(1)}, u32[]{:S(2)}, u32[]{:S(2)}) collective-permute-start(bf16[8,1536]{1,0:T(8,128)(2,1)} %param.10), channel_id=1, source_target_pairs={{0,24},{2,26},{4,28},{6,30},{8,16},{10,18},{12,20},{14,22},{16,8},... | collective-permute-start | bytes 73736 | tf_op jit(solution)/shard_map/ppermute | solution.py:164
  12.2 4.7 %collective-permute-start.3 = (bf16[4,1,8,1536]{3,2,0,1:T(8,128)(2,1)S(1)}, bf16[4,1,8,1536]{3,2,0,1:T(8,128)(2,1)S(1)}, u32[]{:S(2)}, u32[]{:S(2)}) collective-permute-start(bf16[4,1,8,1536]{3,2,0,1:T(8,128)(2,1)S(1)} %maximum_bitcast_fusion), channel_id=1, source_target_pairs={{0,4},{2,6},{4,0},{6,2},{8,12},{10,14},{12,8},{14,10},{16,20},{18,... | collective-permute-start | bytes 294920 | tf_op jit(solution)/shard_map/ppermute | solution.py:164
  16.9 1.5 %collective-permute-start.4 = (bf16[4,2,8,1536]{3,2,0,1:T(8,128)(2,1)S(1)}, bf16[4,2,8,1536]{3,2,0,1:T(8,128)(2,1)S(1)}, u32[]{:S(2)}, u32[]{:S(2)}) collective-permute-start(bf16[4,2,8,1536]{3,2,0,1:T(8,128)(2,1)S(1)} %pad_maximum_fusion.1), channel_id=1, source_target_pairs={{0,2},{2,0},{4,6},{6,4},{8,10},{10,8},{12,14},{14,12},{16,18},{18,... | collective-permute-start | bytes 589832 | tf_op jit(solution)/shard_map/ppermute | solution.py:164
  18.6 1.0 copy-start.4
  21.9 6.9 %copy-start.6 = (s32[2]{0:T(128)S(1)}, s32[2]{0:T(128)}, u32[]{:S(2)}) copy-start(s32[2]{0:T(128)} %len_ref.1) | copy-start | bytes 28
  21.9 19.2 %copy-start.2 = (bf16[2,1024,576]{1,2,0:T(8,128)(2,1)S(1)}, bf16[2,1024,576]{1,2,0:T(8,128)(2,1)}, u32[]{:S(2)}) copy-start(bf16[2,1024,576]{1,2,0:T(8,128)(2,1)} %param.17) | copy-start | bytes 7077892
  21.9 19.2 %copy-start.5 = (bf16[8,576]{1,0:T(8,128)(2,1)S(1)}, bf16[8,576]{1,0:T(8,128)(2,1)}, u32[]{:S(2)}) copy-start(bf16[8,576]{1,0:T(8,128)(2,1)} %new_ref.1) | copy-start | bytes 27652
  21.9 19.2 %copy-start.7 = (s32[2]{0:T(128)S(1)}, s32[2]{0:T(128)}, u32[]{:S(2)}) copy-start(s32[2]{0:T(128)} %count_ref.1) | copy-start | bytes 28
  21.9 19.2 %all-to-all-start = ((bf16[16,144,128]{2,1,0:T(8,128)(2,1)}), bf16[16,144,128]{2,1,0:T(8,128)(2,1)S(1)}, u32[]{:S(2)}, u32[]{:S(2)}) async-start(bf16[16,144,128]{2,1,0:T(8,128)(2,1)} %query.1), calls=%async_computation | async-start | bytes 1179648 | tf_op jit(solution)/shard_map/all_to_all | solution.py:210
  28.5 34.2 %copy-start.3 = (bf16[4,512,128]{2,1,0:T(8,128)(2,1)S(1)}, bf16[4,512,128]{2,1,0:T(8,128)(2,1)}, u32[]{:S(2)}) copy-start(bf16[4,512,128]{2,1,0:T(8,128)(2,1)} %uv_ref.1) | copy-start | bytes 1572868
  28.5 41.4 %collective-permute-start.6 = (bf16[512,1792]{1,0:T(8,128)(2,1)}, bf16[512,1792]{1,0:T(8,128)(2,1)}, u32[]{:S(2)}, u32[]{:S(2)}) collective-permute-start(bf16[512,1792]{1,0:T(8,128)(2,1)} %constant_dynamic-slice_fusion), channel_id=1, source_target_pairs={{0,2},{2,0},{4,6},{6,4},{8,10},{10,8},{12,14},{14,12},{16,18},{18,... | collective-permute-start | bytes 5505032 | tf_op jit(solution)/shard_map/ppermute | solution.py:164
  41.1 30.3 %copy-start = (bf16[512,3584]{1,0:T(8,128)(2,1)S(1)}, bf16[512,3584]{1,0:T(8,128)(2,1)}, u32[]{:S(2)}) copy-start(bf16[512,3584]{1,0:T(8,128)(2,1)} %w_own_ref.1) | copy-start | bytes 11010052
  69.9 1.5 %collective-permute-start.5 = (bf16[256,512]{1,0:T(8,128)(2,1)S(1)}, bf16[256,512]{1,0:T(8,128)(2,1)S(1)}, u32[]{:S(2)}, u32[]{:S(2)}) collective-permute-start(bf16[256,512]{1,0:T(8,128)(2,1)S(1)} %all_gather.3.own_ref), channel_id=1, source_target_pairs={{0,2},{2,0},{4,6},{6,4},{8,10},{10,8},{12,14},{14,12},{16,18},{18,... | collective-permute-start | bytes 786440 | tf_op jit(solution)/shard_map/ppermute | solution.py:164

commit v2 on v1

--- a/solution.py
+++ b/solution.py
@@ -39,13 +39,43 @@
     return lax.dot_general(a, b, (((1,), (1,)), ((), ())), preferred_element_type=f32)
 
 
-def query_kernel(reqs, drafts, heads, me_ref, x_ref, gain_ref, up_ref, uk_ref, out_ref):
+def fetch_kernel(place_ref, *refs):
+    count = (len(refs) - 1) // 2
+    sems = refs[-1]
+    copies = []
+    for i in range(count):
+        source, target = refs[i], refs[count + i]
+        width = target.shape[-1]
+        if source.shape[-1] != width:
+            source = source.at[:, pl.ds(pl.multiple_of(place_ref[0] * width, LANES), width)]
+        copies.append(pltpu.make_async_copy(source, target, sems.at[i]))
+        copies[-1].start()
+    for copy in copies:
+        copy.wait()
+
+
+def fetch(place, arrays, shapes, name):
+    moved = sum(2 * 2 * shape[0] * shape[1] for shape in shapes)
+    return pl.pallas_call(
+        fetch_kernel,
+        out_shape=[pltpu.VMEM(shape, bf16) for shape in shapes],
+        in_specs=[smem_spec()] + [pl.BlockSpec(memory_space=pltpu.MemorySpace.HBM)] * len(arrays),
+        out_specs=[vmem_spec()] * len(arrays),
+        scratch_shapes=[pltpu.SemaphoreType.DMA((len(arrays),))],
+        compiler_params=pltpu.CompilerParams(vmem_limit_bytes=1024 * 1024),
+        cost_estimate=pl.CostEstimate(flops=0, bytes_accessed=moved, transcendentals=0),
+        name=name,
+    )(place, *arrays)
+
+
+def query_kernel(reqs, drafts, heads, place_ref, *refs):
+    *x_refs, gain_ref, up_ref, uk_ref, out_ref = refs
     owners = out_ref.shape[0]
     rows_dev = reqs * drafts
     hd = heads * drafts
-    x = x_ref[...].astype(f32)
+    x = jnp.concatenate([x_ref[...].astype(f32) for x_ref in x_refs], axis=0)
     scaled = x * lax.rsqrt(jnp.mean(x * x, axis=-1, keepdims=True) + rms_eps)
-    normed = (scaled * gain_ref[...]).astype(bf16)
+    normed = (scaled * gain_ref[...][None, :]).astype(bf16)
     full = mm(normed, up_ref[...]).astype(bf16)
     count = owners * reqs * hd
     shape = (count, owners * rows_dev)
@@ -53,8 +83,14 @@
     m = lax.broadcasted_iota(jnp.int32, shape, 1)
     target = n // (reqs * hd)
     local = (n // hd) % reqs * drafts + n % drafts
-    source = m // rows_dev
-    spread = jnp.where((target == (source ^ me_ref[0])) & (local == m % rows_dev), 1.0, 0.0)
+    block = m // rows_dev
+    distance = jnp.zeros_like(block)
+    bit = owners // 2
+    while bit:
+        distance = distance + block % 2 * bit
+        block = block // 2
+        bit //= 2
+    spread = jnp.where((target == (distance ^ place_ref[2])) & (local == m % rows_dev), 1.0, 0.0)
     wide = mm(spread.astype(bf16), full)
     row_head = (lax.broadcasted_iota(jnp.int32, (count, 1), 0) // drafts) % heads
     absorbed = None
@@ -62,7 +98,7 @@
     for h in range(heads):
         mine = row_head == h
         nope_h = jnp.where(mine, wide[:, h * QKD : h * QKD + NOPE], 0.0).astype(bf16)
-        part = mm(nope_h, uk_ref[h])
+        part = mm(nope_h, uk_ref[h * NOPE : (h + 1) * NOPE])
         absorbed = part if absorbed is None else absorbed + part
         rope_h = jnp.where(mine, wide[:, h * QKD + NOPE : (h + 1) * QKD], 0.0)
         rope = rope_h if rope is None else rope + rope_h
@@ -144,8 +180,17 @@
         out_ref[:, h * VDIM : (h + 1) * VDIM] = mm(mine, uv_ref[h]).astype(bf16)
 
 
-def output_kernel(core_ref, own_ref, other_ref, w_own_ref, w_other_ref, out_ref):
-    out_ref[...] = (mm(own_ref[...], w_own_ref[...]) + mm(other_ref[...], w_other_ref[...])).astype(bf16)
+def output_kernel(place_ref, *refs):
+    *value_refs, w_own_ref, w_other_ref, out_ref = refs
+    replicas, rows, half = out_ref.shape
+    own = jnp.concatenate([ref[...] for ref in value_refs[:replicas]], axis=0)
+    other = jnp.concatenate([ref[...] for ref in value_refs[replicas:]], axis=0)
+    tile = 256 if half % 256 == 0 else half
+    for at in range(0, half, tile):
+        part = mm(own, w_own_ref[:, at : at + tile]) + mm(other, w_other_ref[:, at : at + tile])
+        part = part.astype(bf16)
+        for k in range(replicas):
+            out_ref[place_ref[1] ^ k, :, at : at + tile] = part[k * rows : (k + 1) * rows]
 
 
 def sum_kernel(replicas, pairs, x_ref, out_ref):
@@ -179,22 +224,19 @@
     away = lax.dynamic_slice_in_dim(w_o, (1 - core) * half, half, axis=1)
     w_other = step(away, "tensor", owners, 1)
 
-    inner = min(4, owners)
-    blocks = [q_latent] + [step(q_latent, "tensor", owners, k) for k in range(inner, owners, inner)]
-    rows = jnp.stack(blocks)
-    size = inner // 2
-    rows = rows[:, None]
-    while size:
-        rows = jnp.concatenate([rows, step(rows, "tensor", owners, size)], axis=1)
-        size //= 2
-    order = [0]
-    size = inner // 2
-    while size:
-        order = order + [o ^ size for o in order]
-        size //= 2
-    inverse = [order.index(i) for i in range(inner)]
-    rows = jnp.stack([rows[:, i] for i in inverse], axis=1)
-    rows = rows.reshape(owners * rows_dev, qlat)
+    place = jnp.stack([core, lax.axis_index("replica"), me]).astype(jnp.int32)
+    w_uk = w_uk.reshape(heads * NOPE, LATENT)
+    up_near, uk_near = fetch(place, (q_up, w_uk), (q_up.shape, w_uk.shape), "near_query")
+
+    rows = q_latent
+    bit = owners // 2
+    while bit > 2:
+        rows = jnp.concatenate([rows, step(rows, "tensor", owners, bit)], axis=0)
+        bit //= 2
+    parts = [rows]
+    while bit:
+        parts = parts + [step(part, "tensor", owners, bit) for part in parts]
+        bit //= 2
 
     chunks = LATENT // LANES
     packed = (reqs * chunks + reqs * ROPE // LANES) * hd
@@ -202,11 +244,11 @@
     queries = pl.pallas_call(
         functools.partial(query_kernel, reqs, drafts, heads),
         out_shape=jax.ShapeDtypeStruct((owners, packed, LANES), bf16),
-        in_specs=[smem_spec()] + [vmem_spec()] * 4,
+        in_specs=[smem_spec()] + [vmem_spec()] * (len(parts) + 3),
         out_specs=vmem_spec(),
         compiler_params=params,
         name="query",
-    )(me[None].astype(jnp.int32), rows, q_gain[None, :], q_up, w_uk)
+    )(place, *parts, q_gain, up_near, uk_near)
     arrived = lax.all_to_all(queries, "tensor", split_axis=0, concat_axis=0, tiled=True)
 
     frequency = rope_base ** (-(jnp.arange(ROPE // 2).astype(f32) * 2.0 / ROPE))
@@ -240,36 +282,21 @@
         compiler_params=params,
         name="values",
     )(returned, w_uv)
-    own = lax.all_gather(values, "replica", axis=0, tiled=True)
-    other = step(own, "tensor", owners, 1)
-
-    total_rows = own.shape[0]
-    tile = half
-    for t in (256, 128):
-        if half % t == 0:
-            tile = t
-            break
-    tiles = half // tile
-    place = core if half % LANES == 0 else jnp.zeros_like(core)
-    w_own = w_o if half % LANES == 0 else lax.dynamic_slice_in_dim(w_o, core * half, half, axis=1)
-    depth = own.shape[1]
+    own = [values] + [step(values, "replica", replicas, k) for k in range(1, replicas)]
+    other = [step(piece, "tensor", owners, 1) for piece in own]
+
+    w_own = w_o
+    if half % LANES:
+        w_own = lax.dynamic_slice_in_dim(w_o, core * half, half, axis=1)
+    w_own, w_other = fetch(place, (w_own, w_other), (w_other.shape,) * 2, "near_output")
     product = pl.pallas_call(
         output_kernel,
-        out_shape=jax.ShapeDtypeStruct((total_rows, half), bf16),
-        grid_spec=pltpu.PrefetchScalarGridSpec(
-            num_scalar_prefetch=1,
-            grid=(tiles,),
-            in_specs=[
-                pl.BlockSpec((total_rows, depth), lambda i, c: (0, 0)),
-                pl.BlockSpec((total_rows, depth), lambda i, c: (0, 0)),
-                pl.BlockSpec((depth, tile), lambda i, c: (0, c[0] * tiles + i)),
-                pl.BlockSpec((depth, tile), lambda i, c: (0, i)),
-            ],
-            out_specs=pl.BlockSpec((total_rows, tile), lambda i, c: (0, i)),
-        ),
+        out_shape=jax.ShapeDtypeStruct((replicas, owners * rows_dev, half), bf16),
+        in_specs=[smem_spec()] + [vmem_spec()] * (2 * replicas + 2),
+        out_specs=vmem_spec(),
         compiler_params=params,
         name="output",
-    )(place[None].astype(jnp.int32), own, other, w_own, w_other)
+    )(place, *own, *other, w_own, w_other)
     product = product.reshape(replicas * owners, rows_dev, half)
     placed = lax.all_to_all(product, ("replica", "tensor"), split_axis=0, concat_axis=0, tiled=True)
     return pl.pallas_call(

time: 106 us -> 106 us (level)
  blocking collectives: 53 us -> 47.1 us
  starting transfers between devices: 11.3 us -> 16.5 us
  local copies, waits for them, and re-layouts: 4.86 us -> 6.58 us
  waiting for transfers between devices: 23.1 us -> 21.8 us
    all_gather x1 -> x0, blocking collectives: 6.21 us -> none  [shards(): own = lax.all_gather(values, 'replica', axis=0, tiled=True)]
    all_to_all x1, starting transfers between devices: 3.73 us -> 6.66 us  [shards(): lax.all_to_all(queries, 'tensor', split_axis=0, concat_axis=0, tiled=True)]
    unnamed x16 -> x20, local copies, waits for them, and re-layouts: 1.07 us -> 3.51 us
    ppermute x7 -> x9, starting transfers between devices: 7.57 us -> 9.88 us  [step(): return lax.ppermute(x, axis, [(i, i ^ k) for i in range(size)])]
    ppermute x7 -> x9, waiting for transfers between devices: 11.2 us -> 10.2 us  [step(): return lax.ppermute(x, axis, [(i, i ^ k) for i in range(size)])]
    pallas_call x1 -> x3, Pallas kernels: 5.2 us -> 4.61 us  [the longest x2 2.94 us: fetch(): pl.pallas_call(fetch_kernel, out_shape=[pltpu.VMEM(shape, bf16) for shape...]
  transfers between devices with their start and end apart: 8 -> 10, of which waited for: 6 -> 5; matrix products, arithmetic and copies ran while one was open for 4% -> 4% of each run, Pallas kernels for 4% -> 7%
where the time goes in v2:
time: 106 us
  blocking collectives  47.1 us (44%)
  waiting for transfers between devices  21.8 us (21%)
  starting transfers between devices  16.5 us (16%)
  Pallas kernels  12.4 us (12%)
  local copies, waits for them, and re-layouts  6.58 us (6%)
    all_to_all x1, blocking collectives, shards(): lax.all_to_all(product, ('replica', 'tensor'), split_axis=0, concat_axis=...  28.5 us
    all_to_all x1, blocking collectives, shards(): lax.all_to_all(latent, 'tensor', split_axis=0, concat_axis=0, tiled=True)  18.5 us
    all_to_all x1, waiting for transfers between devices, shards(): lax.all_to_all(queries, 'tensor', split_axis=0, concat_axis=0, tiled=True)  11.7 us
    ppermute x9, waiting for transfers between devices, step(): return lax.ppermute(x, axis, [(i, i ^ k) for i in range(size)])  10.2 us
    ppermute x9, starting transfers between devices, step(): return lax.ppermute(x, axis, [(i, i ^ k) for i in range(size)])  9.88 us
    all_to_all x1, starting transfers between devices, shards(): lax.all_to_all(queries, 'tensor', split_axis=0, concat_axis=0, tiled=True)  6.66 us
    unnamed x20, local copies, waits for them, and re-layouts  3.51 us
    pallas_call x1, Pallas kernels, shards(): pl.pallas_call(functools.partial(attend_kernel, reqs, drafts, heads), out...  3.19 us
  transfers between devices with their start and end apart: 10, of which 5 were waited for; matrix products, arithmetic and copies ran while one was open for 4% of the time, Pallas kernels for 7%

profile of v2, /device:TPU:0, one launch (start us, length us, event | category | flops | bytes accessed | tf_op | source)
XLA Modules:
  0.0 105.6 jit_solution(9843348174905283966)
XLA Ops:
  0.0 4.1 %collective-permute-start = (bf16[8,1536]{1,0:T(8,128)(2,1)}, bf16[8,1536]{1,0:T(8,128)(2,1)S(1)}, u32[]{:S(2)}, u32[]{:S(2)}) collective-permute-start(bf16[8,1536]{1,0:T(8,128)(2,1)} %param.10), channel_id=1, source_target_pairs={{0,16},{2,18},{4,20},{6,22},{8,24},{10,26},{12,28},{14,30},{16,0},... | collective-permute-start | bytes 73736 | tf_op jit(solution)/shard_map/ppermute | solution.py:209
  4.1 0.8 constant_dynamic-update-slice_fusion.2
  4.8 1.3 %collective-permute-done = bf16[8,1536]{1,0:T(8,128)(2,1)S(1)} collective-permute-done((bf16[8,1536]{1,0:T(8,128)(2,1)}, bf16[8,1536]{1,0:T(8,128)(2,1)S(1)}, u32[]{:S(2)}, u32[]{:S(2)}) %collective-permute-start) | collective-permute-done | bytes 24608 | tf_op jit(solution)/shard_map/ppermute | solution.py:209
  6.1 0.7 pad_maximum_fusion
  6.8 1.9 %collective-permute-start.1 = (bf16[16,1536]{1,0:T(8,128)(2,1)S(1)}, bf16[16,1536]{1,0:T(8,128)(2,1)S(1)}, u32[]{:S(2)}, u32[]{:S(2)}) collective-permute-start(bf16[16,1536]{1,0:T(8,128)(2,1)S(1)} %pad_maximum_fusion), channel_id=1, source_target_pairs={{0,8},{2,10},{4,12},{6,14},{8,0},{10,2},{12,4},{14,6},{16,24},{18,... | collective-permute-start | bytes 147464 | tf_op jit(solution)/shard_map/ppermute | solution.py:209
  8.7 2.2 %collective-permute-done.1 = bf16[16,1536]{1,0:T(8,128)(2,1)S(1)} collective-permute-done((bf16[16,1536]{1,0:T(8,128)(2,1)S(1)}, bf16[16,1536]{1,0:T(8,128)(2,1)S(1)}, u32[]{:S(2)}, u32[]{:S(2)}) %collective-permute-start.1) | collective-permute-done | bytes 49184 | tf_op jit(solution)/shard_map/ppermute | solution.py:209
  10.9 2.0 %collective-permute-start.2 = (bf16[32,1536]{1,0:T(8,128)(2,1)S(1)}, bf16[32,1536]{1,0:T(8,128)(2,1)S(1)}, u32[]{:S(2)}, u32[]{:S(2)}) collective-permute-start(bf16[32,1536]{1,0:T(8,128)(2,1)S(1)} %constant_dynamic-update-slice_fusion.refs_0_), channel_id=1, source_target_pairs={{0,4},{2,6},{4,0},{6,2},{8,12},{10,14},{12,8},{14,10},{16,20},{18,... | collective-permute-start | bytes 294920 | tf_op jit(solution)/shard_map/ppermute | solution.py:209
  12.9 2.6 %collective-permute-done.2.refs_1_ = bf16[32,1536]{1,0:T(8,128)(2,1)S(1)} collective-permute-done((bf16[32,1536]{1,0:T(8,128)(2,1)S(1)}, bf16[32,1536]{1,0:T(8,128)(2,1)S(1)}, u32[]{:S(2)}, u32[]{:S(2)}) %collective-permute-start.2) | collective-permute-done | bytes 98336 | tf_op jit(solution)/shard_map/ppermute | solution.py:209
  15.6 0.1 pad_add_fusion.place_ref
  15.6 1.7 %copy-done.1 = bf16[1536,768]{1,0:T(8,128)(2,1)S(1)} copy-done((bf16[1536,768]{1,0:T(8,128)(2,1)S(1)}, bf16[1536,768]{1,0:T(8,128)(2,1)}, u32[]{:S(2)}) %copy-start.1) | copy-done | bytes 2359320
  17.3 1.0 copy-done.4
  18.3 0.8 near_query.1
  19.1 0.0 collective-permute-done.3.refs_2_
  19.1 2.8 %query.1 = bf16[16,144,128]{2,1,0:T(8,128)(2,1)} custom-call(s32[3]{0:T(128)S(1)} %pad_add_fusion.place_ref, bf16[32,1536]{1,0:T(8,128)(2,1)S(1)} %constant_dynamic-update-slice_fusion.refs_0_, bf16[32,1536]{1,0:T(8,128)(2,1)S(1)} %collective-permute-done.2.refs_1_, bf16[32,1536]{1,0:T(8,128)(2,1)S(1)} %collective-permute-done.3.refs_2_, ...), custom_call_target="tpu_custom_call" | custom-call | tf_op jit(solution)/shard_map/query/pallas_call | solution.py:244
  22.0 6.7 %all-to-all-start = ((bf16[16,144,128]{2,1,0:T(8,128)(2,1)}), bf16[16,144,128]{2,1,0:T(8,128)(2,1)S(1)}, u32[]{:S(2)}, u32[]{:S(2)}) async-start(bf16[16,144,128]{2,1,0:T(8,128)(2,1)} %query.1), calls=%async_computation | async-start | bytes 1179648 | tf_op jit(solution)/shard_map/all_to_all | solution.py:252
  28.6 2.9 %constant_dynamic-slice_fusion = bf16[512,1792]{1,0:T(8,128)(2,1)} fusion(bf16[512,3584]{1,0:T(8,128)(2,1)} %refs_0_.3, s32[]{:T(128)S(6)} %select_n.11), kind=kLoop, calls=%fused_computation.11 | loop fusion | bytes 3670020 | tf_op jit(solution)/shard_map/dynamic_slice | solution.py:224
  31.5 0.4 collective-permute-start.8
  31.9 0.1 fusion
  32.1 0.1 maximum_bitcast_fusion
  32.2 0.1 broadcast_in_dim.22
  32.3 0.1 broadcast_in_dim.25
  32.3 11.7 %all-to-all-done.q_ref = bf16[16,144,128]{2,1,0:T(8,128)(2,1)S(1)} async-done(((bf16[16,144,128]{2,1,0:T(8,128)(2,1)}), bf16[16,144,128]{2,1,0:T(8,128)(2,1)S(1)}, u32[]{:S(2)}, u32[]{:S(2)}) %all-to-all-start) | async-done | bytes 589856 | tf_op jit(solution)/shard_map/all_to_all | solution.py:252
  44.0 0.0 copy-start
  44.0 3.2 %attend.1 = bf16[16,32,512]{2,1,0:T(8,128)(2,1)S(1)} custom-call(s32[2]{0:T(128)S(1)} %copy-done.7, s32[2]{0:T(128)S(1)} %copy-done.8, bf16[16,144,128]{2,1,0:T(8,128)(2,1)S(1)} %all-to-all-done.q_ref, f32[1,16,128]{2,1,0:T(8,128)S(1)} %bitcast.19, f32[1,16,128]{2,1,0:T(8,128)S(1)} %bitcast.20, bf16[8,576]{1,0:T(8,128)(2,1)S(1)} %copy-done.5, ...), custom_call_target="tpu_custom_call" | custom-call | tf_op jit(solution)/shard_map/attend/pallas_call | solution.py:267
  47.2 18.5 %all_to_all.15.latent_ref = bf16[16,32,512]{2,1,0:T(8,128)(2,1)S(1)} all-to-all(bf16[16,32,512]{2,1,0:T(8,128)(2,1)S(1)} %attend.1), channel_id=1, replica_groups=mesh['groups'=1,'tensor'=16,'replica'=2] {'tensor'}, dimensions={0} | all-to-all | bytes 1048576 | tf_op jit(solution)/shard_map/all_to_all | solution.py:275
  65.8 1.0 values.1.refs_0_
  66.8 1.5 %collective-permute-start.5 = (bf16[128,512]{1,0:T(8,128)(2,1)S(1)}, bf16[128,512]{1,0:T(8,128)(2,1)S(1)}, u32[]{:S(2)}, u32[]{:S(2)}) collective-permute-start(bf16[128,512]{1,0:T(8,128)(2,1)S(1)} %values.1.refs_0_), channel_id=1, source_target_pairs={{0,1},{1,0},{2,3},{3,2},{4,5},{5,4},{6,7},{7,6},{8,9},{9,8},{10,11... | collective-permute-start | bytes 393224 | tf_op jit(solution)/shard_map/ppermute | solution.py:209
  68.3 4.1 %collective-permute-done.5.refs_1_ = bf16[128,512]{1,0:T(8,128)(2,1)S(1)} collective-permute-done((bf16[128,512]{1,0:T(8,128)(2,1)S(1)}, bf16[128,512]{1,0:T(8,128)(2,1)S(1)}, u32[]{:S(2)}, u32[]{:S(2)}) %collective-permute-start.5) | collective-permute-done | bytes 131104 | tf_op jit(solution)/shard_map/ppermute | solution.py:209
  72.4 2.2 %near_output.1 = (bf16[512,1792]{1,0:T(8,128)(2,1)S(1)}, bf16[512,1792]{1,0:T(8,128)(2,1)S(1)}) custom-call(s32[3]{0:T(128)S(1)} %pad_add_fusion.place_ref, bf16[512,3584]{1,0:T(8,128)(2,1)S(1)} %copy-done, bf16[512,1792]{1,0:T(8,128)(2,1)} %collective-permute-done.8.refs_1_), custom_call_target="tpu_custom_call" | custom-call | bytes 7340032 | tf_op jit(solution)/shard_map/near_output/pallas_call | solution.py:59
  74.6 1.7 %output.1 = bf16[2,128,1792]{2,1,0:T(8,128)(2,1)S(1)} custom-call(s32[3]{0:T(128)S(1)} %pad_add_fusion.place_ref, bf16[128,512]{1,0:T(8,128)(2,1)S(1)} %values.1.refs_0_, bf16[128,512]{1,0:T(8,128)(2,1)S(1)} %collective-permute-done.5.refs_1_, bf16[128,512]{1,0:T(8,128)(2,1)S(1)} %collective-permute-done.6.refs_2_, ...), custom_call_target="tpu_custom_call" | custom-call | tf_op jit(solution)/shard_map/output/pallas_call | solution.py:292
  76.3 28.5 %all_to_all.16.x_ref = bf16[32,8,1792]{2,1,0:T(8,128)(2,1)S(1)} all-to-all(bf16[32,8,1792]{2,1,0:T(8,128)(2,1)S(1)} %bitcast.16), channel_id=1, replica_groups=mesh['groups'=1,'tensor'=16,'replica'=2] {'replica','tensor'}, dimensions={0} | all-to-all | bytes 1835008 | tf_op jit(solution)/shard_map/all_to_all | solution.py:301
  104.8 0.8 combine.1
  (29 shorter events, 0.1 us)
Async XLA Ops:
  0.0 19.1 %copy-start.6 = (f32[1536]{0:T(1024)S(1)}, f32[1536]{0:T(1024)}, u32[]{:S(2)}) copy-start(f32[1536]{0:T(1024)} %refs_4_.1) | copy-start | bytes 18436
  0.0 6.1 %collective-permute-start = (bf16[8,1536]{1,0:T(8,128)(2,1)}, bf16[8,1536]{1,0:T(8,128)(2,1)S(1)}, u32[]{:S(2)}, u32[]{:S(2)}) collective-permute-start(bf16[8,1536]{1,0:T(8,128)(2,1)} %param.10), channel_id=1, source_target_pairs={{0,16},{2,18},{4,20},{6,22},{8,24},{10,26},{12,28},{14,30},{16,0},... | collective-permute-start | bytes 73736 | tf_op jit(solution)/shard_map/ppermute | solution.py:209
  6.8 4.1 %collective-permute-start.1 = (bf16[16,1536]{1,0:T(8,128)(2,1)S(1)}, bf16[16,1536]{1,0:T(8,128)(2,1)S(1)}, u32[]{:S(2)}, u32[]{:S(2)}) collective-permute-start(bf16[16,1536]{1,0:T(8,128)(2,1)S(1)} %pad_maximum_fusion), channel_id=1, source_target_pairs={{0,8},{2,10},{4,12},{6,14},{8,0},{10,2},{12,4},{14,6},{16,24},{18,... | collective-permute-start | bytes 147464 | tf_op jit(solution)/shard_map/ppermute | solution.py:209
  10.9 4.6 %collective-permute-start.2 = (bf16[32,1536]{1,0:T(8,128)(2,1)S(1)}, bf16[32,1536]{1,0:T(8,128)(2,1)S(1)}, u32[]{:S(2)}, u32[]{:S(2)}) collective-permute-start(bf16[32,1536]{1,0:T(8,128)(2,1)S(1)} %constant_dynamic-update-slice_fusion.refs_0_), channel_id=1, source_target_pairs={{0,4},{2,6},{4,0},{6,2},{8,12},{10,14},{12,8},{14,10},{16,20},{18,... | collective-permute-start | bytes 294920 | tf_op jit(solution)/shard_map/ppermute | solution.py:209
  12.9 6.2 %collective-permute-start.3 = (bf16[32,1536]{1,0:T(8,128)(2,1)S(1)}, bf16[32,1536]{1,0:T(8,128)(2,1)S(1)}, u32[]{:S(2)}, u32[]{:S(2)}) collective-permute-start(bf16[32,1536]{1,0:T(8,128)(2,1)S(1)} %constant_dynamic-update-slice_fusion.refs_0_), channel_id=1, source_target_pairs={{0,2},{2,0},{4,6},{6,4},{8,10},{10,8},{12,14},{14,12},{16,18},{18,... | collective-permute-start | bytes 294920 | tf_op jit(solution)/shard_map/ppermute | solution.py:209
  15.5 3.6 %collective-permute-start.4 = (bf16[32,1536]{1,0:T(8,128)(2,1)S(1)}, bf16[32,1536]{1,0:T(8,128)(2,1)S(1)}, u32[]{:S(2)}, u32[]{:S(2)}) collective-permute-start(bf16[32,1536]{1,0:T(8,128)(2,1)S(1)} %collective-permute-done.2.refs_1_), channel_id=1, source_target_pairs={{0,2},{2,0},{4,6},{6,4},{8,10},{10,8},{12,14},{14,12},{16,18},{18,... | collective-permute-start | bytes 294920 | tf_op jit(solution)/shard_map/ppermute | solution.py:209
  15.6 1.7 %copy-start.1 = (bf16[1536,768]{1,0:T(8,128)(2,1)S(1)}, bf16[1536,768]{1,0:T(8,128)(2,1)}, u32[]{:S(2)}) copy-start(bf16[1536,768]{1,0:T(8,128)(2,1)} %refs_0_.2) | copy-start | bytes 7077892
  17.3 1.0 copy-start.4
  21.9 10.0 %copy-start.7 = (s32[2]{0:T(128)S(1)}, s32[2]{0:T(128)}, u32[]{:S(2)}) copy-start(s32[2]{0:T(128)} %len_ref.1) | copy-start | bytes 28
  21.9 22.1 %copy-start.2 = (bf16[2,1024,576]{1,2,0:T(8,128)(2,1)S(1)}, bf16[2,1024,576]{1,2,0:T(8,128)(2,1)}, u32[]{:S(2)}) copy-start(bf16[2,1024,576]{1,2,0:T(8,128)(2,1)} %param.17) | copy-start | bytes 7077892
  21.9 22.1 %copy-start.5 = (bf16[8,576]{1,0:T(8,128)(2,1)S(1)}, bf16[8,576]{1,0:T(8,128)(2,1)}, u32[]{:S(2)}) copy-start(bf16[8,576]{1,0:T(8,128)(2,1)} %new_ref.1) | copy-start | bytes 27652
  21.9 22.1 %copy-start.8 = (s32[2]{0:T(128)S(1)}, s32[2]{0:T(128)}, u32[]{:S(2)}) copy-start(s32[2]{0:T(128)} %count_ref.1) | copy-start | bytes 28
  22.0 22.0 %all-to-all-start = ((bf16[16,144,128]{2,1,0:T(8,128)(2,1)}), bf16[16,144,128]{2,1,0:T(8,128)(2,1)S(1)}, u32[]{:S(2)}, u32[]{:S(2)}) async-start(bf16[16,144,128]{2,1,0:T(8,128)(2,1)} %query.1), calls=%async_computation | async-start | bytes 1179648 | tf_op jit(solution)/shard_map/all_to_all | solution.py:252
  31.5 34.3 %copy-start.3 = (bf16[4,512,128]{2,1,0:T(8,128)(2,1)S(1)}, bf16[4,512,128]{2,1,0:T(8,128)(2,1)}, u32[]{:S(2)}) copy-start(bf16[4,512,128]{2,1,0:T(8,128)(2,1)} %uv_ref.1) | copy-start | bytes 1572868
  31.5 40.9 %collective-permute-start.8 = (bf16[512,1792]{1,0:T(8,128)(2,1)}, bf16[512,1792]{1,0:T(8,128)(2,1)}, u32[]{:S(2)}, u32[]{:S(2)}) collective-permute-start(bf16[512,1792]{1,0:T(8,128)(2,1)} %constant_dynamic-slice_fusion), channel_id=1, source_target_pairs={{0,2},{2,0},{4,6},{6,4},{8,10},{10,8},{12,14},{14,12},{16,18},{18,... | collective-permute-start | bytes 5505032 | tf_op jit(solution)/shard_map/ppermute | solution.py:209
  44.0 28.4 %copy-start = (bf16[512,3584]{1,0:T(8,128)(2,1)S(1)}, bf16[512,3584]{1,0:T(8,128)(2,1)}, u32[]{:S(2)}) copy-start(bf16[512,3584]{1,0:T(8,128)(2,1)} %refs_0_.3) | copy-start | bytes 11010052
  66.8 5.6 %collective-permute-start.5 = (bf16[128,512]{1,0:T(8,128)(2,1)S(1)}, bf16[128,512]{1,0:T(8,128)(2,1)S(1)}, u32[]{:S(2)}, u32[]{:S(2)}) collective-permute-start(bf16[128,512]{1,0:T(8,128)(2,1)S(1)} %values.1.refs_0_), channel_id=1, source_target_pairs={{0,1},{1,0},{2,3},{3,2},{4,5},{5,4},{6,7},{7,6},{8,9},{9,8},{10,11... | collective-permute-start | bytes 393224 | tf_op jit(solution)/shard_map/ppermute | solution.py:209
  68.3 6.3 %collective-permute-start.6 = (bf16[128,512]{1,0:T(8,128)(2,1)S(1)}, bf16[128,512]{1,0:T(8,128)(2,1)S(1)}, u32[]{:S(2)}, u32[]{:S(2)}) collective-permute-start(bf16[128,512]{1,0:T(8,128)(2,1)S(1)} %values.1.refs_0_), channel_id=1, source_target_pairs={{0,2},{2,0},{4,6},{6,4},{8,10},{10,8},{12,14},{14,12},{16,18},{18,... | collective-permute-start | bytes 393224 | tf_op jit(solution)/shard_map/ppermute | solution.py:209
  72.4 2.2 %collective-permute-start.7 = (bf16[128,512]{1,0:T(8,128)(2,1)S(1)}, bf16[128,512]{1,0:T(8,128)(2,1)S(1)}, u32[]{:S(2)}, u32[]{:S(2)}) collective-permute-start(bf16[128,512]{1,0:T(8,128)(2,1)S(1)} %collective-permute-done.5.refs_1_), channel_id=1, source_target_pairs={{0,2},{2,0},{4,6},{6,4},{8,10},{10,8},{12,14},{14,12},{16,18},{18,... | collective-permute-start | bytes 393224 | tf_op jit(solution)/shard_map/ppermute | solution.py:209

commit v3 on v2

--- a/solution.py
+++ b/solution.py
@@ -7,6 +7,7 @@
 from jax.experimental.pallas import tpu as pltpu
 from jax.sharding import PartitionSpec as P
 
+
 LATENT = 512
 ROPE = 64
 NOPE = 128
@@ -31,6 +32,14 @@
     return pl.BlockSpec(memory_space=SMEM)
 
 
+def over(x, n):
+    return x >> (n.bit_length() - 1) if n & (n - 1) == 0 else x // n
+
+
+def rest(x, n):
+    return x & (n - 1) if n & (n - 1) == 0 else x % n
+
+
 def mm(a, b):
     return jnp.dot(a, b, preferred_element_type=f32)
 
@@ -39,33 +48,27 @@
     return lax.dot_general(a, b, (((1,), (1,)), ((), ())), preferred_element_type=f32)
 
 
-def fetch_kernel(place_ref, *refs):
-    count = (len(refs) - 1) // 2
-    sems = refs[-1]
-    copies = []
-    for i in range(count):
-        source, target = refs[i], refs[count + i]
-        width = target.shape[-1]
-        if source.shape[-1] != width:
-            source = source.at[:, pl.ds(pl.multiple_of(place_ref[0] * width, LANES), width)]
-        copies.append(pltpu.make_async_copy(source, target, sems.at[i]))
-        copies[-1].start()
+def fetch_kernel(*refs):
+    count = len(refs) // 2
+    copies = [pltpu.make_async_copy(refs[i], refs[count + i], refs[-1].at[i]) for i in range(count)]
+    for copy in copies:
+        copy.start()
     for copy in copies:
         copy.wait()
 
 
-def fetch(place, arrays, shapes, name):
-    moved = sum(2 * 2 * shape[0] * shape[1] for shape in shapes)
+def fetch(arrays):
     return pl.pallas_call(
         fetch_kernel,
-        out_shape=[pltpu.VMEM(shape, bf16) for shape in shapes],
-        in_specs=[smem_spec()] + [pl.BlockSpec(memory_space=pltpu.MemorySpace.HBM)] * len(arrays),
+        out_shape=[pltpu.VMEM(x.shape, x.dtype) for x in arrays],
+        in_specs=[pl.BlockSpec(memory_space=pl.ANY)] * len(arrays),
         out_specs=[vmem_spec()] * len(arrays),
         scratch_shapes=[pltpu.SemaphoreType.DMA((len(arrays),))],
         compiler_params=pltpu.CompilerParams(vmem_limit_bytes=1024 * 1024),
-        cost_estimate=pl.CostEstimate(flops=0, bytes_accessed=moved, transcendentals=0),
-        name=name,
-    )(place, *arrays)
+        cost_estimate=pl.CostEstimate(
+            flops=0, bytes_accessed=sum(4 * x.size for x in arrays), transcendentals=0
+        ),
+    )(*arrays)
 
 
 def query_kernel(reqs, drafts, heads, place_ref, *refs):
@@ -73,7 +76,7 @@
     owners = out_ref.shape[0]
     rows_dev = reqs * drafts
     hd = heads * drafts
-    x = jnp.concatenate([x_ref[...].astype(f32) for x_ref in x_refs], axis=0)
+    x = jnp.concatenate([x_ref[...] for x_ref in x_refs], axis=0).astype(f32)
     scaled = x * lax.rsqrt(jnp.mean(x * x, axis=-1, keepdims=True) + rms_eps)
     normed = (scaled * gain_ref[...][None, :]).astype(bf16)
     full = mm(normed, up_ref[...]).astype(bf16)
@@ -81,18 +84,18 @@
     shape = (count, owners * rows_dev)
     n = lax.broadcasted_iota(jnp.int32, shape, 0)
     m = lax.broadcasted_iota(jnp.int32, shape, 1)
-    target = n // (reqs * hd)
-    local = (n // hd) % reqs * drafts + n % drafts
-    block = m // rows_dev
+    target = over(n, reqs * hd)
+    local = rest(over(n, hd), reqs) * drafts + rest(n, drafts)
+    block = over(m, rows_dev)
     distance = jnp.zeros_like(block)
     bit = owners // 2
     while bit:
-        distance = distance + block % 2 * bit
-        block = block // 2
+        distance = distance + (block & 1) * bit
+        block = block >> 1
         bit //= 2
-    spread = jnp.where((target == (distance ^ place_ref[2])) & (local == m % rows_dev), 1.0, 0.0)
+    spread = jnp.where((target == (distance ^ place_ref[2])) & (local == rest(m, rows_dev)), 1.0, 0.0)
     wide = mm(spread.astype(bf16), full)
-    row_head = (lax.broadcasted_iota(jnp.int32, (count, 1), 0) // drafts) % heads
+    row_head = rest(over(lax.broadcasted_iota(jnp.int32, (count, 1), 0), drafts), heads)
     absorbed = None
     rope = None
     for h in range(heads):
@@ -128,13 +131,13 @@
     for b in range(reqs // per):
         at = (reqs * chunks + b) * hd
         x = q_ref[:, at : at + hd, :].astype(f32).reshape(count, LANES)
-        lane = lax.broadcasted_iota(jnp.int32, x.shape, 1) % ROPE
+        lane = rest(lax.broadcasted_iota(jnp.int32, x.shape, 1), ROPE)
         half = ROPE // 2
         other = jnp.where(lane < half, pltpu.roll(x, LANES - half, 1), pltpu.roll(x, half, 1))
         x = x.reshape(owners, hd, LANES) * cos_ref[b] + other.reshape(owners, hd, LANES) * sin_ref[b]
         x = x.astype(bf16).reshape(count, LANES)
         rotated += [x[:, i * ROPE : (i + 1) * ROPE] for i in range(per)]
-    draft = lax.broadcasted_iota(jnp.int32, (count, 1), 0) % drafts
+    draft = rest(lax.broadcasted_iota(jnp.int32, (count, 1), 0), drafts)
     new_at = lax.broadcasted_iota(jnp.int32, (count, new_ref.shape[0]), 1)
     slot = lax.broadcasted_iota(jnp.int32, (1, slots), 1)
     for q in range(reqs):
@@ -173,7 +176,7 @@
     shape = (rows, owners * reqs * hd)
     m = lax.broadcasted_iota(jnp.int32, shape, 0)
     n = lax.broadcasted_iota(jnp.int32, shape, 1)
-    wanted = (m // drafts) * hd + m % drafts
+    wanted = over(m, drafts) * hd + rest(m, drafts)
     for h in range(heads):
         pick = jnp.where(n == wanted + h * drafts, 1.0, 0.0).astype(bf16)
         mine = mm(pick, latent).astype(bf16)
@@ -186,8 +189,9 @@
     own = jnp.concatenate([ref[...] for ref in value_refs[:replicas]], axis=0)
     other = jnp.concatenate([ref[...] for ref in value_refs[replicas:]], axis=0)
     tile = 256 if half % 256 == 0 else half
+    start = pl.multiple_of(place_ref[0] * half, LANES) if half % LANES == 0 else 0
     for at in range(0, half, tile):
-        part = mm(own, w_own_ref[:, at : at + tile]) + mm(other, w_other_ref[:, at : at + tile])
+        part = mm(own, w_own_ref[:, pl.ds(start + at, tile)]) + mm(other, w_other_ref[:, at : at + tile])
         part = part.astype(bf16)
         for k in range(replicas):
             out_ref[place_ref[1] ^ k, :, at : at + tile] = part[k * rows : (k + 1) * rows]
@@ -209,8 +213,8 @@
     return lax.ppermute(x, axis, [(i, i ^ k) for i in range(size)])
 
 
-def shards(q_latent, q_gain, q_up, w_uk, w_uv, w_o, new_kv, latent_cache, cache_len, draft_count):
-    rows_dev, qlat = q_latent.shape
+def local_step(q_latent, q_gain, q_up, w_uk, w_uv, w_o, new_kv, latent_cache, cache_len, draft_count):
+    rows_dev, _ = q_latent.shape
     owners = lax.axis_size("tensor")
     replicas = lax.axis_size("replica")
     heads = w_uk.shape[0]
@@ -220,16 +224,14 @@
     me = lax.axis_index("tensor")
     core = me % 2
 
-    half = w_o.shape[1] // 2
-    away = lax.dynamic_slice_in_dim(w_o, (1 - core) * half, half, axis=1)
-    w_other = step(away, "tensor", owners, 1)
-
     place = jnp.stack([core, lax.axis_index("replica"), me]).astype(jnp.int32)
     w_uk = w_uk.reshape(heads * NOPE, LATENT)
-    up_near, uk_near = fetch(place, (q_up, w_uk), (q_up.shape, w_uk.shape), "near_query")
-
-    rows = q_latent
-    bit = owners // 2
+    near = fetch((q_up, w_uk, q_latent))
+
+    first = step(q_latent, "tensor", owners, owners // 2)
+    first, up_near, uk_near, rows = lax.optimization_barrier((first, *near))
+    rows = jnp.concatenate([rows, first], axis=0)
+    bit = owners // 4
     while bit > 2:
         rows = jnp.concatenate([rows, step(rows, "tensor", owners, bit)], axis=0)
         bit //= 2
@@ -240,7 +242,7 @@
 
     chunks = LATENT // LANES
     packed = (reqs * chunks + reqs * ROPE // LANES) * hd
-    params = pltpu.CompilerParams(vmem_limit_bytes=32 * 1024 * 1024)
+    params = pltpu.CompilerParams(vmem_limit_bytes=24 * 1024 * 1024)
     queries = pl.pallas_call(
         functools.partial(query_kernel, reqs, drafts, heads),
         out_shape=jax.ShapeDtypeStruct((owners, packed, LANES), bf16),
@@ -250,6 +252,12 @@
         name="query",
     )(place, *parts, q_gain, up_near, uk_near)
     arrived = lax.all_to_all(queries, "tensor", split_axis=0, concat_axis=0, tiled=True)
+
+    half = w_o.shape[1] // 2
+    w_away = lax.dynamic_slice_in_dim(w_o, (1 - core) * half, half, axis=1)
+    w_other = step(w_away, "tensor", owners, 1)
+    arrived, w_other = lax.optimization_barrier((arrived, w_other))
+    w_own = w_o if half % LANES == 0 else lax.dynamic_slice_in_dim(w_o, core * half, half, axis=1)
 
     frequency = rope_base ** (-(jnp.arange(ROPE // 2).astype(f32) * 2.0 / ROPE))
     positions = (cache_len[:, None] + jnp.arange(drafts)[None, :]).astype(f32)
@@ -282,13 +290,11 @@
         compiler_params=params,
         name="values",
     )(returned, w_uv)
-    own = [values] + [step(values, "replica", replicas, k) for k in range(1, replicas)]
+    nearest = step(values, "replica", replicas, 1)
+    own = [values, nearest] + [step(values, "replica", replicas, k) for k in range(2, replicas)]
+    (w_other,) = fetch((w_other,))
     other = [step(piece, "tensor", owners, 1) for piece in own]
 
-    w_own = w_o
-    if half % LANES:
-        w_own = lax.dynamic_slice_in_dim(w_o, core * half, half, axis=1)
-    w_own, w_other = fetch(place, (w_own, w_other), (w_other.shape,) * 2, "near_output")
     product = pl.pallas_call(
         output_kernel,
         out_shape=jax.ShapeDtypeStruct((replicas, owners * rows_dev, half), bf16),
@@ -312,7 +318,7 @@
 def solution(mesh):
     rows = ("groups", "tensor", "replica")
     return jax.shard_map(
-        shards,
+        local_step,
         mesh=mesh,
         in_specs=(
             P(rows, None),

time: 106 us -> 104 us (0.981)
  waiting for transfers between devices: 21.8 us -> 25.9 us
  starting transfers between devices: 16.5 us -> 12.8 us
  Pallas kernels: 12.4 us -> 11.2 us
    all_to_all x1, waiting for transfers between devices: 11.7 us -> 14.9 us  [local_step(): lax.all_to_all(queries, 'tensor', split_axis=0, concat_axis=0, tiled=True)]
    all_to_all x1, starting transfers between devices: 6.66 us -> 3.91 us  [local_step(): lax.all_to_all(queries, 'tensor', split_axis=0, concat_axis=0, tiled=True)]
    pallas_call x7, Pallas kernels: 12.4 us -> 11.2 us  [the longest x1 3.19 us: local_step(): pl.pallas_call(functools.partial(attend_kernel, reqs, drafts, heads), out...]
    unnamed x20 -> x26, local copies, waits for them, and re-layouts: 3.51 us -> 3.13 us
  transfers between devices with their start and end apart: 10 -> 10, of which waited for: 5 -> 5; matrix products, arithmetic and copies ran while one was open for 4% -> 3% of each run, Pallas kernels for 7% -> 4%
where the time goes in v3:
time: 104 us
  blocking collectives  47.1 us (45%)
  waiting for transfers between devices  25.9 us (25%)
  starting transfers between devices  12.8 us (12%)
  Pallas kernels  11.2 us (11%)
  local copies, waits for them, and re-layouts  6.15 us (6%)
    all_to_all x1, blocking collectives, local_step(): lax.all_to_all(product, ('replica', 'tensor'), split_axis=0, concat_axis=...  28.6 us
    all_to_all x1, blocking collectives, local_step(): lax.all_to_all(latent, 'tensor', split_axis=0, concat_axis=0, tiled=True)  18.5 us
    all_to_all x1, waiting for transfers between devices, local_step(): lax.all_to_all(queries, 'tensor', split_axis=0, concat_axis=0, tiled=True)  14.9 us
    ppermute x9, waiting for transfers between devices, step(): return lax.ppermute(x, axis, [(i, i ^ k) for i in range(size)])  10.9 us
    ppermute x9, starting transfers between devices, step(): return lax.ppermute(x, axis, [(i, i ^ k) for i in range(size)])  8.86 us
    all_to_all x1, starting transfers between devices, local_step(): lax.all_to_all(queries, 'tensor', split_axis=0, concat_axis=0, tiled=True)  3.91 us
    pallas_call x1, Pallas kernels, local_step(): pl.pallas_call(functools.partial(attend_kernel, reqs, drafts, heads), out...  3.19 us
    unnamed x26, local copies, waits for them, and re-layouts  3.13 us
  transfers between devices with their start and end apart: 10, of which 5 were waited for; matrix products, arithmetic and copies ran while one was open for 3% of the time, Pallas kernels for 4%

profile of v3, /device:TPU:0, one launch (start us, length us, event | category | flops | bytes accessed | tf_op | source)
XLA Modules:
  0.0 103.5 jit_solution(15348766639719118304)
XLA Ops:
  0.0 4.1 %collective-permute-start = (bf16[8,1536]{1,0:T(8,128)(2,1)}, bf16[8,1536]{1,0:T(8,128)(2,1)S(1)}, u32[]{:S(2)}, u32[]{:S(2)}) collective-permute-start(bf16[8,1536]{1,0:T(8,128)(2,1)} %refs_2_.1), channel_id=1, source_target_pairs={{0,16},{2,18},{4,20},{6,22},{8,24},{10,26},{12,28},{14,30},{16,0},... | collective-permute-start | bytes 73736 | tf_op jit(solution)/shard_map/ppermute | solution.py:213
  4.1 2.8 %constant_dynamic-slice_fusion = bf16[512,1792]{1,0:T(8,128)(2,1)} fusion(bf16[512,3584]{1,0:T(8,128)(2,1)} %refs_4_.3, s32[]{:T(128)S(6)} %select_n.11), kind=kLoop, calls=%fused_computation.11 | loop fusion | bytes 3670020 | tf_op jit(solution)/shard_map/dynamic_slice | solution.py:257
  7.0 0.0 collective-permute-start.5
  7.0 0.3 shard_map.100
  7.3 1.4 %copy-done.3 = bf16[1536,768]{1,0:T(8,128)(2,1)} copy-done((bf16[1536,768]{1,0:T(8,128)(2,1)}, bf16[1536,768]{1,0:T(8,128)(2,1)S(1)}, u32[]{:S(2)}) %copy-start.3) | copy-done | bytes 2359320
  8.7 0.0 collective-permute-done
  8.7 1.6 %collective-permute-start.1 = (bf16[16,1536]{1,0:T(8,128)(2,1)S(1)}, bf16[16,1536]{1,0:T(8,128)(2,1)S(1)}, u32[]{:S(2)}, u32[]{:S(2)}) collective-permute-start(bf16[16,1536]{1,0:T(8,128)(2,1)S(1)} %pad_maximum_fusion), channel_id=1, source_target_pairs={{0,8},{2,10},{4,12},{6,14},{8,0},{10,2},{12,4},{14,6},{16,24},{18,... | collective-permute-start | bytes 147464 | tf_op jit(solution)/shard_map/ppermute | solution.py:213
  10.4 2.6 %collective-permute-done.1 = bf16[16,1536]{1,0:T(8,128)(2,1)S(1)} collective-permute-done((bf16[16,1536]{1,0:T(8,128)(2,1)S(1)}, bf16[16,1536]{1,0:T(8,128)(2,1)S(1)}, u32[]{:S(2)}, u32[]{:S(2)}) %collective-permute-start.1) | collective-permute-done | bytes 49184 | tf_op jit(solution)/shard_map/ppermute | solution.py:213
  12.9 1.5 %collective-permute-start.2 = (bf16[32,1536]{1,0:T(8,128)(2,1)S(1)}, bf16[32,1536]{1,0:T(8,128)(2,1)S(1)}, u32[]{:S(2)}, u32[]{:S(2)}) collective-permute-start(bf16[32,1536]{1,0:T(8,128)(2,1)S(1)} %constant_dynamic-update-slice_fusion.refs_0_), channel_id=1, source_target_pairs={{0,4},{2,6},{4,0},{6,2},{8,12},{10,14},{12,8},{14,10},{16,20},{18,... | collective-permute-start | bytes 294920 | tf_op jit(solution)/shard_map/ppermute | solution.py:213
  14.5 3.1 %collective-permute-done.2.refs_1_ = bf16[32,1536]{1,0:T(8,128)(2,1)S(1)} collective-permute-done((bf16[32,1536]{1,0:T(8,128)(2,1)S(1)}, bf16[32,1536]{1,0:T(8,128)(2,1)S(1)}, u32[]{:S(2)}, u32[]{:S(2)}) %collective-permute-start.2) | collective-permute-done | bytes 98336 | tf_op jit(solution)/shard_map/ppermute | solution.py:213
  17.5 0.0 collective-permute-start.4
  17.6 0.1 pad_add_fusion.place_ref
  17.6 0.0 collective-permute-done.3.refs_2_
  17.6 1.2 %collective-permute-done.4.refs_3_ = bf16[32,1536]{1,0:T(8,128)(2,1)S(1)} collective-permute-done((bf16[32,1536]{1,0:T(8,128)(2,1)S(1)}, bf16[32,1536]{1,0:T(8,128)(2,1)S(1)}, u32[]{:S(2)}, u32[]{:S(2)}) %collective-permute-start.4) | collective-permute-done | bytes 98336 | tf_op jit(solution)/shard_map/ppermute | solution.py:213
  18.9 1.7 %copy-done.4 = bf16[1536,768]{1,0:T(8,128)(2,1)S(1)} copy-done((bf16[1536,768]{1,0:T(8,128)(2,1)S(1)}, bf16[1536,768]{1,0:T(8,128)(2,1)}, u32[]{:S(2)}) %copy-start.4) | copy-done | bytes 2359320
  20.5 2.8 %query.1 = bf16[16,144,128]{2,1,0:T(8,128)(2,1)} custom-call(s32[3]{0:T(128)S(1)} %pad_add_fusion.place_ref, bf16[32,1536]{1,0:T(8,128)(2,1)S(1)} %constant_dynamic-update-slice_fusion.refs_0_, bf16[32,1536]{1,0:T(8,128)(2,1)S(1)} %collective-permute-done.2.refs_1_, bf16[32,1536]{1,0:T(8,128)(2,1)S(1)} %collective-permute-done.3.refs_2_, ...), custom_call_target="tpu_custom_call" | custom-call | tf_op jit(solution)/shard_map/query/pallas_call | solution.py:246
  23.3 3.9 %all-to-all-start = ((bf16[16,144,128]{2,1,0:T(8,128)(2,1)}), bf16[16,144,128]{2,1,0:T(8,128)(2,1)S(1)}, u32[]{:S(2)}, u32[]{:S(2)}) async-start(bf16[16,144,128]{2,1,0:T(8,128)(2,1)} %query.1), calls=%async_computation | async-start | bytes 1179648 | tf_op jit(solution)/shard_map/all_to_all | solution.py:254
  27.3 0.0 copy-start.5
  27.3 0.1 fusion
  27.4 0.1 maximum_bitcast_fusion
  27.5 0.1 broadcast_in_dim.22
  27.6 0.1 broadcast_in_dim.25
  27.7 14.9 %all-to-all-done.q_ref = bf16[16,144,128]{2,1,0:T(8,128)(2,1)S(1)} async-done(((bf16[16,144,128]{2,1,0:T(8,128)(2,1)}), bf16[16,144,128]{2,1,0:T(8,128)(2,1)S(1)}, u32[]{:S(2)}, u32[]{:S(2)}) %all-to-all-start) | async-done | bytes 589856 | tf_op jit(solution)/shard_map/all_to_all | solution.py:254
  42.7 3.2 %attend.1 = bf16[16,32,512]{2,1,0:T(8,128)(2,1)S(1)} custom-call(s32[2]{0:T(128)S(1)} %copy-done.10, s32[2]{0:T(128)S(1)} %copy-done.11, bf16[16,144,128]{2,1,0:T(8,128)(2,1)S(1)} %all-to-all-done.q_ref, f32[1,16,128]{2,1,0:T(8,128)S(1)} %bitcast.19, f32[1,16,128]{2,1,0:T(8,128)S(1)} %bitcast.20, bf16[8,576]{1,0:T(8,128)(2,1)S(1)} %copy-done.8, ...), custom_call_target="tpu_custom_call" | custom-call | tf_op jit(solution)/shard_map/attend/pallas_call | solution.py:275
  45.9 18.5 %all_to_all.15.latent_ref = bf16[16,32,512]{2,1,0:T(8,128)(2,1)S(1)} all-to-all(bf16[16,32,512]{2,1,0:T(8,128)(2,1)S(1)} %attend.1), channel_id=1, replica_groups=mesh['groups'=1,'tensor'=16,'replica'=2] {'tensor'}, dimensions={0} | all-to-all | bytes 1048576 | tf_op jit(solution)/shard_map/all_to_all | solution.py:283
  64.4 1.0 values.1.refs_0_
  65.4 1.6 %collective-permute-start.6 = (bf16[128,512]{1,0:T(8,128)(2,1)S(1)}, bf16[128,512]{1,0:T(8,128)(2,1)S(1)}, u32[]{:S(2)}, u32[]{:S(2)}) collective-permute-start(bf16[128,512]{1,0:T(8,128)(2,1)S(1)} %values.1.refs_0_), channel_id=1, source_target_pairs={{0,1},{1,0},{2,3},{3,2},{4,5},{5,4},{6,7},{7,6},{8,9},{9,8},{10,11... | collective-permute-start | bytes 393224 | tf_op jit(solution)/shard_map/ppermute | solution.py:213
  67.0 4.1 %collective-permute-done.6.refs_1_ = bf16[128,512]{1,0:T(8,128)(2,1)S(1)} collective-permute-done((bf16[128,512]{1,0:T(8,128)(2,1)S(1)}, bf16[128,512]{1,0:T(8,128)(2,1)S(1)}, u32[]{:S(2)}, u32[]{:S(2)}) %collective-permute-start.6) | collective-permute-done | bytes 131104 | tf_op jit(solution)/shard_map/ppermute | solution.py:213
  71.0 1.5 %shard_map.101.refs_5_ = bf16[512,1792]{1,0:T(8,128)(2,1)S(1)} custom-call(bf16[512,1792]{1,0:T(8,128)(2,1)} %collective-permute-done.5.refs_0_), custom_call_target="tpu_custom_call" | custom-call | bytes 3670016 | tf_op jit(solution)/shard_map/pallas_call | solution.py:61
  72.6 1.7 %output.1 = bf16[2,128,1792]{2,1,0:T(8,128)(2,1)S(1)} custom-call(s32[3]{0:T(128)S(1)} %pad_add_fusion.place_ref, bf16[128,512]{1,0:T(8,128)(2,1)S(1)} %values.1.refs_0_, bf16[128,512]{1,0:T(8,128)(2,1)S(1)} %collective-permute-done.6.refs_1_, bf16[128,512]{1,0:T(8,128)(2,1)S(1)} %collective-permute-done.7.refs_2_, ...), custom_call_target="tpu_custom_call" | custom-call | tf_op jit(solution)/shard_map/output/pallas_call | solution.py:298
  74.2 28.6 %all_to_all.16.x_ref = bf16[32,8,1792]{2,1,0:T(8,128)(2,1)S(1)} all-to-all(bf16[32,8,1792]{2,1,0:T(8,128)(2,1)S(1)} %bitcast.16), channel_id=1, replica_groups=mesh['groups'=1,'tensor'=16,'replica'=2] {'replica','tensor'}, dimensions={0} | all-to-all | bytes 1835008 | tf_op jit(solution)/shard_map/all_to_all | solution.py:307
  102.8 0.8 combine.1
  (35 shorter events, 0.1 us)
Async XLA Ops:
  0.0 7.0 %copy-start.7 = (bf16[8,1536]{1,0:T(8,128)(2,1)S(1)}, bf16[8,1536]{1,0:T(8,128)(2,1)}, u32[]{:S(2)}) copy-start(bf16[8,1536]{1,0:T(8,128)(2,1)} %refs_2_.1) | copy-start | bytes 73732
  0.0 7.0 %copy-start.6 = (bf16[4,128,512]{2,1,0:T(8,128)(2,1)S(1)}, bf16[4,128,512]{2,1,0:T(8,128)(2,1)}, u32[]{:S(2)}) copy-start(bf16[4,128,512]{2,1,0:T(8,128)(2,1)} %param.13) | copy-start | bytes 1572868
  0.0 7.0 %copy-start.1 = (bf16[1536,768]{1,0:T(8,128)(2,1)S(1)}, bf16[1536,768]{1,0:T(8,128)(2,1)}, u32[]{:S(2)}) copy-start(bf16[1536,768]{1,0:T(8,128)(2,1)} %refs_0_.1) | copy-start | bytes 7077892
  0.0 8.7 %collective-permute-start = (bf16[8,1536]{1,0:T(8,128)(2,1)}, bf16[8,1536]{1,0:T(8,128)(2,1)S(1)}, u32[]{:S(2)}, u32[]{:S(2)}) collective-permute-start(bf16[8,1536]{1,0:T(8,128)(2,1)} %refs_2_.1), channel_id=1, source_target_pairs={{0,16},{2,18},{4,20},{6,22},{8,24},{10,26},{12,28},{14,30},{16,0},... | collective-permute-start | bytes 73736 | tf_op jit(solution)/shard_map/ppermute | solution.py:213
  7.0 11.9 %copy-start.9 = (f32[1536]{0:T(1024)S(1)}, f32[1536]{0:T(1024)}, u32[]{:S(2)}) copy-start(f32[1536]{0:T(1024)} %refs_4_.2) | copy-start | bytes 18436
  7.0 35.6 %collective-permute-start.5 = (bf16[512,1792]{1,0:T(8,128)(2,1)}, bf16[512,1792]{1,0:T(8,128)(2,1)}, u32[]{:S(2)}, u32[]{:S(2)}) collective-permute-start(bf16[512,1792]{1,0:T(8,128)(2,1)} %constant_dynamic-slice_fusion), channel_id=1, source_target_pairs={{0,2},{2,0},{4,6},{6,4},{8,10},{10,8},{12,14},{14,12},{16,18},{18,... | collective-permute-start | bytes 5505032 | tf_op jit(solution)/shard_map/ppermute | solution.py:213
  7.3 1.4 %copy-start.3 = (bf16[1536,768]{1,0:T(8,128)(2,1)}, bf16[1536,768]{1,0:T(8,128)(2,1)S(1)}, u32[]{:S(2)}) copy-start(bf16[1536,768]{1,0:T(8,128)(2,1)S(1)} %get-tuple-element.19.refs_5_) | copy-start | bytes 7077892
  8.7 4.2 %collective-permute-start.1 = (bf16[16,1536]{1,0:T(8,128)(2,1)S(1)}, bf16[16,1536]{1,0:T(8,128)(2,1)S(1)}, u32[]{:S(2)}, u32[]{:S(2)}) collective-permute-start(bf16[16,1536]{1,0:T(8,128)(2,1)S(1)} %pad_maximum_fusion), channel_id=1, source_target_pairs={{0,8},{2,10},{4,12},{6,14},{8,0},{10,2},{12,4},{14,6},{16,24},{18,... | collective-permute-start | bytes 147464 | tf_op jit(solution)/shard_map/ppermute | solution.py:213
  12.9 4.6 %collective-permute-start.2 = (bf16[32,1536]{1,0:T(8,128)(2,1)S(1)}, bf16[32,1536]{1,0:T(8,128)(2,1)S(1)}, u32[]{:S(2)}, u32[]{:S(2)}) collective-permute-start(bf16[32,1536]{1,0:T(8,128)(2,1)S(1)} %constant_dynamic-update-slice_fusion.refs_0_), channel_id=1, source_target_pairs={{0,4},{2,6},{4,0},{6,2},{8,12},{10,14},{12,8},{14,10},{16,20},{18,... | collective-permute-start | bytes 294920 | tf_op jit(solution)/shard_map/ppermute | solution.py:213
  14.4 3.2 %collective-permute-start.3 = (bf16[32,1536]{1,0:T(8,128)(2,1)S(1)}, bf16[32,1536]{1,0:T(8,128)(2,1)S(1)}, u32[]{:S(2)}, u32[]{:S(2)}) collective-permute-start(bf16[32,1536]{1,0:T(8,128)(2,1)S(1)} %constant_dynamic-update-slice_fusion.refs_0_), channel_id=1, source_target_pairs={{0,2},{2,0},{4,6},{6,4},{8,10},{10,8},{12,14},{14,12},{16,18},{18,... | collective-permute-start | bytes 294920 | tf_op jit(solution)/shard_map/ppermute | solution.py:213
  17.5 1.3 %collective-permute-start.4 = (bf16[32,1536]{1,0:T(8,128)(2,1)S(1)}, bf16[32,1536]{1,0:T(8,128)(2,1)S(1)}, u32[]{:S(2)}, u32[]{:S(2)}) collective-permute-start(bf16[32,1536]{1,0:T(8,128)(2,1)S(1)} %collective-permute-done.2.refs_1_), channel_id=1, source_target_pairs={{0,2},{2,0},{4,6},{6,4},{8,10},{10,8},{12,14},{14,12},{16,18},{18,... | collective-permute-start | bytes 294920 | tf_op jit(solution)/shard_map/ppermute | solution.py:213
  17.6 9.7 %copy-start.10 = (s32[2]{0:T(128)S(1)}, s32[2]{0:T(128)}, u32[]{:S(2)}) copy-start(s32[2]{0:T(128)} %len_ref.1) | copy-start | bytes 28
  17.6 25.1 %copy-start.11 = (s32[2]{0:T(128)S(1)}, s32[2]{0:T(128)}, u32[]{:S(2)}) copy-start(s32[2]{0:T(128)} %count_ref.1) | copy-start | bytes 28
  17.6 25.0 %copy-start.2 = (bf16[2,1024,576]{1,2,0:T(8,128)(2,1)S(1)}, bf16[2,1024,576]{1,2,0:T(8,128)(2,1)}, u32[]{:S(2)}) copy-start(bf16[2,1024,576]{1,2,0:T(8,128)(2,1)} %param.17) | copy-start | bytes 7077892
  18.9 1.7 %copy-start.4 = (bf16[1536,768]{1,0:T(8,128)(2,1)S(1)}, bf16[1536,768]{1,0:T(8,128)(2,1)}, u32[]{:S(2)}) copy-start(bf16[1536,768]{1,0:T(8,128)(2,1)} %copy-done.3) | copy-start | bytes 7077892
  20.5 22.1 %copy-start.8 = (bf16[8,576]{1,0:T(8,128)(2,1)S(1)}, bf16[8,576]{1,0:T(8,128)(2,1)}, u32[]{:S(2)}) copy-start(bf16[8,576]{1,0:T(8,128)(2,1)} %new_ref.1) | copy-start | bytes 27652
  23.3 19.3 %all-to-all-start = ((bf16[16,144,128]{2,1,0:T(8,128)(2,1)}), bf16[16,144,128]{2,1,0:T(8,128)(2,1)S(1)}, u32[]{:S(2)}, u32[]{:S(2)}) async-start(bf16[16,144,128]{2,1,0:T(8,128)(2,1)} %query.1), calls=%async_computation | async-start | bytes 1179648 | tf_op jit(solution)/shard_map/all_to_all | solution.py:254
  27.3 37.1 %copy-start.5 = (bf16[4,512,128]{2,1,0:T(8,128)(2,1)S(1)}, bf16[4,512,128]{2,1,0:T(8,128)(2,1)}, u32[]{:S(2)}) copy-start(bf16[4,512,128]{2,1,0:T(8,128)(2,1)} %uv_ref.1) | copy-start | bytes 1572868
  64.4 8.2 %copy-start = (bf16[512,3584]{1,0:T(8,128)(2,1)S(1)}, bf16[512,3584]{1,0:T(8,128)(2,1)}, u32[]{:S(2)}) copy-start(bf16[512,3584]{1,0:T(8,128)(2,1)} %refs_4_.3) | copy-start | bytes 11010052
  65.4 5.6 %collective-permute-start.6 = (bf16[128,512]{1,0:T(8,128)(2,1)S(1)}, bf16[128,512]{1,0:T(8,128)(2,1)S(1)}, u32[]{:S(2)}, u32[]{:S(2)}) collective-permute-start(bf16[128,512]{1,0:T(8,128)(2,1)S(1)} %values.1.refs_0_), channel_id=1, source_target_pairs={{0,1},{1,0},{2,3},{3,2},{4,5},{5,4},{6,7},{7,6},{8,9},{9,8},{10,11... | collective-permute-start | bytes 393224 | tf_op jit(solution)/shard_map/ppermute | solution.py:213
  67.0 5.6 %collective-permute-start.7 = (bf16[128,512]{1,0:T(8,128)(2,1)S(1)}, bf16[128,512]{1,0:T(8,128)(2,1)S(1)}, u32[]{:S(2)}, u32[]{:S(2)}) collective-permute-start(bf16[128,512]{1,0:T(8,128)(2,1)S(1)} %values.1.refs_0_), channel_id=1, source_target_pairs={{0,2},{2,0},{4,6},{6,4},{8,10},{10,8},{12,14},{14,12},{16,18},{18,... | collective-permute-start | bytes 393224 | tf_op jit(solution)/shard_map/ppermute | solution.py:213
  71.0 1.5 %collective-permute-start.8 = (bf16[128,512]{1,0:T(8,128)(2,1)S(1)}, bf16[128,512]{1,0:T(8,128)(2,1)S(1)}, u32[]{:S(2)}, u32[]{:S(2)}) collective-permute-start(bf16[128,512]{1,0:T(8,128)(2,1)S(1)} %collective-permute-done.6.refs_1_), channel_id=1, source_target_pairs={{0,2},{2,0},{4,6},{6,4},{8,10},{10,8},{12,14},{14,12},{16,18},{18,... | collective-permute-start | bytes 393224 | tf_op jit(solution)/shard_map/ppermute | solution.py:213

commit v4 on v3

--- a/solution.py
+++ b/solution.py
@@ -14,6 +14,9 @@
 VDIM = 128
 QKD = NOPE + ROPE
 LANES = 128
+UP_PARTS = 4
+QUERY_VMEM = 56_000_000
+OUTPUT_VMEM = 54_000_000
 
 rms_eps = 1e-06
 rope_base = 50000.0
@@ -48,38 +51,28 @@
     return lax.dot_general(a, b, (((1,), (1,)), ((), ())), preferred_element_type=f32)
 
 
-def fetch_kernel(*refs):
-    count = len(refs) // 2
-    copies = [pltpu.make_async_copy(refs[i], refs[count + i], refs[-1].at[i]) for i in range(count)]
+def query_kernel(reqs, drafts, heads, place_ref, *refs):
+    *x_refs, gain_ref, up_hbm, uk_hbm, out_ref, up_ref, uk_ref, sems = refs
+    deep = up_ref.shape[0] // UP_PARTS
+    copies = [
+        pltpu.make_async_copy(up_hbm.at[pl.ds(i * deep, deep)], up_ref.at[pl.ds(i * deep, deep)], sems.at[i])
+        for i in range(UP_PARTS)
+    ]
+    copies.append(pltpu.make_async_copy(uk_hbm, uk_ref, sems.at[UP_PARTS]))
     for copy in copies:
         copy.start()
-    for copy in copies:
-        copy.wait()
-
-
-def fetch(arrays):
-    return pl.pallas_call(
-        fetch_kernel,
-        out_shape=[pltpu.VMEM(x.shape, x.dtype) for x in arrays],
-        in_specs=[pl.BlockSpec(memory_space=pl.ANY)] * len(arrays),
-        out_specs=[vmem_spec()] * len(arrays),
-        scratch_shapes=[pltpu.SemaphoreType.DMA((len(arrays),))],
-        compiler_params=pltpu.CompilerParams(vmem_limit_bytes=1024 * 1024),
-        cost_estimate=pl.CostEstimate(
-            flops=0, bytes_accessed=sum(4 * x.size for x in arrays), transcendentals=0
-        ),
-    )(*arrays)
-
-
-def query_kernel(reqs, drafts, heads, place_ref, *refs):
-    *x_refs, gain_ref, up_ref, uk_ref, out_ref = refs
     owners = out_ref.shape[0]
     rows_dev = reqs * drafts
     hd = heads * drafts
     x = jnp.concatenate([x_ref[...] for x_ref in x_refs], axis=0).astype(f32)
     scaled = x * lax.rsqrt(jnp.mean(x * x, axis=-1, keepdims=True) + rms_eps)
     normed = (scaled * gain_ref[...][None, :]).astype(bf16)
-    full = mm(normed, up_ref[...]).astype(bf16)
+    full = None
+    for i in range(UP_PARTS):
+        copies[i].wait()
+        part = mm(normed[:, i * deep : (i + 1) * deep], up_ref[i * deep : (i + 1) * deep])
+        full = part if full is None else full + part
+    full = full.astype(bf16)
     count = owners * reqs * hd
     shape = (count, owners * rows_dev)
     n = lax.broadcasted_iota(jnp.int32, shape, 0)
@@ -98,10 +91,11 @@
     row_head = rest(over(lax.broadcasted_iota(jnp.int32, (count, 1), 0), drafts), heads)
     absorbed = None
     rope = None
+    copies[UP_PARTS].wait()
     for h in range(heads):
         mine = row_head == h
         nope_h = jnp.where(mine, wide[:, h * QKD : h * QKD + NOPE], 0.0).astype(bf16)
-        part = mm(nope_h, uk_ref[h * NOPE : (h + 1) * NOPE])
+        part = mm(nope_h, uk_ref[h])
         absorbed = part if absorbed is None else absorbed + part
         rope_h = jnp.where(mine, wide[:, h * QKD + NOPE : (h + 1) * QKD], 0.0)
         rope = rope_h if rope is None else rope + rope_h
@@ -184,17 +178,33 @@
 
 
 def output_kernel(place_ref, *refs):
-    *value_refs, w_own_ref, w_other_ref, out_ref = refs
+    *value_refs, own_hbm, other_hbm, out_ref, own_ref, other_ref, sems = refs
     replicas, rows, half = out_ref.shape
+    tile = 256 if half % 256 == 0 else half
+    tiles = half // tile
+    start = 0
+    if own_hbm.shape[1] != half:
+        start = pl.multiple_of(place_ref[0] * half, LANES)
+    copies = []
+    for i in range(tiles):
+        to = pl.ds(i * tile, tile)
+        own_copy = pltpu.make_async_copy(
+            own_hbm.at[:, pl.ds(start + i * tile, tile)], own_ref.at[:, to], sems.at[0, i]
+        )
+        other_copy = pltpu.make_async_copy(other_hbm.at[:, to], other_ref.at[:, to], sems.at[1, i])
+        copies.append((own_copy, other_copy))
+        own_copy.start()
+        other_copy.start()
     own = jnp.concatenate([ref[...] for ref in value_refs[:replicas]], axis=0)
     other = jnp.concatenate([ref[...] for ref in value_refs[replicas:]], axis=0)
-    tile = 256 if half % 256 == 0 else half
-    start = pl.multiple_of(place_ref[0] * half, LANES) if half % LANES == 0 else 0
-    for at in range(0, half, tile):
-        part = mm(own, w_own_ref[:, pl.ds(start + at, tile)]) + mm(other, w_other_ref[:, at : at + tile])
-        part = part.astype(bf16)
+    for i in range(tiles):
+        at = slice(i * tile, (i + 1) * tile)
+        copies[i][0].wait()
+        part = mm(own, own_ref[:, at])
+        copies[i][1].wait()
+        part = (part + mm(other, other_ref[:, at])).astype(bf16)
         for k in range(replicas):
-            out_ref[place_ref[1] ^ k, :, at : at + tile] = part[k * rows : (k + 1) * rows]
+            out_ref[place_ref[1] ^ k, :, at] = part[k * rows : (k + 1) * rows]
 
 
 def sum_kernel(replicas, pairs, x_ref, out_ref):
@@ -225,13 +235,9 @@
     core = me % 2
 
     place = jnp.stack([core, lax.axis_index("replica"), me]).astype(jnp.int32)
-    w_uk = w_uk.reshape(heads * NOPE, LATENT)
-    near = fetch((q_up, w_uk, q_latent))
-
-    first = step(q_latent, "tensor", owners, owners // 2)
-    first, up_near, uk_near, rows = lax.optimization_barrier((first, *near))
-    rows = jnp.concatenate([rows, first], axis=0)
-    bit = owners // 4
+
+    rows = q_latent
+    bit = owners // 2
     while bit > 2:
         rows = jnp.concatenate([rows, step(rows, "tensor", owners, bit)], axis=0)
         bit //= 2
@@ -246,11 +252,16 @@
     queries = pl.pallas_call(
         functools.partial(query_kernel, reqs, drafts, heads),
         out_shape=jax.ShapeDtypeStruct((owners, packed, LANES), bf16),
-        in_specs=[smem_spec()] + [vmem_spec()] * (len(parts) + 3),
-        out_specs=vmem_spec(),
-        compiler_params=params,
+        in_specs=[smem_spec()] + [vmem_spec()] * (len(parts) + 1) + [pl.BlockSpec(memory_space=pl.ANY)] * 2,
+        out_specs=vmem_spec(),
+        scratch_shapes=[
+            pltpu.VMEM(q_up.shape, bf16),
+            pltpu.VMEM(w_uk.shape, bf16),
+            pltpu.SemaphoreType.DMA((UP_PARTS + 1,)),
+        ],
+        compiler_params=pltpu.CompilerParams(vmem_limit_bytes=QUERY_VMEM),
         name="query",
-    )(place, *parts, q_gain, up_near, uk_near)
+    )(place, *parts, q_gain, q_up, w_uk)
     arrived = lax.all_to_all(queries, "tensor", split_axis=0, concat_axis=0, tiled=True)
 
     half = w_o.shape[1] // 2
@@ -290,17 +301,20 @@
         compiler_params=params,
         name="values",
     )(returned, w_uv)
-    nearest = step(values, "replica", replicas, 1)
-    own = [values, nearest] + [step(values, "replica", replicas, k) for k in range(2, replicas)]
-    (w_other,) = fetch((w_other,))
+    own = [values] + [step(values, "replica", replicas, k) for k in range(1, replicas)]
     other = [step(piece, "tensor", owners, 1) for piece in own]
 
     product = pl.pallas_call(
         output_kernel,
         out_shape=jax.ShapeDtypeStruct((replicas, owners * rows_dev, half), bf16),
-        in_specs=[smem_spec()] + [vmem_spec()] * (2 * replicas + 2),
-        out_specs=vmem_spec(),
-        compiler_params=params,
+        in_specs=[smem_spec()] + [vmem_spec()] * (2 * replicas) + [pl.BlockSpec(memory_space=pl.ANY)] * 2,
+        out_specs=vmem_spec(),
+        scratch_shapes=[
+            pltpu.VMEM(w_other.shape, bf16),
+            pltpu.VMEM(w_other.shape, bf16),
+            pltpu.SemaphoreType.DMA((2, half // 256 if half % 256 == 0 else 1)),
+        ],
+        compiler_params=pltpu.CompilerParams(vmem_limit_bytes=OUTPUT_VMEM),
         name="output",
     )(place, *own, *other, w_own, w_other)
     product = product.reshape(replicas * owners, rows_dev, half)

time: 104 us -> 109 us (1.048)
  local copies, waits for them, and re-layouts: 6.15 us -> 3.09 us
  Pallas kernels: 11.2 us -> 14.2 us
  starting transfers between devices: 12.8 us -> 15.6 us
  waiting for transfers between devices: 25.9 us -> 28.5 us
    unnamed x26 -> x16, local copies, waits for them, and re-layouts: 3.13 us -> 0.03 us
    pallas_call x1, Pallas kernels: 1.66 us -> 4.63 us  [local_step(): pl.pallas_call(output_kernel, out_shape=jax.ShapeDtypeStruct((replicas, o...]
    ppermute x9, waiting for transfers between devices: 10.9 us -> 13.6 us  [step(): return lax.ppermute(x, axis, [(i, i ^ k) for i in range(size)])]
    all_to_all x1, starting transfers between devices: 3.91 us -> 6.42 us  [local_step(): lax.all_to_all(queries, 'tensor', split_axis=0, concat_axis=0, tiled=True)]
    pallas_call x1, Pallas kernels: 2.81 us -> 4.6 us  [local_step(): pl.pallas_call(functools.partial(query_kernel, reqs, drafts, heads), out_...]
    pallas_call x2 -> x0, Pallas kernels: 1.77 us -> none  [fetch(): pl.pallas_call(fetch_kernel, out_shape=[pltpu.VMEM(x.shape, x.dtype) for...]
  transfers between devices with their start and end apart: 10 -> 10, of which waited for: 5 -> 7; matrix products, arithmetic and copies ran while one was open for 3% -> 0% of each run, Pallas kernels for 4% -> 4%
where the time goes in v4:
time: 109 us
  blocking collectives  47 us (43%)
  waiting for transfers between devices  28.5 us (26%)
  starting transfers between devices  15.6 us (14%)
  Pallas kernels  14.2 us (13%)
  local copies, waits for them, and re-layouts  3.09 us (3%)
    all_to_all x1, blocking collectives, local_step(): lax.all_to_all(product, ('replica', 'tensor'), split_axis=0, concat_axis=...  28.4 us
    all_to_all x1, blocking collectives, local_step(): lax.all_to_all(latent, 'tensor', split_axis=0, concat_axis=0, tiled=True)  18.5 us
    all_to_all x1, waiting for transfers between devices, local_step(): lax.all_to_all(queries, 'tensor', split_axis=0, concat_axis=0, tiled=True)  14.9 us
    ppermute x9, waiting for transfers between devices, step(): return lax.ppermute(x, axis, [(i, i ^ k) for i in range(size)])  13.6 us
    ppermute x9, starting transfers between devices, step(): return lax.ppermute(x, axis, [(i, i ^ k) for i in range(size)])  9.23 us
    all_to_all x1, starting transfers between devices, local_step(): lax.all_to_all(queries, 'tensor', split_axis=0, concat_axis=0, tiled=True)  6.42 us
    pallas_call x1, Pallas kernels, local_step(): pl.pallas_call(output_kernel, out_shape=jax.ShapeDtypeStruct((replicas, o...  4.63 us
    pallas_call x1, Pallas kernels, local_step(): pl.pallas_call(functools.partial(query_kernel, reqs, drafts, heads), out_...  4.6 us
  transfers between devices with their start and end apart: 10, of which 7 were waited for; matrix products, arithmetic and copies ran while one was open for 0% of the time, Pallas kernels for 4%

profile of v4, /device:TPU:0, one launch (start us, length us, event | category | flops | bytes accessed | tf_op | source)
XLA Modules:
  0.0 108.9 jit_solution(5401471914426898086)
XLA Ops:
  0.0 2.9 %constant_dynamic-slice_fusion = bf16[512,1792]{1,0:T(8,128)(2,1)} fusion(bf16[512,3584]{1,0:T(8,128)(2,1)} %refs_4_.3, s32[]{:T(128)S(6)} %select_n.11), kind=kLoop, calls=%fused_computation.11 | loop fusion | bytes 3670020 | tf_op jit(solution)/shard_map/dynamic_slice | solution.py:268
  2.9 0.5 collective-permute-start.5
  3.4 3.6 %collective-permute-start = (bf16[8,1536]{1,0:T(8,128)(2,1)S(1)}, bf16[8,1536]{1,0:T(8,128)(2,1)S(1)}, u32[]{:S(2)}, u32[]{:S(2)}) collective-permute-start(bf16[8,1536]{1,0:T(8,128)(2,1)S(1)} %copy-done.6), channel_id=1, source_target_pairs={{0,16},{2,18},{4,20},{6,22},{8,24},{10,26},{12,28},{14,30},{16,0},... | collective-permute-start | bytes 73736 | tf_op jit(solution)/shard_map/ppermute | solution.py:223
  7.0 1.9 %collective-permute-done = bf16[8,1536]{1,0:T(8,128)(2,1)S(1)} collective-permute-done((bf16[8,1536]{1,0:T(8,128)(2,1)S(1)}, bf16[8,1536]{1,0:T(8,128)(2,1)S(1)}, u32[]{:S(2)}, u32[]{:S(2)}) %collective-permute-start) | collective-permute-done | bytes 24608 | tf_op jit(solution)/shard_map/ppermute | solution.py:223
  8.8 1.8 %collective-permute-start.1 = (bf16[16,1536]{1,0:T(8,128)(2,1)S(1)}, bf16[16,1536]{1,0:T(8,128)(2,1)S(1)}, u32[]{:S(2)}, u32[]{:S(2)}) collective-permute-start(bf16[16,1536]{1,0:T(8,128)(2,1)S(1)} %pad_maximum_fusion), channel_id=1, source_target_pairs={{0,8},{2,10},{4,12},{6,14},{8,0},{10,2},{12,4},{14,6},{16,24},{18,... | collective-permute-start | bytes 147464 | tf_op jit(solution)/shard_map/ppermute | solution.py:223
  10.7 2.3 %collective-permute-done.1 = bf16[16,1536]{1,0:T(8,128)(2,1)S(1)} collective-permute-done((bf16[16,1536]{1,0:T(8,128)(2,1)S(1)}, bf16[16,1536]{1,0:T(8,128)(2,1)S(1)}, u32[]{:S(2)}, u32[]{:S(2)}) %collective-permute-start.1) | collective-permute-done | bytes 49184 | tf_op jit(solution)/shard_map/ppermute | solution.py:223
  12.9 1.8 %collective-permute-start.2 = (bf16[32,1536]{1,0:T(8,128)(2,1)S(1)}, bf16[32,1536]{1,0:T(8,128)(2,1)S(1)}, u32[]{:S(2)}, u32[]{:S(2)}) collective-permute-start(bf16[32,1536]{1,0:T(8,128)(2,1)S(1)} %constant_dynamic-update-slice_fusion.refs_0_), channel_id=1, source_target_pairs={{0,4},{2,6},{4,0},{6,2},{8,12},{10,14},{12,8},{14,10},{16,20},{18,... | collective-permute-start | bytes 294920 | tf_op jit(solution)/shard_map/ppermute | solution.py:223
  14.7 0.0 collective-permute-start.3
  14.7 2.8 %collective-permute-done.2.refs_1_ = bf16[32,1536]{1,0:T(8,128)(2,1)S(1)} collective-permute-done((bf16[32,1536]{1,0:T(8,128)(2,1)S(1)}, bf16[32,1536]{1,0:T(8,128)(2,1)S(1)}, u32[]{:S(2)}, u32[]{:S(2)}) %collective-permute-start.2) | collective-permute-done | bytes 98336 | tf_op jit(solution)/shard_map/ppermute | solution.py:223
  17.6 0.0 collective-permute-start.4
  17.6 0.1 pad_add_fusion.place_ref
  17.7 0.0 collective-permute-done.3.refs_2_
  17.7 1.2 %collective-permute-done.4.refs_3_ = bf16[32,1536]{1,0:T(8,128)(2,1)S(1)} collective-permute-done((bf16[32,1536]{1,0:T(8,128)(2,1)S(1)}, bf16[32,1536]{1,0:T(8,128)(2,1)S(1)}, u32[]{:S(2)}, u32[]{:S(2)}) %collective-permute-start.4) | collective-permute-done | bytes 98336 | tf_op jit(solution)/shard_map/ppermute | solution.py:223
  18.9 4.6 %query.1 = bf16[16,144,128]{2,1,0:T(8,128)(2,1)} custom-call(s32[3]{0:T(128)S(1)} %pad_add_fusion.place_ref, bf16[32,1536]{1,0:T(8,128)(2,1)S(1)} %constant_dynamic-update-slice_fusion.refs_0_, bf16[32,1536]{1,0:T(8,128)(2,1)S(1)} %collective-permute-done.2.refs_1_, bf16[32,1536]{1,0:T(8,128)(2,1)S(1)} %collective-permute-done.3.refs_2_, ...), custom_call_target="tpu_custom_call" | custom-call | tf_op jit(solution)/shard_map/query/pallas_call | solution.py:252
  23.5 6.4 %all-to-all-start = ((bf16[16,144,128]{2,1,0:T(8,128)(2,1)}), bf16[16,144,128]{2,1,0:T(8,128)(2,1)S(1)}, u32[]{:S(2)}, u32[]{:S(2)}) async-start(bf16[16,144,128]{2,1,0:T(8,128)(2,1)} %query.1), calls=%async_computation | async-start | bytes 1179648 | tf_op jit(solution)/shard_map/all_to_all | solution.py:265
  29.9 0.0 copy-start.1
  29.9 0.1 fusion
  30.1 0.1 maximum_bitcast_fusion
  30.2 0.1 broadcast_in_dim.22
  30.3 0.1 broadcast_in_dim.25
  30.3 14.9 %all-to-all-done.q_ref = bf16[16,144,128]{2,1,0:T(8,128)(2,1)S(1)} async-done(((bf16[16,144,128]{2,1,0:T(8,128)(2,1)}), bf16[16,144,128]{2,1,0:T(8,128)(2,1)S(1)}, u32[]{:S(2)}, u32[]{:S(2)}) %all-to-all-start) | async-done | bytes 589856 | tf_op jit(solution)/shard_map/all_to_all | solution.py:265
  45.3 3.2 %attend.1 = bf16[16,32,512]{2,1,0:T(8,128)(2,1)S(1)} custom-call(s32[2]{0:T(128)S(1)} %copy-done.4, s32[2]{0:T(128)S(1)} %copy-done.5, bf16[16,144,128]{2,1,0:T(8,128)(2,1)S(1)} %all-to-all-done.q_ref, f32[1,16,128]{2,1,0:T(8,128)S(1)} %bitcast.17, f32[1,16,128]{2,1,0:T(8,128)S(1)} %bitcast.18, bf16[8,576]{1,0:T(8,128)(2,1)S(1)} %copy-done.2, ...), custom_call_target="tpu_custom_call" | custom-call | tf_op jit(solution)/shard_map/attend/pallas_call | solution.py:286
  48.5 18.5 %all_to_all.15.latent_ref = bf16[16,32,512]{2,1,0:T(8,128)(2,1)S(1)} all-to-all(bf16[16,32,512]{2,1,0:T(8,128)(2,1)S(1)} %attend.1), channel_id=1, replica_groups=mesh['groups'=1,'tensor'=16,'replica'=2] {'tensor'}, dimensions={0} | all-to-all | bytes 1048576 | tf_op jit(solution)/shard_map/all_to_all | solution.py:294
  67.0 1.0 values.1.refs_0_
  68.1 1.6 %collective-permute-start.6 = (bf16[128,512]{1,0:T(8,128)(2,1)S(1)}, bf16[128,512]{1,0:T(8,128)(2,1)S(1)}, u32[]{:S(2)}, u32[]{:S(2)}) collective-permute-start(bf16[128,512]{1,0:T(8,128)(2,1)S(1)} %values.1.refs_0_), channel_id=1, source_target_pairs={{0,1},{1,0},{2,3},{3,2},{4,5},{5,4},{6,7},{7,6},{8,9},{9,8},{10,11... | collective-permute-start | bytes 393224 | tf_op jit(solution)/shard_map/ppermute | solution.py:223
  69.6 4.0 %collective-permute-done.6.refs_1_ = bf16[128,512]{1,0:T(8,128)(2,1)S(1)} collective-permute-done((bf16[128,512]{1,0:T(8,128)(2,1)S(1)}, bf16[128,512]{1,0:T(8,128)(2,1)S(1)}, u32[]{:S(2)}, u32[]{:S(2)}) %collective-permute-start.6) | collective-permute-done | bytes 131104 | tf_op jit(solution)/shard_map/ppermute | solution.py:223
  73.7 0.0 collective-permute-start.8
  73.7 0.0 collective-permute-done.7.refs_2_
  73.7 1.3 %collective-permute-done.8.refs_3_ = bf16[128,512]{1,0:T(8,128)(2,1)S(1)} collective-permute-done((bf16[128,512]{1,0:T(8,128)(2,1)S(1)}, bf16[128,512]{1,0:T(8,128)(2,1)S(1)}, u32[]{:S(2)}, u32[]{:S(2)}) %collective-permute-start.8) | collective-permute-done | bytes 131104 | tf_op jit(solution)/shard_map/ppermute | solution.py:223
  75.0 4.6 %output.1 = bf16[2,128,1792]{2,1,0:T(8,128)(2,1)S(1)} custom-call(s32[3]{0:T(128)S(1)} %pad_add_fusion.place_ref, bf16[128,512]{1,0:T(8,128)(2,1)S(1)} %values.1.refs_0_, bf16[128,512]{1,0:T(8,128)(2,1)S(1)} %collective-permute-done.6.refs_1_, bf16[128,512]{1,0:T(8,128)(2,1)S(1)} %collective-permute-done.7.refs_2_, ...), custom_call_target="tpu_custom_call" | custom-call | tf_op jit(solution)/shard_map/output/pallas_call | solution.py:307
  79.7 28.4 %all_to_all.16.x_ref = bf16[32,8,1792]{2,1,0:T(8,128)(2,1)S(1)} all-to-all(bf16[32,8,1792]{2,1,0:T(8,128)(2,1)S(1)} %bitcast.15), channel_id=1, replica_groups=mesh['groups'=1,'tensor'=16,'replica'=2] {'replica','tensor'}, dimensions={0} | all-to-all | bytes 1835008 | tf_op jit(solution)/shard_map/all_to_all | solution.py:321
  108.1 0.8 combine.1
  (23 shorter events, 0.1 us)
Async XLA Ops:
  0.0 3.4 %copy-start.6 = (bf16[8,1536]{1,0:T(8,128)(2,1)S(1)}, bf16[8,1536]{1,0:T(8,128)(2,1)}, u32[]{:S(2)}) copy-start(bf16[8,1536]{1,0:T(8,128)(2,1)} %param.10) | copy-start | bytes 73732
  0.0 18.9 %copy-start.3 = (f32[1536]{0:T(1024)S(1)}, f32[1536]{0:T(1024)}, u32[]{:S(2)}) copy-start(f32[1536]{0:T(1024)} %refs_4_.2) | copy-start | bytes 18436
  2.9 42.4 %collective-permute-start.5 = (bf16[512,1792]{1,0:T(8,128)(2,1)}, bf16[512,1792]{1,0:T(8,128)(2,1)}, u32[]{:S(2)}, u32[]{:S(2)}) collective-permute-start(bf16[512,1792]{1,0:T(8,128)(2,1)} %constant_dynamic-slice_fusion), channel_id=1, source_target_pairs={{0,2},{2,0},{4,6},{6,4},{8,10},{10,8},{12,14},{14,12},{16,18},{18,... | collective-permute-start | bytes 5505032 | tf_op jit(solution)/shard_map/ppermute | solution.py:223
  3.4 5.5 %collective-permute-start = (bf16[8,1536]{1,0:T(8,128)(2,1)S(1)}, bf16[8,1536]{1,0:T(8,128)(2,1)S(1)}, u32[]{:S(2)}, u32[]{:S(2)}) collective-permute-start(bf16[8,1536]{1,0:T(8,128)(2,1)S(1)} %copy-done.6), channel_id=1, source_target_pairs={{0,16},{2,18},{4,20},{6,22},{8,24},{10,26},{12,28},{14,30},{16,0},... | collective-permute-start | bytes 73736 | tf_op jit(solution)/shard_map/ppermute | solution.py:223
  8.8 4.1 %collective-permute-start.1 = (bf16[16,1536]{1,0:T(8,128)(2,1)S(1)}, bf16[16,1536]{1,0:T(8,128)(2,1)S(1)}, u32[]{:S(2)}, u32[]{:S(2)}) collective-permute-start(bf16[16,1536]{1,0:T(8,128)(2,1)S(1)} %pad_maximum_fusion), channel_id=1, source_target_pairs={{0,8},{2,10},{4,12},{6,14},{8,0},{10,2},{12,4},{14,6},{16,24},{18,... | collective-permute-start | bytes 147464 | tf_op jit(solution)/shard_map/ppermute | solution.py:223
  12.9 4.6 %collective-permute-start.2 = (bf16[32,1536]{1,0:T(8,128)(2,1)S(1)}, bf16[32,1536]{1,0:T(8,128)(2,1)S(1)}, u32[]{:S(2)}, u32[]{:S(2)}) collective-permute-start(bf16[32,1536]{1,0:T(8,128)(2,1)S(1)} %constant_dynamic-update-slice_fusion.refs_0_), channel_id=1, source_target_pairs={{0,4},{2,6},{4,0},{6,2},{8,12},{10,14},{12,8},{14,10},{16,20},{18,... | collective-permute-start | bytes 294920 | tf_op jit(solution)/shard_map/ppermute | solution.py:223
  14.7 2.9 %collective-permute-start.3 = (bf16[32,1536]{1,0:T(8,128)(2,1)S(1)}, bf16[32,1536]{1,0:T(8,128)(2,1)S(1)}, u32[]{:S(2)}, u32[]{:S(2)}) collective-permute-start(bf16[32,1536]{1,0:T(8,128)(2,1)S(1)} %constant_dynamic-update-slice_fusion.refs_0_), channel_id=1, source_target_pairs={{0,2},{2,0},{4,6},{6,4},{8,10},{10,8},{12,14},{14,12},{16,18},{18,... | collective-permute-start | bytes 294920 | tf_op jit(solution)/shard_map/ppermute | solution.py:223
  17.6 1.3 %collective-permute-start.4 = (bf16[32,1536]{1,0:T(8,128)(2,1)S(1)}, bf16[32,1536]{1,0:T(8,128)(2,1)S(1)}, u32[]{:S(2)}, u32[]{:S(2)}) collective-permute-start(bf16[32,1536]{1,0:T(8,128)(2,1)S(1)} %collective-permute-done.2.refs_1_), channel_id=1, source_target_pairs={{0,2},{2,0},{4,6},{6,4},{8,10},{10,8},{12,14},{14,12},{16,18},{18,... | collective-permute-start | bytes 294920 | tf_op jit(solution)/shard_map/ppermute | solution.py:223
  17.6 12.3 %copy-start.4 = (s32[2]{0:T(128)S(1)}, s32[2]{0:T(128)}, u32[]{:S(2)}) copy-start(s32[2]{0:T(128)} %len_ref.1) | copy-start | bytes 28
  17.6 27.6 %copy-start = (bf16[2,1024,576]{1,2,0:T(8,128)(2,1)S(1)}, bf16[2,1024,576]{1,2,0:T(8,128)(2,1)}, u32[]{:S(2)}) copy-start(bf16[2,1024,576]{1,2,0:T(8,128)(2,1)} %param.17) | copy-start | bytes 7077892
  17.6 27.6 %copy-start.2 = (bf16[8,576]{1,0:T(8,128)(2,1)S(1)}, bf16[8,576]{1,0:T(8,128)(2,1)}, u32[]{:S(2)}) copy-start(bf16[8,576]{1,0:T(8,128)(2,1)} %new_ref.1) | copy-start | bytes 27652
  17.6 27.7 %copy-start.5 = (s32[2]{0:T(128)S(1)}, s32[2]{0:T(128)}, u32[]{:S(2)}) copy-start(s32[2]{0:T(128)} %count_ref.1) | copy-start | bytes 28
  23.5 21.8 %all-to-all-start = ((bf16[16,144,128]{2,1,0:T(8,128)(2,1)}), bf16[16,144,128]{2,1,0:T(8,128)(2,1)S(1)}, u32[]{:S(2)}, u32[]{:S(2)}) async-start(bf16[16,144,128]{2,1,0:T(8,128)(2,1)} %query.1), calls=%async_computation | async-start | bytes 1179648 | tf_op jit(solution)/shard_map/all_to_all | solution.py:265
  29.9 37.1 %copy-start.1 = (bf16[4,512,128]{2,1,0:T(8,128)(2,1)S(1)}, bf16[4,512,128]{2,1,0:T(8,128)(2,1)}, u32[]{:S(2)}) copy-start(bf16[4,512,128]{2,1,0:T(8,128)(2,1)} %uv_ref.1) | copy-start | bytes 1572868
  68.1 5.6 %collective-permute-start.6 = (bf16[128,512]{1,0:T(8,128)(2,1)S(1)}, bf16[128,512]{1,0:T(8,128)(2,1)S(1)}, u32[]{:S(2)}, u32[]{:S(2)}) collective-permute-start(bf16[128,512]{1,0:T(8,128)(2,1)S(1)} %values.1.refs_0_), channel_id=1, source_target_pairs={{0,1},{1,0},{2,3},{3,2},{4,5},{5,4},{6,7},{7,6},{8,9},{9,8},{10,11... | collective-permute-start | bytes 393224 | tf_op jit(solution)/shard_map/ppermute | solution.py:223
  69.6 4.1 %collective-permute-start.7 = (bf16[128,512]{1,0:T(8,128)(2,1)S(1)}, bf16[128,512]{1,0:T(8,128)(2,1)S(1)}, u32[]{:S(2)}, u32[]{:S(2)}) collective-permute-start(bf16[128,512]{1,0:T(8,128)(2,1)S(1)} %values.1.refs_0_), channel_id=1, source_target_pairs={{0,2},{2,0},{4,6},{6,4},{8,10},{10,8},{12,14},{14,12},{16,18},{18,... | collective-permute-start | bytes 393224 | tf_op jit(solution)/shard_map/ppermute | solution.py:223
  73.7 1.3 %collective-permute-start.8 = (bf16[128,512]{1,0:T(8,128)(2,1)S(1)}, bf16[128,512]{1,0:T(8,128)(2,1)S(1)}, u32[]{:S(2)}, u32[]{:S(2)}) collective-permute-start(bf16[128,512]{1,0:T(8,128)(2,1)S(1)} %collective-permute-done.6.refs_1_), channel_id=1, source_target_pairs={{0,2},{2,0},{4,6},{6,4},{8,10},{10,8},{12,14},{14,12},{16,18},{18,... | collective-permute-start | bytes 393224 | tf_op jit(solution)/shard_map/ppermute | solution.py:223

commit v5 on v3

--- a/solution.py
+++ b/solution.py
@@ -48,27 +48,22 @@
     return lax.dot_general(a, b, (((1,), (1,)), ((), ())), preferred_element_type=f32)
 
 
-def fetch_kernel(*refs):
-    count = len(refs) // 2
-    copies = [pltpu.make_async_copy(refs[i], refs[count + i], refs[-1].at[i]) for i in range(count)]
-    for copy in copies:
-        copy.start()
-    for copy in copies:
-        copy.wait()
-
-
-def fetch(arrays):
+def join_kernel(first_ref, second_ref, out_ref):
+    rows = first_ref.shape[0]
+    out_ref[:rows] = first_ref[...]
+    out_ref[rows:] = second_ref[...]
+
+
+def join(first, second):
     return pl.pallas_call(
-        fetch_kernel,
-        out_shape=[pltpu.VMEM(x.shape, x.dtype) for x in arrays],
-        in_specs=[pl.BlockSpec(memory_space=pl.ANY)] * len(arrays),
-        out_specs=[vmem_spec()] * len(arrays),
-        scratch_shapes=[pltpu.SemaphoreType.DMA((len(arrays),))],
-        compiler_params=pltpu.CompilerParams(vmem_limit_bytes=1024 * 1024),
-        cost_estimate=pl.CostEstimate(
-            flops=0, bytes_accessed=sum(4 * x.size for x in arrays), transcendentals=0
-        ),
-    )(*arrays)
+        join_kernel,
+        out_shape=jax.ShapeDtypeStruct((2 * first.shape[0], first.shape[1]), first.dtype),
+        in_specs=[vmem_spec()] * 2,
+        out_specs=vmem_spec(),
+        compiler_params=pltpu.CompilerParams(vmem_limit_bytes=4 * 1024 * 1024),
+        cost_estimate=pl.CostEstimate(flops=0, bytes_accessed=8 * first.size, transcendentals=0),
+        name="join",
+    )(first, second)
 
 
 def query_kernel(reqs, drafts, heads, place_ref, *refs):
@@ -101,7 +96,7 @@
     for h in range(heads):
         mine = row_head == h
         nope_h = jnp.where(mine, wide[:, h * QKD : h * QKD + NOPE], 0.0).astype(bf16)
-        part = mm(nope_h, uk_ref[h * NOPE : (h + 1) * NOPE])
+        part = mm(nope_h, uk_ref[h])
         absorbed = part if absorbed is None else absorbed + part
         rope_h = jnp.where(mine, wide[:, h * QKD + NOPE : (h + 1) * QKD], 0.0)
         rope = rope_h if rope is None else rope + rope_h
@@ -213,6 +208,10 @@
     return lax.ppermute(x, axis, [(i, i ^ k) for i in range(size)])
 
 
+def near(x, size):
+    return step(x, "tensor", size, 0)
+
+
 def local_step(q_latent, q_gain, q_up, w_uk, w_uv, w_o, new_kv, latent_cache, cache_len, draft_count):
     rows_dev, _ = q_latent.shape
     owners = lax.axis_size("tensor")
@@ -225,15 +224,14 @@
     core = me % 2
 
     place = jnp.stack([core, lax.axis_index("replica"), me]).astype(jnp.int32)
-    w_uk = w_uk.reshape(heads * NOPE, LATENT)
-    near = fetch((q_up, w_uk, q_latent))
-
-    first = step(q_latent, "tensor", owners, owners // 2)
-    first, up_near, uk_near, rows = lax.optimization_barrier((first, *near))
-    rows = jnp.concatenate([rows, first], axis=0)
-    bit = owners // 4
+
+    rows, gain, q_up, w_uk = (near(x, owners) for x in (q_latent, q_gain, q_up, w_uk))
+
+    bit = owners // 2
+    mine = q_latent
     while bit > 2:
-        rows = jnp.concatenate([rows, step(rows, "tensor", owners, bit)], axis=0)
+        rows = join(rows, step(mine, "tensor", owners, bit))
+        mine = rows
         bit //= 2
     parts = [rows]
     while bit:
@@ -250,7 +248,7 @@
         out_specs=vmem_spec(),
         compiler_params=params,
         name="query",
-    )(place, *parts, q_gain, up_near, uk_near)
+    )(place, *parts, gain, q_up, w_uk)
     arrived = lax.all_to_all(queries, "tensor", split_axis=0, concat_axis=0, tiled=True)
 
     half = w_o.shape[1] // 2
@@ -282,6 +280,8 @@
     )(cache_len, draft_count, arrived, table(cosine, cosine), table(-sine, sine), new_kv, jnp.swapaxes(latent_cache, 1, 2))
     returned = lax.all_to_all(latent, "tensor", split_axis=0, concat_axis=0, tiled=True)
 
+    returned, w_own, w_other = lax.optimization_barrier((returned, w_own, w_other))
+    w_own, w_other = near(w_own, owners), near(w_other, owners)
     values = pl.pallas_call(
         functools.partial(value_kernel, reqs, drafts, heads),
         out_shape=jax.ShapeDtypeStruct((owners * rows_dev, heads * VDIM), bf16),
@@ -290,9 +290,7 @@
         compiler_params=params,
         name="values",
     )(returned, w_uv)
-    nearest = step(values, "replica", replicas, 1)
-    own = [values, nearest] + [step(values, "replica", replicas, k) for k in range(2, replicas)]
-    (w_other,) = fetch((w_other,))
+    own = [values] + [step(values, "replica", replicas, k) for k in range(1, replicas)]
     other = [step(piece, "tensor", owners, 1) for piece in own]
 
     product = pl.pallas_call(

time: 104 us -> 128 us (1.23)
  starting transfers between devices: 12.8 us -> 37.3 us
  local copies, waits for them, and re-layouts: 6.15 us -> 3.07 us
  waiting for transfers between devices: 25.9 us -> 28.4 us
    ppermute x9 -> x15, starting transfers between devices: 8.86 us -> 30.9 us  [step(): return lax.ppermute(x, axis, [(i, i ^ k) for i in range(size)])]
    unnamed x26 -> x16, local copies, waits for them, and re-layouts: 3.13 us -> 0.03 us
    ppermute x9 -> x15, waiting for transfers between devices: 10.9 us -> 13.5 us  [step(): return lax.ppermute(x, axis, [(i, i ^ k) for i in range(size)])]
    all_to_all x1, starting transfers between devices: 3.91 us -> 6.4 us  [local_step(): lax.all_to_all(queries, 'tensor', split_axis=0, concat_axis=0, tiled=True)]
    pallas_call x2, Pallas kernels: 1.77 us -> 0.01 us  [join(): pl.pallas_call(join_kernel, out_shape=jax.ShapeDtypeStruct((2 * first.sha...]
  transfers between devices with their start and end apart: 10 -> 16, of which waited for: 5 -> 7; matrix products, arithmetic and copies ran while one was open for 3% -> 3% of each run, Pallas kernels for 4% -> 4%
where the time goes in v5:
time: 128 us; the launch traced here: 127 us
  blocking collectives  47 us (37%)
  starting transfers between devices  37.3 us (29%)
  waiting for transfers between devices  28.4 us (22%)
  Pallas kernels  10.6 us (8%)
  local copies, waits for them, and re-layouts  3.07 us (2%)
    ppermute x15, starting transfers between devices, step(): return lax.ppermute(x, axis, [(i, i ^ k) for i in range(size)])  30.9 us
    all_to_all x1, blocking collectives, local_step(): lax.all_to_all(product, ('replica', 'tensor'), split_axis=0, concat_axis=...  28.4 us
    all_to_all x1, blocking collectives, local_step(): lax.all_to_all(latent, 'tensor', split_axis=0, concat_axis=0, tiled=True)  18.5 us
    all_to_all x1, waiting for transfers between devices, local_step(): lax.all_to_all(queries, 'tensor', split_axis=0, concat_axis=0, tiled=True)  14.9 us
    ppermute x15, waiting for transfers between devices, step(): return lax.ppermute(x, axis, [(i, i ^ k) for i in range(size)])  13.5 us
    all_to_all x1, starting transfers between devices, local_step(): lax.all_to_all(queries, 'tensor', split_axis=0, concat_axis=0, tiled=True)  6.4 us
    pallas_call x1, Pallas kernels, local_step(): pl.pallas_call(functools.partial(query_kernel, reqs, drafts, heads), out_...  3.93 us
    pallas_call x1, Pallas kernels, local_step(): pl.pallas_call(functools.partial(attend_kernel, reqs, drafts, heads), out...  3.19 us
  transfers between devices with their start and end apart: 16, of which 7 were waited for; matrix products, arithmetic and copies ran while one was open for 3% of the time, Pallas kernels for 4%

profile of v5, /device:TPU:0, one launch (start us, length us, event | category | flops | bytes accessed | tf_op | source)
XLA Modules:
  0.0 126.7 jit_solution(7428674721341803598)
XLA Ops:
  0.0 18.6 %collective-permute-start.7 = (bf16[1536,768]{1,0:T(8,128)(2,1)}, bf16[1536,768]{1,0:T(8,128)(2,1)}, u32[]{:S(2)}, u32[]{:S(2)}) collective-permute-start(bf16[1536,768]{1,0:T(8,128)(2,1)} %param.12), channel_id=1, source_target_pairs={{0,0},{2,2},{4,4},{6,6},{8,8},{10,10},{12,12},{14,14},{16,16},{18,... | collective-permute-start | bytes 7077896 | tf_op jit(solution)/shard_map/ppermute | solution.py:208
  18.6 2.9 %constant_dynamic-slice_fusion = bf16[512,1792]{1,0:T(8,128)(2,1)} fusion(bf16[512,3584]{1,0:T(8,128)(2,1)} %param.15, s32[]{:T(128)S(6)} %select_n.11), kind=kLoop, calls=%fused_computation.7 | loop fusion | bytes 3670020 | tf_op jit(solution)/shard_map/dynamic_slice | solution.py:255
  21.5 0.5 collective-permute-start.9
  22.0 1.0 collective-permute-start.8
  23.0 3.6 %collective-permute-start.1 = (bf16[8,1536]{1,0:T(8,128)(2,1)S(1)}, bf16[8,1536]{1,0:T(8,128)(2,1)S(1)}, u32[]{:S(2)}, u32[]{:S(2)}) collective-permute-start(bf16[8,1536]{1,0:T(8,128)(2,1)S(1)} %copy-done.6), channel_id=1, source_target_pairs={{0,16},{2,18},{4,20},{6,22},{8,24},{10,26},{12,28},{14,30},{16,0},... | collective-permute-start | bytes 73736 | tf_op jit(solution)/shard_map/ppermute | solution.py:208
  26.6 1.9 %collective-permute-done.1.second_ref = bf16[8,1536]{1,0:T(8,128)(2,1)S(1)} collective-permute-done((bf16[8,1536]{1,0:T(8,128)(2,1)S(1)}, bf16[8,1536]{1,0:T(8,128)(2,1)S(1)}, u32[]{:S(2)}, u32[]{:S(2)}) %collective-permute-start.1) | collective-permute-done | bytes 24608 | tf_op jit(solution)/shard_map/ppermute | solution.py:208
  28.5 1.9 %collective-permute-start.2 = (bf16[16,1536]{1,0:T(8,128)(2,1)S(1)}, bf16[16,1536]{1,0:T(8,128)(2,1)S(1)}, u32[]{:S(2)}, u32[]{:S(2)}) collective-permute-start(bf16[16,1536]{1,0:T(8,128)(2,1)S(1)} %join.2.first_ref), channel_id=1, source_target_pairs={{0,8},{2,10},{4,12},{6,14},{8,0},{10,2},{12,4},{14,6},{16,24},{18,... | collective-permute-start | bytes 147464 | tf_op jit(solution)/shard_map/ppermute | solution.py:208
  30.4 2.3 %collective-permute-done.2.second_ref = bf16[16,1536]{1,0:T(8,128)(2,1)S(1)} collective-permute-done((bf16[16,1536]{1,0:T(8,128)(2,1)S(1)}, bf16[16,1536]{1,0:T(8,128)(2,1)S(1)}, u32[]{:S(2)}, u32[]{:S(2)}) %collective-permute-start.2) | collective-permute-done | bytes 49184 | tf_op jit(solution)/shard_map/ppermute | solution.py:208
  32.7 1.8 %collective-permute-start.3 = (bf16[32,1536]{1,0:T(8,128)(2,1)S(1)}, bf16[32,1536]{1,0:T(8,128)(2,1)S(1)}, u32[]{:S(2)}, u32[]{:S(2)}) collective-permute-start(bf16[32,1536]{1,0:T(8,128)(2,1)S(1)} %join.3.refs_0_), channel_id=1, source_target_pairs={{0,4},{2,6},{4,0},{6,2},{8,12},{10,14},{12,8},{14,10},{16,20},{18,... | collective-permute-start | bytes 294920 | tf_op jit(solution)/shard_map/ppermute | solution.py:208
  34.5 0.1 collective-permute-start.4
  34.6 2.8 %collective-permute-done.3.refs_1_ = bf16[32,1536]{1,0:T(8,128)(2,1)S(1)} collective-permute-done((bf16[32,1536]{1,0:T(8,128)(2,1)S(1)}, bf16[32,1536]{1,0:T(8,128)(2,1)S(1)}, u32[]{:S(2)}, u32[]{:S(2)}) %collective-permute-start.3) | collective-permute-done | bytes 98336 | tf_op jit(solution)/shard_map/ppermute | solution.py:208
  37.4 0.1 pad_add_fusion.place_ref
  37.5 1.2 collective-permute-done.5.refs_3_
  38.7 3.9 %query.1 = bf16[16,144,128]{2,1,0:T(8,128)(2,1)} custom-call(s32[3]{0:T(128)S(1)} %pad_add_fusion.place_ref, bf16[32,1536]{1,0:T(8,128)(2,1)S(1)} %join.3.refs_0_, bf16[32,1536]{1,0:T(8,128)(2,1)S(1)} %collective-permute-done.3.refs_1_, bf16[32,1536]{1,0:T(8,128)(2,1)S(1)} %collective-permute-done.4.refs_2_, ...), custom_call_target="tpu_custom_call" | custom-call | tf_op jit(solution)/shard_map/query/pallas_call | solution.py:244
  42.6 6.4 %all-to-all-start = ((bf16[16,144,128]{2,1,0:T(8,128)(2,1)}), bf16[16,144,128]{2,1,0:T(8,128)(2,1)S(1)}, u32[]{:S(2)}, u32[]{:S(2)}) async-start(bf16[16,144,128]{2,1,0:T(8,128)(2,1)} %query.1), calls=%async_computation | async-start | bytes 1179648 | tf_op jit(solution)/shard_map/all_to_all | solution.py:252
  49.0 0.0 copy-start.1
  49.1 0.1 fusion
  49.2 0.1 maximum_bitcast_fusion
  49.3 0.1 broadcast_in_dim.22
  49.4 0.1 broadcast_in_dim.25
  49.4 14.9 %all-to-all-done.q_ref = bf16[16,144,128]{2,1,0:T(8,128)(2,1)S(1)} async-done(((bf16[16,144,128]{2,1,0:T(8,128)(2,1)}), bf16[16,144,128]{2,1,0:T(8,128)(2,1)S(1)}, u32[]{:S(2)}, u32[]{:S(2)}) %all-to-all-start) | async-done | bytes 589856 | tf_op jit(solution)/shard_map/all_to_all | solution.py:252
  64.4 3.2 %attend.1 = bf16[16,32,512]{2,1,0:T(8,128)(2,1)S(1)} custom-call(s32[2]{0:T(128)S(1)} %copy-done.3, s32[2]{0:T(128)S(1)} %copy-done.4, bf16[16,144,128]{2,1,0:T(8,128)(2,1)S(1)} %all-to-all-done.q_ref, f32[1,16,128]{2,1,0:T(8,128)S(1)} %bitcast.18, f32[1,16,128]{2,1,0:T(8,128)S(1)} %bitcast.17, bf16[8,576]{1,0:T(8,128)(2,1)S(1)} %copy-done.2, ...), custom_call_target="tpu_custom_call" | custom-call | tf_op jit(solution)/shard_map/attend/pallas_call | solution.py:273
  67.6 18.5 %all_to_all.15.latent_ref = bf16[16,32,512]{2,1,0:T(8,128)(2,1)S(1)} all-to-all(bf16[16,32,512]{2,1,0:T(8,128)(2,1)S(1)} %attend.1), channel_id=1, replica_groups=mesh['groups'=1,'tensor'=16,'replica'=2] {'tensor'}, dimensions={0} | all-to-all | bytes 1048576 | tf_op jit(solution)/shard_map/all_to_all | solution.py:281
  86.1 0.2 collective-permute-start.13
  86.4 1.5 %collective-permute-start.14 = (bf16[512,1792]{1,0:T(8,128)(2,1)}, bf16[512,1792]{1,0:T(8,128)(2,1)S(1)}, u32[]{:S(2)}, u32[]{:S(2)}) collective-permute-start(bf16[512,1792]{1,0:T(8,128)(2,1)} %collective-permute-done.9), channel_id=1, source_target_pairs={{0,0},{2,2},{4,4},{6,6},{8,8},{10,10},{12,12},{14,14},{16,16},{18,... | collective-permute-start | bytes 5505032 | tf_op jit(solution)/shard_map/ppermute | solution.py:208
  87.9 1.0 values.1.refs_0_
  88.9 1.6 %collective-permute-start.10 = (bf16[128,512]{1,0:T(8,128)(2,1)S(1)}, bf16[128,512]{1,0:T(8,128)(2,1)S(1)}, u32[]{:S(2)}, u32[]{:S(2)}) collective-permute-start(bf16[128,512]{1,0:T(8,128)(2,1)S(1)} %values.1.refs_0_), channel_id=1, source_target_pairs={{0,1},{1,0},{2,3},{3,2},{4,5},{5,4},{6,7},{7,6},{8,9},{9,8},{10,11... | collective-permute-start | bytes 393224 | tf_op jit(solution)/shard_map/ppermute | solution.py:208
  90.5 4.0 %collective-permute-done.10.refs_1_ = bf16[128,512]{1,0:T(8,128)(2,1)S(1)} collective-permute-done((bf16[128,512]{1,0:T(8,128)(2,1)S(1)}, bf16[128,512]{1,0:T(8,128)(2,1)S(1)}, u32[]{:S(2)}, u32[]{:S(2)}) %collective-permute-start.10) | collective-permute-done | bytes 131104 | tf_op jit(solution)/shard_map/ppermute | solution.py:208
  94.5 1.3 %collective-permute-done.12.refs_3_ = bf16[128,512]{1,0:T(8,128)(2,1)S(1)} collective-permute-done((bf16[128,512]{1,0:T(8,128)(2,1)S(1)}, bf16[128,512]{1,0:T(8,128)(2,1)S(1)}, u32[]{:S(2)}, u32[]{:S(2)}) %collective-permute-start.12) | collective-permute-done | bytes 131104 | tf_op jit(solution)/shard_map/ppermute | solution.py:208
  95.9 1.7 %output.1 = bf16[2,128,1792]{2,1,0:T(8,128)(2,1)S(1)} custom-call(s32[3]{0:T(128)S(1)} %pad_add_fusion.place_ref, bf16[128,512]{1,0:T(8,128)(2,1)S(1)} %values.1.refs_0_, bf16[128,512]{1,0:T(8,128)(2,1)S(1)} %collective-permute-done.10.refs_1_, bf16[128,512]{1,0:T(8,128)(2,1)S(1)} %collective-permute-done.11.refs_2_, ...), custom_call_target="tpu_custom_call" | custom-call | tf_op jit(solution)/shard_map/output/pallas_call | solution.py:296
  97.5 28.4 %all_to_all.16.x_ref = bf16[32,8,1792]{2,1,0:T(8,128)(2,1)S(1)} all-to-all(bf16[32,8,1792]{2,1,0:T(8,128)(2,1)S(1)} %bitcast.15), channel_id=1, replica_groups=mesh['groups'=1,'tensor'=16,'replica'=2] {'replica','tensor'}, dimensions={0} | all-to-all | bytes 1835008 | tf_op jit(solution)/shard_map/all_to_all | solution.py:305
  126.0 0.8 combine.1
  (35 shorter events, 0.1 us)
Async XLA Ops:
  0.0 23.0 %copy-start.6 = (bf16[8,1536]{1,0:T(8,128)(2,1)S(1)}, bf16[8,1536]{1,0:T(8,128)(2,1)}, u32[]{:S(2)}) copy-start(bf16[8,1536]{1,0:T(8,128)(2,1)} %param.10) | copy-start | bytes 73732
  0.0 34.5 %copy-start.7 = (f32[1536]{0:T(1024)S(1)}, f32[1536]{0:T(1024)}, u32[]{:S(2)}) copy-start(f32[1536]{0:T(1024)} %param.11) | copy-start | bytes 18436
  0.0 38.7 %collective-permute-start.7 = (bf16[1536,768]{1,0:T(8,128)(2,1)}, bf16[1536,768]{1,0:T(8,128)(2,1)}, u32[]{:S(2)}, u32[]{:S(2)}) collective-permute-start(bf16[1536,768]{1,0:T(8,128)(2,1)} %param.12), channel_id=1, source_target_pairs={{0,0},{2,2},{4,4},{6,6},{8,8},{10,10},{12,12},{14,14},{16,16},{18,... | collective-permute-start | bytes 7077896 | tf_op jit(solution)/shard_map/ppermute | solution.py:208
  21.5 28.0 %collective-permute-start.9 = (bf16[512,1792]{1,0:T(8,128)(2,1)}, bf16[512,1792]{1,0:T(8,128)(2,1)}, u32[]{:S(2)}, u32[]{:S(2)}) collective-permute-start(bf16[512,1792]{1,0:T(8,128)(2,1)} %constant_dynamic-slice_fusion), channel_id=1, source_target_pairs={{0,2},{2,0},{4,6},{6,4},{8,10},{10,8},{12,14},{14,12},{16,18},{18,... | collective-permute-start | bytes 5505032 | tf_op jit(solution)/shard_map/ppermute | solution.py:208
  22.0 16.7 %collective-permute-start.8 = (bf16[4,128,512]{2,1,0:T(8,128)(2,1)}, bf16[4,128,512]{2,1,0:T(8,128)(2,1)S(1)}, u32[]{:S(2)}, u32[]{:S(2)}) collective-permute-start(bf16[4,128,512]{2,1,0:T(8,128)(2,1)} %param.13), channel_id=1, source_target_pairs={{0,0},{2,2},{4,4},{6,6},{8,8},{10,10},{12,12},{14,14},{16,16},{18,... | collective-permute-start | bytes 1572872 | tf_op jit(solution)/shard_map/ppermute | solution.py:208
  23.0 5.5 %collective-permute-start.1 = (bf16[8,1536]{1,0:T(8,128)(2,1)S(1)}, bf16[8,1536]{1,0:T(8,128)(2,1)S(1)}, u32[]{:S(2)}, u32[]{:S(2)}) collective-permute-start(bf16[8,1536]{1,0:T(8,128)(2,1)S(1)} %copy-done.6), channel_id=1, source_target_pairs={{0,16},{2,18},{4,20},{6,22},{8,24},{10,26},{12,28},{14,30},{16,0},... | collective-permute-start | bytes 73736 | tf_op jit(solution)/shard_map/ppermute | solution.py:208
  26.6 1.9 %collective-permute-start = (bf16[8,1536]{1,0:T(8,128)(2,1)S(1)}, bf16[8,1536]{1,0:T(8,128)(2,1)S(1)}, u32[]{:S(2)}, u32[]{:S(2)}) collective-permute-start(bf16[8,1536]{1,0:T(8,128)(2,1)S(1)} %copy-done.6), channel_id=1, source_target_pairs={{0,0},{2,2},{4,4},{6,6},{8,8},{10,10},{12,12},{14,14},{16,16},{18,... | collective-permute-start | bytes 73736 | tf_op jit(solution)/shard_map/ppermute | solution.py:208
  28.5 4.2 %collective-permute-start.2 = (bf16[16,1536]{1,0:T(8,128)(2,1)S(1)}, bf16[16,1536]{1,0:T(8,128)(2,1)S(1)}, u32[]{:S(2)}, u32[]{:S(2)}) collective-permute-start(bf16[16,1536]{1,0:T(8,128)(2,1)S(1)} %join.2.first_ref), channel_id=1, source_target_pairs={{0,8},{2,10},{4,12},{6,14},{8,0},{10,2},{12,4},{14,6},{16,24},{18,... | collective-permute-start | bytes 147464 | tf_op jit(solution)/shard_map/ppermute | solution.py:208
  32.7 4.7 %collective-permute-start.3 = (bf16[32,1536]{1,0:T(8,128)(2,1)S(1)}, bf16[32,1536]{1,0:T(8,128)(2,1)S(1)}, u32[]{:S(2)}, u32[]{:S(2)}) collective-permute-start(bf16[32,1536]{1,0:T(8,128)(2,1)S(1)} %join.3.refs_0_), channel_id=1, source_target_pairs={{0,4},{2,6},{4,0},{6,2},{8,12},{10,14},{12,8},{14,10},{16,20},{18,... | collective-permute-start | bytes 294920 | tf_op jit(solution)/shard_map/ppermute | solution.py:208
  34.5 2.9 %collective-permute-start.4 = (bf16[32,1536]{1,0:T(8,128)(2,1)S(1)}, bf16[32,1536]{1,0:T(8,128)(2,1)S(1)}, u32[]{:S(2)}, u32[]{:S(2)}) collective-permute-start(bf16[32,1536]{1,0:T(8,128)(2,1)S(1)} %join.3.refs_0_), channel_id=1, source_target_pairs={{0,2},{2,0},{4,6},{6,4},{8,10},{10,8},{12,14},{14,12},{16,18},{18,... | collective-permute-start | bytes 294920 | tf_op jit(solution)/shard_map/ppermute | solution.py:208
  37.4 1.3 %collective-permute-start.5 = (bf16[32,1536]{1,0:T(8,128)(2,1)S(1)}, bf16[32,1536]{1,0:T(8,128)(2,1)S(1)}, u32[]{:S(2)}, u32[]{:S(2)}) collective-permute-start(bf16[32,1536]{1,0:T(8,128)(2,1)S(1)} %collective-permute-done.3.refs_1_), channel_id=1, source_target_pairs={{0,2},{2,0},{4,6},{6,4},{8,10},{10,8},{12,14},{14,12},{16,18},{18,... | collective-permute-start | bytes 294920 | tf_op jit(solution)/shard_map/ppermute | solution.py:208
  37.4 11.6 %copy-start.3 = (s32[2]{0:T(128)S(1)}, s32[2]{0:T(128)}, u32[]{:S(2)}) copy-start(s32[2]{0:T(128)} %len_ref.1) | copy-start | bytes 28
  37.4 26.9 %copy-start = (bf16[2,1024,576]{1,2,0:T(8,128)(2,1)S(1)}, bf16[2,1024,576]{1,2,0:T(8,128)(2,1)}, u32[]{:S(2)}) copy-start(bf16[2,1024,576]{1,2,0:T(8,128)(2,1)} %param.17) | copy-start | bytes 7077892
  37.4 26.9 %copy-start.2 = (bf16[8,576]{1,0:T(8,128)(2,1)S(1)}, bf16[8,576]{1,0:T(8,128)(2,1)}, u32[]{:S(2)}) copy-start(bf16[8,576]{1,0:T(8,128)(2,1)} %new_ref.1) | copy-start | bytes 27652
  37.4 27.0 %copy-start.4 = (s32[2]{0:T(128)S(1)}, s32[2]{0:T(128)}, u32[]{:S(2)}) copy-start(s32[2]{0:T(128)} %count_ref.1) | copy-start | bytes 28
  42.6 21.8 %all-to-all-start = ((bf16[16,144,128]{2,1,0:T(8,128)(2,1)}), bf16[16,144,128]{2,1,0:T(8,128)(2,1)S(1)}, u32[]{:S(2)}, u32[]{:S(2)}) async-start(bf16[16,144,128]{2,1,0:T(8,128)(2,1)} %query.1), calls=%async_computation | async-start | bytes 1179648 | tf_op jit(solution)/shard_map/all_to_all | solution.py:252
  49.0 38.9 %copy-start.1 = (bf16[4,512,128]{2,1,0:T(8,128)(2,1)S(1)}, bf16[4,512,128]{2,1,0:T(8,128)(2,1)}, u32[]{:S(2)}) copy-start(bf16[4,512,128]{2,1,0:T(8,128)(2,1)} %uv_ref.1) | copy-start | bytes 1572868
  64.4 21.8 %copy-start.5 = (bf16[512,3584]{1,0:T(8,128)(2,1)S(1)}, bf16[512,3584]{1,0:T(8,128)(2,1)}, u32[]{:S(2)}) copy-start(bf16[512,3584]{1,0:T(8,128)(2,1)} %param.15) | copy-start | bytes 11010052
  86.1 9.7 %collective-permute-start.13 = (bf16[512,3584]{1,0:T(8,128)(2,1)S(1)}, bf16[512,3584]{1,0:T(8,128)(2,1)S(1)}, u32[]{:S(2)}, u32[]{:S(2)}) collective-permute-start(bf16[512,3584]{1,0:T(8,128)(2,1)S(1)} %copy-done.5), channel_id=1, source_target_pairs={{0,0},{2,2},{4,4},{6,6},{8,8},{10,10},{12,12},{14,14},{16,16},{18,... | collective-permute-start | bytes 11010056 | tf_op jit(solution)/shard_map/ppermute | solution.py:208
  86.4 9.5 %collective-permute-start.14 = (bf16[512,1792]{1,0:T(8,128)(2,1)}, bf16[512,1792]{1,0:T(8,128)(2,1)S(1)}, u32[]{:S(2)}, u32[]{:S(2)}) collective-permute-start(bf16[512,1792]{1,0:T(8,128)(2,1)} %collective-permute-done.9), channel_id=1, source_target_pairs={{0,0},{2,2},{4,4},{6,6},{8,8},{10,10},{12,12},{14,14},{16,16},{18,... | collective-permute-start | bytes 5505032 | tf_op jit(solution)/shard_map/ppermute | solution.py:208
  88.9 5.6 %collective-permute-start.10 = (bf16[128,512]{1,0:T(8,128)(2,1)S(1)}, bf16[128,512]{1,0:T(8,128)(2,1)S(1)}, u32[]{:S(2)}, u32[]{:S(2)}) collective-permute-start(bf16[128,512]{1,0:T(8,128)(2,1)S(1)} %values.1.refs_0_), channel_id=1, source_target_pairs={{0,1},{1,0},{2,3},{3,2},{4,5},{5,4},{6,7},{7,6},{8,9},{9,8},{10,11... | collective-permute-start | bytes 393224 | tf_op jit(solution)/shard_map/ppermute | solution.py:208
  90.5 4.1 %collective-permute-start.11 = (bf16[128,512]{1,0:T(8,128)(2,1)S(1)}, bf16[128,512]{1,0:T(8,128)(2,1)S(1)}, u32[]{:S(2)}, u32[]{:S(2)}) collective-permute-start(bf16[128,512]{1,0:T(8,128)(2,1)S(1)} %values.1.refs_0_), channel_id=1, source_target_pairs={{0,2},{2,0},{4,6},{6,4},{8,10},{10,8},{12,14},{14,12},{16,18},{18,... | collective-permute-start | bytes 393224 | tf_op jit(solution)/shard_map/ppermute | solution.py:208
  94.5 1.3 %collective-permute-start.12 = (bf16[128,512]{1,0:T(8,128)(2,1)S(1)}, bf16[128,512]{1,0:T(8,128)(2,1)S(1)}, u32[]{:S(2)}, u32[]{:S(2)}) collective-permute-start(bf16[128,512]{1,0:T(8,128)(2,1)S(1)} %collective-permute-done.10.refs_1_), channel_id=1, source_target_pairs={{0,2},{2,0},{4,6},{6,4},{8,10},{10,8},{12,14},{14,12},{16,18},{18,... | collective-permute-start | bytes 393224 | tf_op jit(solution)/shard_map/ppermute | solution.py:208
  (1 other events, 0.0 us)

commit v6 on v3

--- a/solution.py
+++ b/solution.py
@@ -14,6 +14,8 @@
 VDIM = 128
 QKD = NOPE + ROPE
 LANES = 128
+
+FETCH_VMEM = 53_700_000
 
 rms_eps = 1e-06
 rope_base = 50000.0
@@ -57,14 +59,14 @@
         copy.wait()
 
 
-def fetch(arrays):
+def fetch(arrays, limit):
     return pl.pallas_call(
         fetch_kernel,
         out_shape=[pltpu.VMEM(x.shape, x.dtype) for x in arrays],
         in_specs=[pl.BlockSpec(memory_space=pl.ANY)] * len(arrays),
         out_specs=[vmem_spec()] * len(arrays),
         scratch_shapes=[pltpu.SemaphoreType.DMA((len(arrays),))],
-        compiler_params=pltpu.CompilerParams(vmem_limit_bytes=1024 * 1024),
+        compiler_params=pltpu.CompilerParams(vmem_limit_bytes=limit),
         cost_estimate=pl.CostEstimate(
             flops=0, bytes_accessed=sum(4 * x.size for x in arrays), transcendentals=0
         ),
@@ -226,10 +228,10 @@
 
     place = jnp.stack([core, lax.axis_index("replica"), me]).astype(jnp.int32)
     w_uk = w_uk.reshape(heads * NOPE, LATENT)
-    near = fetch((q_up, w_uk, q_latent))
+    near = fetch((q_up, w_uk, q_gain, q_latent), FETCH_VMEM)
 
     first = step(q_latent, "tensor", owners, owners // 2)
-    first, up_near, uk_near, rows = lax.optimization_barrier((first, *near))
+    first, q_up, w_uk, gain, rows = lax.optimization_barrier((first, *near))
     rows = jnp.concatenate([rows, first], axis=0)
     bit = owners // 4
     while bit > 2:
@@ -250,7 +252,7 @@
         out_specs=vmem_spec(),
         compiler_params=params,
         name="query",
-    )(place, *parts, q_gain, up_near, uk_near)
+    )(place, *parts, gain, q_up, w_uk)
     arrived = lax.all_to_all(queries, "tensor", split_axis=0, concat_axis=0, tiled=True)
 
     half = w_o.shape[1] // 2
@@ -292,7 +294,7 @@
     )(returned, w_uv)
     nearest = step(values, "replica", replicas, 1)
     own = [values, nearest] + [step(values, "replica", replicas, k) for k in range(2, replicas)]
-    (w_other,) = fetch((w_other,))
+    (w_other,) = fetch((w_other,), 1024 * 1024)
     other = [step(piece, "tensor", owners, 1) for piece in own]
 
     product = pl.pallas_call(

time: 104 us -> 105 us (level)
  Pallas kernels: 11.2 us -> 12.7 us
    pallas_call x2, Pallas kernels: 1.77 us -> 3.3 us  [fetch(): pl.pallas_call(fetch_kernel, out_shape=[pltpu.VMEM(x.shape, x.dtype) for...]
    unnamed x26 -> x18, local copies, waits for them, and re-layouts: 3.13 us -> 3.12 us
  transfers between devices with their start and end apart: 10 -> 10, of which waited for: 5 -> 5; matrix products, arithmetic and copies ran while one was open for 3% -> 3% of each run, Pallas kernels for 4% -> 6%
where the time goes in v6:
time: 105 us
  blocking collectives  47.1 us (45%)
  waiting for transfers between devices  25.9 us (25%)
  starting transfers between devices  12.7 us (12%)
  Pallas kernels  12.7 us (12%)
  local copies, waits for them, and re-layouts  6.14 us (6%)
    all_to_all x1, blocking collectives, local_step(): lax.all_to_all(product, ('replica', 'tensor'), split_axis=0, concat_axis=...  28.5 us
    all_to_all x1, blocking collectives, local_step(): lax.all_to_all(latent, 'tensor', split_axis=0, concat_axis=0, tiled=True)  18.6 us
    all_to_all x1, waiting for transfers between devices, local_step(): lax.all_to_all(queries, 'tensor', split_axis=0, concat_axis=0, tiled=True)  14.9 us
    ppermute x9, waiting for transfers between devices, step(): return lax.ppermute(x, axis, [(i, i ^ k) for i in range(size)])  10.9 us
    ppermute x9, starting transfers between devices, step(): return lax.ppermute(x, axis, [(i, i ^ k) for i in range(size)])  8.79 us
    all_to_all x1, starting transfers between devices, local_step(): lax.all_to_all(queries, 'tensor', split_axis=0, concat_axis=0, tiled=True)  3.91 us
    pallas_call x2, Pallas kernels, fetch(): pl.pallas_call(fetch_kernel, out_shape=[pltpu.VMEM(x.shape, x.dtype) for...  3.3 us
    pallas_call x1, Pallas kernels, local_step(): pl.pallas_call(functools.partial(attend_kernel, reqs, drafts, heads), out...  3.17 us
  transfers between devices with their start and end apart: 10, of which 5 were waited for; matrix products, arithmetic and copies ran while one was open for 3% of the time, Pallas kernels for 6%

profile of v6, /device:TPU:0, one launch (start us, length us, event | category | flops | bytes accessed | tf_op | source)
XLA Modules:
  0.0 105.0 jit_solution(7461492290077828680)
XLA Ops:
  0.0 4.1 %collective-permute-start = (bf16[8,1536]{1,0:T(8,128)(2,1)}, bf16[8,1536]{1,0:T(8,128)(2,1)S(1)}, u32[]{:S(2)}, u32[]{:S(2)}) collective-permute-start(bf16[8,1536]{1,0:T(8,128)(2,1)} %refs_3_.1), channel_id=1, source_target_pairs={{0,16},{2,18},{4,20},{6,22},{8,24},{10,26},{12,28},{14,30},{16,0},... | collective-permute-start | bytes 73736 | tf_op jit(solution)/shard_map/ppermute | solution.py:215
  4.1 2.8 %constant_dynamic-slice_fusion = bf16[512,1792]{1,0:T(8,128)(2,1)} fusion(bf16[512,3584]{1,0:T(8,128)(2,1)} %refs_4_.1, s32[]{:T(128)S(6)} %select_n.11), kind=kLoop, calls=%fused_computation.11 | loop fusion | bytes 3670020 | tf_op jit(solution)/shard_map/dynamic_slice | solution.py:259
  6.9 0.0 collective-permute-start.5
  6.9 1.8 %shard_map.100 = (bf16[1536,768]{1,0:T(8,128)(2,1)S(1)}, bf16[512,512]{1,0:T(8,128)(2,1)S(1)}, f32[1536]{0:T(1024)S(1)}, bf16[8,1536]{1,0:T(8,128)(2,1)S(1)}) custom-call(bf16[1536,768]{1,0:T(8,128)(2,1)} %refs_0_.1, bf16[512,512]{1,0:T(8,128)(2,1)} %bitcast.20, f32[1536]{0:T(1024)} %refs_2_.1, bf16[8,1536]{1,0:T(8,128)(2,1)} %refs_3_.1), custom_call_target="tpu_custom_call" | custom-call | bytes 5822464 | tf_op jit(solution)/shard_map/pallas_call | solution.py:63
  8.7 1.4 %copy-done.2 = bf16[1536,768]{1,0:T(8,128)(2,1)} copy-done((bf16[1536,768]{1,0:T(8,128)(2,1)}, bf16[1536,768]{1,0:T(8,128)(2,1)S(1)}, u32[]{:S(2)}) %copy-start.2) | copy-done | bytes 2359320
  10.1 0.0 collective-permute-done
  10.2 1.6 %collective-permute-start.1 = (bf16[16,1536]{1,0:T(8,128)(2,1)S(1)}, bf16[16,1536]{1,0:T(8,128)(2,1)S(1)}, u32[]{:S(2)}, u32[]{:S(2)}) collective-permute-start(bf16[16,1536]{1,0:T(8,128)(2,1)S(1)} %pad_maximum_fusion), channel_id=1, source_target_pairs={{0,8},{2,10},{4,12},{6,14},{8,0},{10,2},{12,4},{14,6},{16,24},{18,... | collective-permute-start | bytes 147464 | tf_op jit(solution)/shard_map/ppermute | solution.py:215
  11.8 2.6 %collective-permute-done.1 = bf16[16,1536]{1,0:T(8,128)(2,1)S(1)} collective-permute-done((bf16[16,1536]{1,0:T(8,128)(2,1)S(1)}, bf16[16,1536]{1,0:T(8,128)(2,1)S(1)}, u32[]{:S(2)}, u32[]{:S(2)}) %collective-permute-start.1) | collective-permute-done | bytes 49184 | tf_op jit(solution)/shard_map/ppermute | solution.py:215
  14.4 1.5 %collective-permute-start.2 = (bf16[32,1536]{1,0:T(8,128)(2,1)S(1)}, bf16[32,1536]{1,0:T(8,128)(2,1)S(1)}, u32[]{:S(2)}, u32[]{:S(2)}) collective-permute-start(bf16[32,1536]{1,0:T(8,128)(2,1)S(1)} %constant_dynamic-update-slice_fusion.refs_0_), channel_id=1, source_target_pairs={{0,4},{2,6},{4,0},{6,2},{8,12},{10,14},{12,8},{14,10},{16,20},{18,... | collective-permute-start | bytes 294920 | tf_op jit(solution)/shard_map/ppermute | solution.py:215
  15.9 3.1 %collective-permute-done.2.refs_1_ = bf16[32,1536]{1,0:T(8,128)(2,1)S(1)} collective-permute-done((bf16[32,1536]{1,0:T(8,128)(2,1)S(1)}, bf16[32,1536]{1,0:T(8,128)(2,1)S(1)}, u32[]{:S(2)}, u32[]{:S(2)}) %collective-permute-start.2) | collective-permute-done | bytes 98336 | tf_op jit(solution)/shard_map/ppermute | solution.py:215
  19.0 0.0 collective-permute-start.4
  19.0 0.1 pad_add_fusion.place_ref
  19.1 0.0 collective-permute-done.3.refs_2_
  19.1 1.2 %collective-permute-done.4.refs_3_ = bf16[32,1536]{1,0:T(8,128)(2,1)S(1)} collective-permute-done((bf16[32,1536]{1,0:T(8,128)(2,1)S(1)}, bf16[32,1536]{1,0:T(8,128)(2,1)S(1)}, u32[]{:S(2)}, u32[]{:S(2)}) %collective-permute-start.4) | collective-permute-done | bytes 98336 | tf_op jit(solution)/shard_map/ppermute | solution.py:215
  20.3 1.7 %copy-done.3 = bf16[1536,768]{1,0:T(8,128)(2,1)S(1)} copy-done((bf16[1536,768]{1,0:T(8,128)(2,1)S(1)}, bf16[1536,768]{1,0:T(8,128)(2,1)}, u32[]{:S(2)}) %copy-start.3) | copy-done | bytes 2359320
  22.0 2.8 %query.1 = bf16[16,144,128]{2,1,0:T(8,128)(2,1)} custom-call(s32[3]{0:T(128)S(1)} %pad_add_fusion.place_ref, bf16[32,1536]{1,0:T(8,128)(2,1)S(1)} %constant_dynamic-update-slice_fusion.refs_0_, bf16[32,1536]{1,0:T(8,128)(2,1)S(1)} %collective-permute-done.2.refs_1_, bf16[32,1536]{1,0:T(8,128)(2,1)S(1)} %collective-permute-done.3.refs_2_, ...), custom_call_target="tpu_custom_call" | custom-call | tf_op jit(solution)/shard_map/query/pallas_call | solution.py:248
  24.8 3.9 %all-to-all-start = ((bf16[16,144,128]{2,1,0:T(8,128)(2,1)}), bf16[16,144,128]{2,1,0:T(8,128)(2,1)S(1)}, u32[]{:S(2)}, u32[]{:S(2)}) async-start(bf16[16,144,128]{2,1,0:T(8,128)(2,1)} %query.1), calls=%async_computation | async-start | bytes 1179648 | tf_op jit(solution)/shard_map/all_to_all | solution.py:256
  28.7 0.0 copy-start.4
  28.7 0.1 fusion
  28.9 0.1 maximum_bitcast_fusion
  29.0 0.1 broadcast_in_dim.22
  29.0 0.1 broadcast_in_dim.25
  29.1 14.9 %all-to-all-done.q_ref = bf16[16,144,128]{2,1,0:T(8,128)(2,1)S(1)} async-done(((bf16[16,144,128]{2,1,0:T(8,128)(2,1)}), bf16[16,144,128]{2,1,0:T(8,128)(2,1)S(1)}, u32[]{:S(2)}, u32[]{:S(2)}) %all-to-all-start) | async-done | bytes 589856 | tf_op jit(solution)/shard_map/all_to_all | solution.py:256
  44.1 3.2 %attend.1 = bf16[16,32,512]{2,1,0:T(8,128)(2,1)S(1)} custom-call(s32[2]{0:T(128)S(1)} %copy-done.6, s32[2]{0:T(128)S(1)} %copy-done.7, bf16[16,144,128]{2,1,0:T(8,128)(2,1)S(1)} %all-to-all-done.q_ref, f32[1,16,128]{2,1,0:T(8,128)S(1)} %bitcast.18, f32[1,16,128]{2,1,0:T(8,128)S(1)} %bitcast.19, bf16[8,576]{1,0:T(8,128)(2,1)S(1)} %copy-done.5, ...), custom_call_target="tpu_custom_call" | custom-call | tf_op jit(solution)/shard_map/attend/pallas_call | solution.py:277
  47.3 18.6 %all_to_all.15.latent_ref = bf16[16,32,512]{2,1,0:T(8,128)(2,1)S(1)} all-to-all(bf16[16,32,512]{2,1,0:T(8,128)(2,1)S(1)} %attend.1), channel_id=1, replica_groups=mesh['groups'=1,'tensor'=16,'replica'=2] {'tensor'}, dimensions={0} | all-to-all | bytes 1048576 | tf_op jit(solution)/shard_map/all_to_all | solution.py:285
  65.8 1.0 values.1.refs_0_
  66.9 1.6 %collective-permute-start.6 = (bf16[128,512]{1,0:T(8,128)(2,1)S(1)}, bf16[128,512]{1,0:T(8,128)(2,1)S(1)}, u32[]{:S(2)}, u32[]{:S(2)}) collective-permute-start(bf16[128,512]{1,0:T(8,128)(2,1)S(1)} %values.1.refs_0_), channel_id=1, source_target_pairs={{0,1},{1,0},{2,3},{3,2},{4,5},{5,4},{6,7},{7,6},{8,9},{9,8},{10,11... | collective-permute-start | bytes 393224 | tf_op jit(solution)/shard_map/ppermute | solution.py:215
  68.4 4.0 %collective-permute-done.6.refs_1_ = bf16[128,512]{1,0:T(8,128)(2,1)S(1)} collective-permute-done((bf16[128,512]{1,0:T(8,128)(2,1)S(1)}, bf16[128,512]{1,0:T(8,128)(2,1)S(1)}, u32[]{:S(2)}, u32[]{:S(2)}) %collective-permute-start.6) | collective-permute-done | bytes 131104 | tf_op jit(solution)/shard_map/ppermute | solution.py:215
  72.5 1.5 %shard_map.101.refs_5_ = bf16[512,1792]{1,0:T(8,128)(2,1)S(1)} custom-call(bf16[512,1792]{1,0:T(8,128)(2,1)} %collective-permute-done.5.refs_0_), custom_call_target="tpu_custom_call" | custom-call | bytes 3670016 | tf_op jit(solution)/shard_map/pallas_call | solution.py:63
  74.0 1.7 %output.1 = bf16[2,128,1792]{2,1,0:T(8,128)(2,1)S(1)} custom-call(s32[3]{0:T(128)S(1)} %pad_add_fusion.place_ref, bf16[128,512]{1,0:T(8,128)(2,1)S(1)} %values.1.refs_0_, bf16[128,512]{1,0:T(8,128)(2,1)S(1)} %collective-permute-done.6.refs_1_, bf16[128,512]{1,0:T(8,128)(2,1)S(1)} %collective-permute-done.7.refs_2_, ...), custom_call_target="tpu_custom_call" | custom-call | tf_op jit(solution)/shard_map/output/pallas_call | solution.py:300
  75.7 28.5 %all_to_all.16.x_ref = bf16[32,8,1792]{2,1,0:T(8,128)(2,1)S(1)} all-to-all(bf16[32,8,1792]{2,1,0:T(8,128)(2,1)S(1)} %bitcast.16), channel_id=1, replica_groups=mesh['groups'=1,'tensor'=16,'replica'=2] {'replica','tensor'}, dimensions={0} | all-to-all | bytes 1835008 | tf_op jit(solution)/shard_map/all_to_all | solution.py:309
  104.2 0.8 combine.1
  (27 shorter events, 0.1 us)
Async XLA Ops:
  0.0 10.1 %collective-permute-start = (bf16[8,1536]{1,0:T(8,128)(2,1)}, bf16[8,1536]{1,0:T(8,128)(2,1)S(1)}, u32[]{:S(2)}, u32[]{:S(2)}) collective-permute-start(bf16[8,1536]{1,0:T(8,128)(2,1)} %refs_3_.1), channel_id=1, source_target_pairs={{0,16},{2,18},{4,20},{6,22},{8,24},{10,26},{12,28},{14,30},{16,0},... | collective-permute-start | bytes 73736 | tf_op jit(solution)/shard_map/ppermute | solution.py:215
  6.9 37.2 %collective-permute-start.5 = (bf16[512,1792]{1,0:T(8,128)(2,1)}, bf16[512,1792]{1,0:T(8,128)(2,1)}, u32[]{:S(2)}, u32[]{:S(2)}) collective-permute-start(bf16[512,1792]{1,0:T(8,128)(2,1)} %constant_dynamic-slice_fusion), channel_id=1, source_target_pairs={{0,2},{2,0},{4,6},{6,4},{8,10},{10,8},{12,14},{14,12},{16,18},{18,... | collective-permute-start | bytes 5505032 | tf_op jit(solution)/shard_map/ppermute | solution.py:215
  8.7 1.4 %copy-start.2 = (bf16[1536,768]{1,0:T(8,128)(2,1)}, bf16[1536,768]{1,0:T(8,128)(2,1)S(1)}, u32[]{:S(2)}) copy-start(bf16[1536,768]{1,0:T(8,128)(2,1)S(1)} %get-tuple-element.23.refs_5_) | copy-start | bytes 7077892
  10.2 4.2 %collective-permute-start.1 = (bf16[16,1536]{1,0:T(8,128)(2,1)S(1)}, bf16[16,1536]{1,0:T(8,128)(2,1)S(1)}, u32[]{:S(2)}, u32[]{:S(2)}) collective-permute-start(bf16[16,1536]{1,0:T(8,128)(2,1)S(1)} %pad_maximum_fusion), channel_id=1, source_target_pairs={{0,8},{2,10},{4,12},{6,14},{8,0},{10,2},{12,4},{14,6},{16,24},{18,... | collective-permute-start | bytes 147464 | tf_op jit(solution)/shard_map/ppermute | solution.py:215
  14.4 4.6 %collective-permute-start.2 = (bf16[32,1536]{1,0:T(8,128)(2,1)S(1)}, bf16[32,1536]{1,0:T(8,128)(2,1)S(1)}, u32[]{:S(2)}, u32[]{:S(2)}) collective-permute-start(bf16[32,1536]{1,0:T(8,128)(2,1)S(1)} %constant_dynamic-update-slice_fusion.refs_0_), channel_id=1, source_target_pairs={{0,4},{2,6},{4,0},{6,2},{8,12},{10,14},{12,8},{14,10},{16,20},{18,... | collective-permute-start | bytes 294920 | tf_op jit(solution)/shard_map/ppermute | solution.py:215
  15.9 3.2 %collective-permute-start.3 = (bf16[32,1536]{1,0:T(8,128)(2,1)S(1)}, bf16[32,1536]{1,0:T(8,128)(2,1)S(1)}, u32[]{:S(2)}, u32[]{:S(2)}) collective-permute-start(bf16[32,1536]{1,0:T(8,128)(2,1)S(1)} %constant_dynamic-update-slice_fusion.refs_0_), channel_id=1, source_target_pairs={{0,2},{2,0},{4,6},{6,4},{8,10},{10,8},{12,14},{14,12},{16,18},{18,... | collective-permute-start | bytes 294920 | tf_op jit(solution)/shard_map/ppermute | solution.py:215
  19.0 1.3 %collective-permute-start.4 = (bf16[32,1536]{1,0:T(8,128)(2,1)S(1)}, bf16[32,1536]{1,0:T(8,128)(2,1)S(1)}, u32[]{:S(2)}, u32[]{:S(2)}) collective-permute-start(bf16[32,1536]{1,0:T(8,128)(2,1)S(1)} %collective-permute-done.2.refs_1_), channel_id=1, source_target_pairs={{0,2},{2,0},{4,6},{6,4},{8,10},{10,8},{12,14},{14,12},{16,18},{18,... | collective-permute-start | bytes 294920 | tf_op jit(solution)/shard_map/ppermute | solution.py:215
  19.0 9.7 %copy-start.6 = (s32[2]{0:T(128)S(1)}, s32[2]{0:T(128)}, u32[]{:S(2)}) copy-start(s32[2]{0:T(128)} %len_ref.1) | copy-start | bytes 28
  19.0 25.1 %copy-start.7 = (s32[2]{0:T(128)S(1)}, s32[2]{0:T(128)}, u32[]{:S(2)}) copy-start(s32[2]{0:T(128)} %count_ref.1) | copy-start | bytes 28
  19.1 25.0 %copy-start.1 = (bf16[2,1024,576]{1,2,0:T(8,128)(2,1)S(1)}, bf16[2,1024,576]{1,2,0:T(8,128)(2,1)}, u32[]{:S(2)}) copy-start(bf16[2,1024,576]{1,2,0:T(8,128)(2,1)} %param.17) | copy-start | bytes 7077892
  20.3 1.7 %copy-start.3 = (bf16[1536,768]{1,0:T(8,128)(2,1)S(1)}, bf16[1536,768]{1,0:T(8,128)(2,1)}, u32[]{:S(2)}) copy-start(bf16[1536,768]{1,0:T(8,128)(2,1)} %copy-done.2) | copy-start | bytes 7077892
  22.0 22.1 %copy-start.5 = (bf16[8,576]{1,0:T(8,128)(2,1)S(1)}, bf16[8,576]{1,0:T(8,128)(2,1)}, u32[]{:S(2)}) copy-start(bf16[8,576]{1,0:T(8,128)(2,1)} %new_ref.1) | copy-start | bytes 27652
  24.8 19.3 %all-to-all-start = ((bf16[16,144,128]{2,1,0:T(8,128)(2,1)}), bf16[16,144,128]{2,1,0:T(8,128)(2,1)S(1)}, u32[]{:S(2)}, u32[]{:S(2)}) async-start(bf16[16,144,128]{2,1,0:T(8,128)(2,1)} %query.1), calls=%async_computation | async-start | bytes 1179648 | tf_op jit(solution)/shard_map/all_to_all | solution.py:256
  28.7 37.2 %copy-start.4 = (bf16[4,512,128]{2,1,0:T(8,128)(2,1)S(1)}, bf16[4,512,128]{2,1,0:T(8,128)(2,1)}, u32[]{:S(2)}) copy-start(bf16[4,512,128]{2,1,0:T(8,128)(2,1)} %uv_ref.1) | copy-start | bytes 1572868
  65.8 8.2 %copy-start = (bf16[512,3584]{1,0:T(8,128)(2,1)S(1)}, bf16[512,3584]{1,0:T(8,128)(2,1)}, u32[]{:S(2)}) copy-start(bf16[512,3584]{1,0:T(8,128)(2,1)} %refs_4_.1) | copy-start | bytes 11010052
  66.9 5.6 %collective-permute-start.6 = (bf16[128,512]{1,0:T(8,128)(2,1)S(1)}, bf16[128,512]{1,0:T(8,128)(2,1)S(1)}, u32[]{:S(2)}, u32[]{:S(2)}) collective-permute-start(bf16[128,512]{1,0:T(8,128)(2,1)S(1)} %values.1.refs_0_), channel_id=1, source_target_pairs={{0,1},{1,0},{2,3},{3,2},{4,5},{5,4},{6,7},{7,6},{8,9},{9,8},{10,11... | collective-permute-start | bytes 393224 | tf_op jit(solution)/shard_map/ppermute | solution.py:215
  68.4 5.6 %collective-permute-start.7 = (bf16[128,512]{1,0:T(8,128)(2,1)S(1)}, bf16[128,512]{1,0:T(8,128)(2,1)S(1)}, u32[]{:S(2)}, u32[]{:S(2)}) collective-permute-start(bf16[128,512]{1,0:T(8,128)(2,1)S(1)} %values.1.refs_0_), channel_id=1, source_target_pairs={{0,2},{2,0},{4,6},{6,4},{8,10},{10,8},{12,14},{14,12},{16,18},{18,... | collective-permute-start | bytes 393224 | tf_op jit(solution)/shard_map/ppermute | solution.py:215
  72.5 1.5 %collective-permute-start.8 = (bf16[128,512]{1,0:T(8,128)(2,1)S(1)}, bf16[128,512]{1,0:T(8,128)(2,1)S(1)}, u32[]{:S(2)}, u32[]{:S(2)}) collective-permute-start(bf16[128,512]{1,0:T(8,128)(2,1)S(1)} %collective-permute-done.6.refs_1_), channel_id=1, source_target_pairs={{0,2},{2,0},{4,6},{6,4},{8,10},{10,8},{12,14},{14,12},{16,18},{18,... | collective-permute-start | bytes 393224 | tf_op jit(solution)/shard_map/ppermute | solution.py:215

commit v7 on v6

--- a/solution.py
+++ b/solution.py
@@ -73,52 +73,54 @@
     )(*arrays)
 
 
+def regroup(pieces, groups, size):
+    assert groups == 2 and len(pieces) % 2 == 0
+    rows = lax.broadcasted_iota(jnp.int32, pieces[0].shape, 0)
+    low = rest(over(rows, size), 2) == 0
+    total = pieces[0].shape[0]
+    width = pieces[0].shape[1]
+    firsts, seconds = [], []
+    for h in range(0, len(pieces), 2):
+        a, b = pieces[h], pieces[h + 1]
+        firsts.append(jnp.where(low, a, pltpu.roll(b, size, 0)))
+        seconds.append(jnp.where(low, pltpu.roll(a, total - size, 0), b))
+
+    def stack(parts):
+        parts = [part.reshape(total // (2 * size), 2 * size, width) for part in parts]
+        return jnp.concatenate(parts, axis=1).reshape(total * len(parts), width)
+
+    return [stack(firsts), stack(seconds)]
+
+
 def query_kernel(reqs, drafts, heads, place_ref, *refs):
     *x_refs, gain_ref, up_ref, uk_ref, out_ref = refs
     owners = out_ref.shape[0]
-    rows_dev = reqs * drafts
     hd = heads * drafts
     x = jnp.concatenate([x_ref[...] for x_ref in x_refs], axis=0).astype(f32)
     scaled = x * lax.rsqrt(jnp.mean(x * x, axis=-1, keepdims=True) + rms_eps)
     normed = (scaled * gain_ref[...][None, :]).astype(bf16)
     full = mm(normed, up_ref[...]).astype(bf16)
-    count = owners * reqs * hd
-    shape = (count, owners * rows_dev)
-    n = lax.broadcasted_iota(jnp.int32, shape, 0)
-    m = lax.broadcasted_iota(jnp.int32, shape, 1)
-    target = over(n, reqs * hd)
-    local = rest(over(n, hd), reqs) * drafts + rest(n, drafts)
-    block = over(m, rows_dev)
-    distance = jnp.zeros_like(block)
-    bit = owners // 2
-    while bit:
-        distance = distance + (block & 1) * bit
-        block = block >> 1
-        bit //= 2
-    spread = jnp.where((target == (distance ^ place_ref[2])) & (local == rest(m, rows_dev)), 1.0, 0.0)
-    wide = mm(spread.astype(bf16), full)
-    row_head = rest(over(lax.broadcasted_iota(jnp.int32, (count, 1), 0), drafts), heads)
-    absorbed = None
-    rope = None
-    for h in range(heads):
-        mine = row_head == h
-        nope_h = jnp.where(mine, wide[:, h * QKD : h * QKD + NOPE], 0.0).astype(bf16)
-        part = mm(nope_h, uk_ref[h * NOPE : (h + 1) * NOPE])
-        absorbed = part if absorbed is None else absorbed + part
-        rope_h = jnp.where(mine, wide[:, h * QKD + NOPE : (h + 1) * QKD], 0.0)
-        rope = rope_h if rope is None else rope + rope_h
+    absorbed = [mm(full[:, h * QKD : h * QKD + NOPE], uk_ref[h * NOPE : (h + 1) * NOPE]) for h in range(heads)]
+    rope = [full[:, h * QKD + NOPE : (h + 1) * QKD].astype(f32) for h in range(heads)]
+    absorbed = regroup(absorbed, reqs, drafts)
+    rope = regroup(rope, reqs, drafts)
     chunks = LATENT // LANES
-    absorbed = absorbed.reshape(owners, reqs, hd, LATENT)
-    rope = rope.reshape(owners, reqs, hd, ROPE)
-    for q in range(reqs):
-        for c in range(chunks):
-            at = (q * chunks + c) * hd
-            out_ref[:, at : at + hd, :] = absorbed[:, q, :, c * LANES : (c + 1) * LANES].astype(bf16)
     per = LANES // ROPE
-    for b in range(reqs // per):
-        at = (reqs * chunks + b) * hd
-        both = jnp.concatenate([rope[:, b * per + i] for i in range(per)], axis=-1)
-        out_ref[:, at : at + hd, :] = both.astype(bf16)
+    absorbed = [x.reshape(owners, hd, LATENT).astype(bf16) for x in absorbed]
+    rope = [
+        jnp.concatenate(rope[b * per : (b + 1) * per], axis=-1).reshape(owners, hd, LANES).astype(bf16)
+        for b in range(reqs // per)
+    ]
+    for k in range(owners):
+        distance = int(format(k, f"0{owners.bit_length() - 1}b")[::-1], 2)
+        target = place_ref[2] ^ distance
+        for q in range(reqs):
+            for c in range(chunks):
+                at = (q * chunks + c) * hd
+                out_ref[target, at : at + hd, :] = absorbed[q][k, :, c * LANES : (c + 1) * LANES]
+        for b in range(reqs // per):
+            at = (reqs * chunks + b) * hd
+            out_ref[target, at : at + hd, :] = rope[b][k]
 
 
 def attend_kernel(reqs, drafts, heads, len_ref, count_ref, q_ref, cos_ref, sin_ref, new_ref, cache_ref, out_ref):
@@ -170,19 +172,19 @@
         out_ref[:, q * hd : (q + 1) * hd, :] = mix.reshape(owners, hd, LATENT)
 
 
-def value_kernel(reqs, drafts, heads, latent_ref, uv_ref, out_ref):
+def value_kernel(drafts, heads, latent_ref, uv_ref, out_ref):
     owners = latent_ref.shape[0]
     hd = heads * drafts
-    rows = owners * reqs * drafts
-    latent = latent_ref[...].reshape(owners * reqs * hd, LATENT)
-    shape = (rows, owners * reqs * hd)
-    m = lax.broadcasted_iota(jnp.int32, shape, 0)
-    n = lax.broadcasted_iota(jnp.int32, shape, 1)
-    wanted = over(m, drafts) * hd + rest(m, drafts)
-    for h in range(heads):
-        pick = jnp.where(n == wanted + h * drafts, 1.0, 0.0).astype(bf16)
-        mine = mm(pick, latent).astype(bf16)
-        out_ref[:, h * VDIM : (h + 1) * VDIM] = mm(mine, uv_ref[h]).astype(bf16)
+    pair = 2 * drafts
+    rows = owners * pair
+    low = rest(over(lax.broadcasted_iota(jnp.int32, (rows, LATENT), 0), drafts), 2) == 0
+    for h in range(0, heads, 2):
+        a = latent_ref[:, h * drafts : h * drafts + pair, :].astype(f32).reshape(rows, LATENT)
+        b = latent_ref[:, hd + h * drafts : hd + h * drafts + pair, :].astype(f32).reshape(rows, LATENT)
+        first = jnp.where(low, a, pltpu.roll(b, drafts, 0)).astype(bf16)
+        second = jnp.where(low, pltpu.roll(a, rows - drafts, 0), b).astype(bf16)
+        out_ref[:, h * VDIM : (h + 1) * VDIM] = mm(first, uv_ref[h]).astype(bf16)
+        out_ref[:, (h + 1) * VDIM : (h + 2) * VDIM] = mm(second, uv_ref[h + 1]).astype(bf16)
 
 
 def output_kernel(place_ref, *refs):
@@ -285,7 +287,7 @@
     returned = lax.all_to_all(latent, "tensor", split_axis=0, concat_axis=0, tiled=True)
 
     values = pl.pallas_call(
-        functools.partial(value_kernel, reqs, drafts, heads),
+        functools.partial(value_kernel, drafts, heads),
         out_shape=jax.ShapeDtypeStruct((owners * rows_dev, heads * VDIM), bf16),
         in_specs=[vmem_spec()] * 2,
         out_specs=vmem_spec(),

time: 105 us -> 104 us (level)
  Pallas kernels: 12.7 us -> 11.6 us
  transfers between devices with their start and end apart: 10 -> 10, of which waited for: 5 -> 5; matrix products, arithmetic and copies ran while one was open for 3% -> 3% of each run, Pallas kernels for 6% -> 5%
where the time goes in v7:
time: 104 us
  blocking collectives  47.1 us (45%)
  waiting for transfers between devices  25.9 us (25%)
  starting transfers between devices  12.7 us (12%)
  Pallas kernels  11.6 us (11%)
  local copies, waits for them, and re-layouts  6.14 us (6%)
    all_to_all x1, blocking collectives, local_step(): lax.all_to_all(product, ('replica', 'tensor'), split_axis=0, concat_axis=...  28.5 us
    all_to_all x1, blocking collectives, local_step(): lax.all_to_all(latent, 'tensor', split_axis=0, concat_axis=0, tiled=True)  18.6 us
    all_to_all x1, waiting for transfers between devices, local_step(): lax.all_to_all(queries, 'tensor', split_axis=0, concat_axis=0, tiled=True)  14.9 us
    ppermute x9, waiting for transfers between devices, step(): return lax.ppermute(x, axis, [(i, i ^ k) for i in range(size)])  11 us
    ppermute x9, starting transfers between devices, step(): return lax.ppermute(x, axis, [(i, i ^ k) for i in range(size)])  8.77 us
    all_to_all x1, starting transfers between devices, local_step(): lax.all_to_all(queries, 'tensor', split_axis=0, concat_axis=0, tiled=True)  3.91 us
    pallas_call x2, Pallas kernels, fetch(): pl.pallas_call(fetch_kernel, out_shape=[pltpu.VMEM(x.shape, x.dtype) for...  3.3 us
    pallas_call x1, Pallas kernels, local_step(): pl.pallas_call(functools.partial(attend_kernel, reqs, drafts, heads), out...  3.16 us
  transfers between devices with their start and end apart: 10, of which 5 were waited for; matrix products, arithmetic and copies ran while one was open for 3% of the time, Pallas kernels for 5%

profile of v7, /device:TPU:0, one launch (start us, length us, event | category | flops | bytes accessed | tf_op | source)
XLA Modules:
  0.0 103.9 jit_solution(10488686640850059219)
XLA Ops:
  0.0 4.1 %collective-permute-start = (bf16[8,1536]{1,0:T(8,128)(2,1)}, bf16[8,1536]{1,0:T(8,128)(2,1)S(1)}, u32[]{:S(2)}, u32[]{:S(2)}) collective-permute-start(bf16[8,1536]{1,0:T(8,128)(2,1)} %refs_3_.1), channel_id=1, source_target_pairs={{0,16},{2,18},{4,20},{6,22},{8,24},{10,26},{12,28},{14,30},{16,0},... | collective-permute-start | bytes 73736 | tf_op jit(solution)/shard_map/ppermute | solution.py:217
  4.1 2.8 %constant_dynamic-slice_fusion = bf16[512,1792]{1,0:T(8,128)(2,1)} fusion(bf16[512,3584]{1,0:T(8,128)(2,1)} %refs_4_.1, s32[]{:T(128)S(6)} %select_n.11), kind=kLoop, calls=%fused_computation.11 | loop fusion | bytes 3670020 | tf_op jit(solution)/shard_map/dynamic_slice | solution.py:261
  6.9 0.0 collective-permute-start.5
  6.9 1.8 %shard_map.100 = (bf16[1536,768]{1,0:T(8,128)(2,1)S(1)}, bf16[512,512]{1,0:T(8,128)(2,1)S(1)}, f32[1536]{0:T(1024)S(1)}, bf16[8,1536]{1,0:T(8,128)(2,1)S(1)}) custom-call(bf16[1536,768]{1,0:T(8,128)(2,1)} %refs_0_.1, bf16[512,512]{1,0:T(8,128)(2,1)} %bitcast.20, f32[1536]{0:T(1024)} %refs_2_.1, bf16[8,1536]{1,0:T(8,128)(2,1)} %refs_3_.1), custom_call_target="tpu_custom_call" | custom-call | bytes 5822464 | tf_op jit(solution)/shard_map/pallas_call | solution.py:63
  8.7 1.4 %copy-done.2 = bf16[1536,768]{1,0:T(8,128)(2,1)} copy-done((bf16[1536,768]{1,0:T(8,128)(2,1)}, bf16[1536,768]{1,0:T(8,128)(2,1)S(1)}, u32[]{:S(2)}) %copy-start.2) | copy-done | bytes 2359320
  10.1 0.0 collective-permute-done
  10.2 1.6 %collective-permute-start.1 = (bf16[16,1536]{1,0:T(8,128)(2,1)S(1)}, bf16[16,1536]{1,0:T(8,128)(2,1)S(1)}, u32[]{:S(2)}, u32[]{:S(2)}) collective-permute-start(bf16[16,1536]{1,0:T(8,128)(2,1)S(1)} %pad_maximum_fusion), channel_id=1, source_target_pairs={{0,8},{2,10},{4,12},{6,14},{8,0},{10,2},{12,4},{14,6},{16,24},{18,... | collective-permute-start | bytes 147464 | tf_op jit(solution)/shard_map/ppermute | solution.py:217
  11.8 2.6 %collective-permute-done.1 = bf16[16,1536]{1,0:T(8,128)(2,1)S(1)} collective-permute-done((bf16[16,1536]{1,0:T(8,128)(2,1)S(1)}, bf16[16,1536]{1,0:T(8,128)(2,1)S(1)}, u32[]{:S(2)}, u32[]{:S(2)}) %collective-permute-start.1) | collective-permute-done | bytes 49184 | tf_op jit(solution)/shard_map/ppermute | solution.py:217
  14.4 1.5 %collective-permute-start.2 = (bf16[32,1536]{1,0:T(8,128)(2,1)S(1)}, bf16[32,1536]{1,0:T(8,128)(2,1)S(1)}, u32[]{:S(2)}, u32[]{:S(2)}) collective-permute-start(bf16[32,1536]{1,0:T(8,128)(2,1)S(1)} %constant_dynamic-update-slice_fusion.refs_0_), channel_id=1, source_target_pairs={{0,4},{2,6},{4,0},{6,2},{8,12},{10,14},{12,8},{14,10},{16,20},{18,... | collective-permute-start | bytes 294920 | tf_op jit(solution)/shard_map/ppermute | solution.py:217
  15.9 3.1 %collective-permute-done.2.refs_1_ = bf16[32,1536]{1,0:T(8,128)(2,1)S(1)} collective-permute-done((bf16[32,1536]{1,0:T(8,128)(2,1)S(1)}, bf16[32,1536]{1,0:T(8,128)(2,1)S(1)}, u32[]{:S(2)}, u32[]{:S(2)}) %collective-permute-start.2) | collective-permute-done | bytes 98336 | tf_op jit(solution)/shard_map/ppermute | solution.py:217
  19.0 0.0 collective-permute-start.4
  19.0 0.1 pad_add_fusion.place_ref
  19.1 0.0 collective-permute-done.3.refs_2_
  19.1 1.2 %collective-permute-done.4.refs_3_ = bf16[32,1536]{1,0:T(8,128)(2,1)S(1)} collective-permute-done((bf16[32,1536]{1,0:T(8,128)(2,1)S(1)}, bf16[32,1536]{1,0:T(8,128)(2,1)S(1)}, u32[]{:S(2)}, u32[]{:S(2)}) %collective-permute-start.4) | collective-permute-done | bytes 98336 | tf_op jit(solution)/shard_map/ppermute | solution.py:217
  20.3 1.7 %copy-done.3 = bf16[1536,768]{1,0:T(8,128)(2,1)S(1)} copy-done((bf16[1536,768]{1,0:T(8,128)(2,1)S(1)}, bf16[1536,768]{1,0:T(8,128)(2,1)}, u32[]{:S(2)}) %copy-start.3) | copy-done | bytes 2359320
  22.0 2.3 %query.1 = bf16[16,144,128]{2,1,0:T(8,128)(2,1)} custom-call(s32[3]{0:T(128)S(1)} %pad_add_fusion.place_ref, bf16[32,1536]{1,0:T(8,128)(2,1)S(1)} %constant_dynamic-update-slice_fusion.refs_0_, bf16[32,1536]{1,0:T(8,128)(2,1)S(1)} %collective-permute-done.2.refs_1_, bf16[32,1536]{1,0:T(8,128)(2,1)S(1)} %collective-permute-done.3.refs_2_, ...), custom_call_target="tpu_custom_call" | custom-call | tf_op jit(solution)/shard_map/query/pallas_call | solution.py:250
  24.3 3.9 %all-to-all-start = ((bf16[16,144,128]{2,1,0:T(8,128)(2,1)}), bf16[16,144,128]{2,1,0:T(8,128)(2,1)S(1)}, u32[]{:S(2)}, u32[]{:S(2)}) async-start(bf16[16,144,128]{2,1,0:T(8,128)(2,1)} %query.1), calls=%async_computation | async-start | bytes 1179648 | tf_op jit(solution)/shard_map/all_to_all | solution.py:258
  28.2 0.0 copy-start.4
  28.3 0.1 fusion
  28.4 0.1 maximum_bitcast_fusion
  28.5 0.1 broadcast_in_dim.22
  28.6 0.1 broadcast_in_dim.25
  28.7 14.9 %all-to-all-done.q_ref = bf16[16,144,128]{2,1,0:T(8,128)(2,1)S(1)} async-done(((bf16[16,144,128]{2,1,0:T(8,128)(2,1)}), bf16[16,144,128]{2,1,0:T(8,128)(2,1)S(1)}, u32[]{:S(2)}, u32[]{:S(2)}) %all-to-all-start) | async-done | bytes 589856 | tf_op jit(solution)/shard_map/all_to_all | solution.py:258
  43.6 3.2 %attend.1 = bf16[16,32,512]{2,1,0:T(8,128)(2,1)S(1)} custom-call(s32[2]{0:T(128)S(1)} %copy-done.6, s32[2]{0:T(128)S(1)} %copy-done.7, bf16[16,144,128]{2,1,0:T(8,128)(2,1)S(1)} %all-to-all-done.q_ref, f32[1,16,128]{2,1,0:T(8,128)S(1)} %bitcast.18, f32[1,16,128]{2,1,0:T(8,128)S(1)} %bitcast.19, bf16[8,576]{1,0:T(8,128)(2,1)S(1)} %copy-done.5, ...), custom_call_target="tpu_custom_call" | custom-call | tf_op jit(solution)/shard_map/attend/pallas_call | solution.py:279
  46.8 18.6 %all_to_all.15.latent_ref = bf16[16,32,512]{2,1,0:T(8,128)(2,1)S(1)} all-to-all(bf16[16,32,512]{2,1,0:T(8,128)(2,1)S(1)} %attend.1), channel_id=1, replica_groups=mesh['groups'=1,'tensor'=16,'replica'=2] {'tensor'}, dimensions={0} | all-to-all | bytes 1048576 | tf_op jit(solution)/shard_map/all_to_all | solution.py:287
  65.4 0.3 values.1.refs_0_
  65.7 1.5 %collective-permute-start.6 = (bf16[128,512]{1,0:T(8,128)(2,1)S(1)}, bf16[128,512]{1,0:T(8,128)(2,1)S(1)}, u32[]{:S(2)}, u32[]{:S(2)}) collective-permute-start(bf16[128,512]{1,0:T(8,128)(2,1)S(1)} %values.1.refs_0_), channel_id=1, source_target_pairs={{0,1},{1,0},{2,3},{3,2},{4,5},{5,4},{6,7},{7,6},{8,9},{9,8},{10,11... | collective-permute-start | bytes 393224 | tf_op jit(solution)/shard_map/ppermute | solution.py:217
  67.3 4.1 %collective-permute-done.6.refs_1_ = bf16[128,512]{1,0:T(8,128)(2,1)S(1)} collective-permute-done((bf16[128,512]{1,0:T(8,128)(2,1)S(1)}, bf16[128,512]{1,0:T(8,128)(2,1)S(1)}, u32[]{:S(2)}, u32[]{:S(2)}) %collective-permute-start.6) | collective-permute-done | bytes 131104 | tf_op jit(solution)/shard_map/ppermute | solution.py:217
  71.3 1.5 %shard_map.101.refs_5_ = bf16[512,1792]{1,0:T(8,128)(2,1)S(1)} custom-call(bf16[512,1792]{1,0:T(8,128)(2,1)} %collective-permute-done.5.refs_0_), custom_call_target="tpu_custom_call" | custom-call | bytes 3670016 | tf_op jit(solution)/shard_map/pallas_call | solution.py:63
  72.9 1.7 %output.1 = bf16[2,128,1792]{2,1,0:T(8,128)(2,1)S(1)} custom-call(s32[3]{0:T(128)S(1)} %pad_add_fusion.place_ref, bf16[128,512]{1,0:T(8,128)(2,1)S(1)} %values.1.refs_0_, bf16[128,512]{1,0:T(8,128)(2,1)S(1)} %collective-permute-done.6.refs_1_, bf16[128,512]{1,0:T(8,128)(2,1)S(1)} %collective-permute-done.7.refs_2_, ...), custom_call_target="tpu_custom_call" | custom-call | tf_op jit(solution)/shard_map/output/pallas_call | solution.py:302
  74.6 28.5 %all_to_all.16.x_ref = bf16[32,8,1792]{2,1,0:T(8,128)(2,1)S(1)} all-to-all(bf16[32,8,1792]{2,1,0:T(8,128)(2,1)S(1)} %bitcast.16), channel_id=1, replica_groups=mesh['groups'=1,'tensor'=16,'replica'=2] {'replica','tensor'}, dimensions={0} | all-to-all | bytes 1835008 | tf_op jit(solution)/shard_map/all_to_all | solution.py:311
  103.1 0.8 combine.1
  (27 shorter events, 0.1 us)
Async XLA Ops:
  0.0 10.1 %collective-permute-start = (bf16[8,1536]{1,0:T(8,128)(2,1)}, bf16[8,1536]{1,0:T(8,128)(2,1)S(1)}, u32[]{:S(2)}, u32[]{:S(2)}) collective-permute-start(bf16[8,1536]{1,0:T(8,128)(2,1)} %refs_3_.1), channel_id=1, source_target_pairs={{0,16},{2,18},{4,20},{6,22},{8,24},{10,26},{12,28},{14,30},{16,0},... | collective-permute-start | bytes 73736 | tf_op jit(solution)/shard_map/ppermute | solution.py:217
  6.9 36.7 %collective-permute-start.5 = (bf16[512,1792]{1,0:T(8,128)(2,1)}, bf16[512,1792]{1,0:T(8,128)(2,1)}, u32[]{:S(2)}, u32[]{:S(2)}) collective-permute-start(bf16[512,1792]{1,0:T(8,128)(2,1)} %constant_dynamic-slice_fusion), channel_id=1, source_target_pairs={{0,2},{2,0},{4,6},{6,4},{8,10},{10,8},{12,14},{14,12},{16,18},{18,... | collective-permute-start | bytes 5505032 | tf_op jit(solution)/shard_map/ppermute | solution.py:217
  8.7 1.4 %copy-start.2 = (bf16[1536,768]{1,0:T(8,128)(2,1)}, bf16[1536,768]{1,0:T(8,128)(2,1)S(1)}, u32[]{:S(2)}) copy-start(bf16[1536,768]{1,0:T(8,128)(2,1)S(1)} %get-tuple-element.23.refs_5_) | copy-start | bytes 7077892
  10.2 4.2 %collective-permute-start.1 = (bf16[16,1536]{1,0:T(8,128)(2,1)S(1)}, bf16[16,1536]{1,0:T(8,128)(2,1)S(1)}, u32[]{:S(2)}, u32[]{:S(2)}) collective-permute-start(bf16[16,1536]{1,0:T(8,128)(2,1)S(1)} %pad_maximum_fusion), channel_id=1, source_target_pairs={{0,8},{2,10},{4,12},{6,14},{8,0},{10,2},{12,4},{14,6},{16,24},{18,... | collective-permute-start | bytes 147464 | tf_op jit(solution)/shard_map/ppermute | solution.py:217
  14.4 4.6 %collective-permute-start.2 = (bf16[32,1536]{1,0:T(8,128)(2,1)S(1)}, bf16[32,1536]{1,0:T(8,128)(2,1)S(1)}, u32[]{:S(2)}, u32[]{:S(2)}) collective-permute-start(bf16[32,1536]{1,0:T(8,128)(2,1)S(1)} %constant_dynamic-update-slice_fusion.refs_0_), channel_id=1, source_target_pairs={{0,4},{2,6},{4,0},{6,2},{8,12},{10,14},{12,8},{14,10},{16,20},{18,... | collective-permute-start | bytes 294920 | tf_op jit(solution)/shard_map/ppermute | solution.py:217
  15.9 3.2 %collective-permute-start.3 = (bf16[32,1536]{1,0:T(8,128)(2,1)S(1)}, bf16[32,1536]{1,0:T(8,128)(2,1)S(1)}, u32[]{:S(2)}, u32[]{:S(2)}) collective-permute-start(bf16[32,1536]{1,0:T(8,128)(2,1)S(1)} %constant_dynamic-update-slice_fusion.refs_0_), channel_id=1, source_target_pairs={{0,2},{2,0},{4,6},{6,4},{8,10},{10,8},{12,14},{14,12},{16,18},{18,... | collective-permute-start | bytes 294920 | tf_op jit(solution)/shard_map/ppermute | solution.py:217
  19.0 1.3 %collective-permute-start.4 = (bf16[32,1536]{1,0:T(8,128)(2,1)S(1)}, bf16[32,1536]{1,0:T(8,128)(2,1)S(1)}, u32[]{:S(2)}, u32[]{:S(2)}) collective-permute-start(bf16[32,1536]{1,0:T(8,128)(2,1)S(1)} %collective-permute-done.2.refs_1_), channel_id=1, source_target_pairs={{0,2},{2,0},{4,6},{6,4},{8,10},{10,8},{12,14},{14,12},{16,18},{18,... | collective-permute-start | bytes 294920 | tf_op jit(solution)/shard_map/ppermute | solution.py:217
  19.0 9.2 %copy-start.6 = (s32[2]{0:T(128)S(1)}, s32[2]{0:T(128)}, u32[]{:S(2)}) copy-start(s32[2]{0:T(128)} %len_ref.1) | copy-start | bytes 28
  19.0 24.6 %copy-start.7 = (s32[2]{0:T(128)S(1)}, s32[2]{0:T(128)}, u32[]{:S(2)}) copy-start(s32[2]{0:T(128)} %count_ref.1) | copy-start | bytes 28
  19.1 24.5 %copy-start.1 = (bf16[2,1024,576]{1,2,0:T(8,128)(2,1)S(1)}, bf16[2,1024,576]{1,2,0:T(8,128)(2,1)}, u32[]{:S(2)}) copy-start(bf16[2,1024,576]{1,2,0:T(8,128)(2,1)} %param.17) | copy-start | bytes 7077892
  20.3 1.7 %copy-start.3 = (bf16[1536,768]{1,0:T(8,128)(2,1)S(1)}, bf16[1536,768]{1,0:T(8,128)(2,1)}, u32[]{:S(2)}) copy-start(bf16[1536,768]{1,0:T(8,128)(2,1)} %copy-done.2) | copy-start | bytes 7077892
  22.0 21.7 %copy-start.5 = (bf16[8,576]{1,0:T(8,128)(2,1)S(1)}, bf16[8,576]{1,0:T(8,128)(2,1)}, u32[]{:S(2)}) copy-start(bf16[8,576]{1,0:T(8,128)(2,1)} %new_ref.1) | copy-start | bytes 27652
  24.3 19.3 %all-to-all-start = ((bf16[16,144,128]{2,1,0:T(8,128)(2,1)}), bf16[16,144,128]{2,1,0:T(8,128)(2,1)S(1)}, u32[]{:S(2)}, u32[]{:S(2)}) async-start(bf16[16,144,128]{2,1,0:T(8,128)(2,1)} %query.1), calls=%async_computation | async-start | bytes 1179648 | tf_op jit(solution)/shard_map/all_to_all | solution.py:258
  28.2 37.2 %copy-start.4 = (bf16[4,512,128]{2,1,0:T(8,128)(2,1)S(1)}, bf16[4,512,128]{2,1,0:T(8,128)(2,1)}, u32[]{:S(2)}) copy-start(bf16[4,512,128]{2,1,0:T(8,128)(2,1)} %uv_ref.1) | copy-start | bytes 1572868
  65.4 7.5 %copy-start = (bf16[512,3584]{1,0:T(8,128)(2,1)S(1)}, bf16[512,3584]{1,0:T(8,128)(2,1)}, u32[]{:S(2)}) copy-start(bf16[512,3584]{1,0:T(8,128)(2,1)} %refs_4_.1) | copy-start | bytes 11010052
  65.7 5.6 %collective-permute-start.6 = (bf16[128,512]{1,0:T(8,128)(2,1)S(1)}, bf16[128,512]{1,0:T(8,128)(2,1)S(1)}, u32[]{:S(2)}, u32[]{:S(2)}) collective-permute-start(bf16[128,512]{1,0:T(8,128)(2,1)S(1)} %values.1.refs_0_), channel_id=1, source_target_pairs={{0,1},{1,0},{2,3},{3,2},{4,5},{5,4},{6,7},{7,6},{8,9},{9,8},{10,11... | collective-permute-start | bytes 393224 | tf_op jit(solution)/shard_map/ppermute | solution.py:217
  67.3 5.6 %collective-permute-start.7 = (bf16[128,512]{1,0:T(8,128)(2,1)S(1)}, bf16[128,512]{1,0:T(8,128)(2,1)S(1)}, u32[]{:S(2)}, u32[]{:S(2)}) collective-permute-start(bf16[128,512]{1,0:T(8,128)(2,1)S(1)} %values.1.refs_0_), channel_id=1, source_target_pairs={{0,2},{2,0},{4,6},{6,4},{8,10},{10,8},{12,14},{14,12},{16,18},{18,... | collective-permute-start | bytes 393224 | tf_op jit(solution)/shard_map/ppermute | solution.py:217
  71.3 1.5 %collective-permute-start.8 = (bf16[128,512]{1,0:T(8,128)(2,1)S(1)}, bf16[128,512]{1,0:T(8,128)(2,1)S(1)}, u32[]{:S(2)}, u32[]{:S(2)}) collective-permute-start(bf16[128,512]{1,0:T(8,128)(2,1)S(1)} %collective-permute-done.6.refs_1_), channel_id=1, source_target_pairs={{0,2},{2,0},{4,6},{6,4},{8,10},{10,8},{12,14},{14,12},{16,18},{18,... | collective-permute-start | bytes 393224 | tf_op jit(solution)/shard_map/ppermute | solution.py:217
